TPU v7x, 32 devices: a whole 2x2x4 slice. The times are simulated.
32 devices in a mesh: dp: 8 (over z, y), tensor: 4 (over x, core).
Axes of the slice: x: 2, y: 2, z: 4, core: 2. Of those that a mesh axis runs over, the one named last changes fastest.
Arguments:
- tokens: bfloat16 [4096, 2048], P('dp'), may hold values from -6 to 6
- g_attn: float32 [2048], replicated, may hold values from 0.25 to 1.75
- w_query: bfloat16 [2048, 2048], P(None, 'tensor'), may hold values from -0.125 to 0.125
- w_key: bfloat16 [2048, 1024], P(None, 'tensor'), may hold values from -0.125 to 0.125
- w_value: bfloat16 [2048, 1024], P(None, 'tensor'), may hold values from -0.125 to 0.125
- q_gain: float32 [128], replicated, may hold values from 0.25 to 1.75
- k_gain: float32 [128], replicated, may hold values from 0.25 to 1.75
- w_out: bfloat16 [2048, 2048], P('tensor'), may hold values from -0.5 to 0.5
- g_mlp: float32 [2048], replicated, may hold values from 0.25 to 1.75
- w_gate: bfloat16 [2048, 6144], P(None, 'tensor'), may hold values from -0.125 to 0.125
- w_up: bfloat16 [2048, 6144], P(None, 'tensor'), may hold values from -0.125 to 0.125
- w_down: bfloat16 [6144, 2048], P('tensor'), may hold values from -0.078125 to 0.078125
- cotangent: bfloat16 [4096, 2048], P('dp'), may hold values from -6 to 6
Outputs:
- output: bfloat16 [4096, 2048], P('dp')
- grad_tokens: float32 [4096, 2048], P('dp')
- grad_g_attn: float32 [2048], replicated
- grad_query: float32 [2048, 2048], P('dp', 'tensor')
- grad_key: float32 [2048, 1024], P('dp', 'tensor')
- grad_value: float32 [2048, 1024], P('dp', 'tensor')
- grad_q_gain: float32 [128], replicated
- grad_k_gain: float32 [128], replicated
- grad_out: float32 [2048, 2048], P('tensor', 'dp')
- grad_g_mlp: float32 [2048], replicated
- grad_gate: float32 [2048, 6144], P('dp', 'tensor')
- grad_up: float32 [2048, 6144], P('dp', 'tensor')
- grad_down: float32 [6144, 2048], P('tensor', 'dp')
All inputs are finite; a program needn't handle non-finite values.
Results may differ from a plain program's by a relative error of at most 0.014.
Values sent between devices are 32-bit elements; how exact they have to be, the bound alone decides.
No kernel may reach another device: no remote copies, remote signals or barrier semaphores. Data moves between devices by JAX's collectives and lax.ppermute only.
A program may use at most 256 MiB of HBM per device.

v0:
```python
import jax
import jax.numpy as jnp
from jax import lax
from jax.sharding import PartitionSpec as P

SEQ_LEN = 256


EPS = 1e-06
THETA = 1000000.0


def rope_tables(length, width):
    half = width // 2
    inverse = THETA ** (-(jnp.arange(half).astype(jnp.float32) * 2.0 / width))
    angles = jnp.arange(length).astype(jnp.float32)[:, None] * inverse[None, :]
    angles = jnp.concatenate([angles, angles], axis=1)
    return (jnp.cos(angles)[None, :, None, :], jnp.sin(angles)[None, :, None, :])


def rotate(values, cosine, sine):
    half = values.shape[-1] // 2
    turned = jnp.concatenate([-values[..., half:], values[..., :half]], axis=-1)
    return values * cosine + turned * sine


def rotate_back(grads, cosine, sine):
    half = grads.shape[-1] // 2
    sined = grads * sine
    return grads * cosine + jnp.concatenate([sined[..., half:], -sined[..., :half]], axis=-1)


def rms_norm(values, gain):
    inv_rms = lax.rsqrt(jnp.mean(values * values, axis=-1, keepdims=True) + EPS)
    unit_rows = values * inv_rms
    return (unit_rows * gain, unit_rows, inv_rms)


def rms_back(grads, gain, unit_rows, inv_rms):
    scaled = grads * gain
    return inv_rms * (scaled - unit_rows * jnp.mean(scaled * unit_rows, axis=-1, keepdims=True))


def causal_scores(query_five, keys, scale):
    length = query_five.shape[1]
    scores = (
        jnp.einsum("sqkgd,spkd->skgqp", query_five, keys, preferred_element_type=jnp.float32)
        * scale
    )
    allowed = jnp.arange(length)[:, None] >= jnp.arange(length)[None, :]
    return jnp.where(allowed, scores, -1e30)


def own_rows(product):
    share = product.shape[0] // lax.axis_size("tensor")
    start = lax.axis_index("tensor") * share
    return jnp.sum(lax.dynamic_slice_in_dim(product, start, share, 0), axis=0)


def body(
    tokens,
    g_attn,
    w_query,
    w_key,
    w_value,
    q_gain,
    k_gain,
    w_out,
    g_mlp,
    w_gate,
    w_up,
    w_down,
    cotangent,
):
    f32 = jnp.float32
    b16 = jnp.bfloat16
    rows = tokens.shape[0]
    head_dim = q_gain.shape[0]
    heads = w_query.shape[1] // head_dim
    kv_heads = w_key.shape[1] // head_dim
    group = heads // kv_heads
    seqs = rows // SEQ_LEN
    scale = head_dim ** (-0.5)
    cosine, sine = rope_tables(SEQ_LEN, head_dim)
    x_full = tokens.astype(f32)
    normed1, unit1, rms1 = rms_norm(x_full, g_attn)
    normed1 = normed1.astype(b16)
    query = jnp.dot(normed1, w_query, preferred_element_type=f32).reshape(
        seqs, SEQ_LEN, heads, head_dim
    )
    keyvec = jnp.dot(normed1, w_key, preferred_element_type=f32).reshape(
        seqs, SEQ_LEN, kv_heads, head_dim
    )
    values = (
        jnp.dot(normed1, w_value, preferred_element_type=f32)
        .astype(b16)
        .reshape(seqs, SEQ_LEN, kv_heads, head_dim)
    )
    q_normed, q_unit, q_inv = rms_norm(query, q_gain)
    k_normed, k_unit, k_inv = rms_norm(keyvec, k_gain)
    q_rot = rotate(q_normed, cosine, sine).astype(b16)
    k_rot = rotate(k_normed, cosine, sine).astype(b16)
    q_group = q_rot.reshape(seqs, SEQ_LEN, kv_heads, group, head_dim)
    scores = causal_scores(q_group, k_rot, scale)
    row_top = jnp.max(scores, axis=-1, keepdims=True)
    log_total = row_top + jnp.log(jnp.sum(jnp.exp(scores - row_top), axis=-1, keepdims=True))
    probs_b = jnp.exp(scores - log_total).astype(b16)
    att_five = jnp.einsum("skgqp,spkd->sqkgd", probs_b, values, preferred_element_type=f32).astype(
        b16
    )
    attended = att_five.reshape(rows, heads * head_dim)
    mixed = lax.psum(jnp.dot(attended, w_out, preferred_element_type=f32), "tensor")
    resid = x_full + mixed
    normed2, unit2, rms2 = rms_norm(resid, g_mlp)
    normed2 = normed2.astype(b16)
    gate_pre = jnp.dot(normed2, w_gate, preferred_element_type=f32)
    up_pre = jnp.dot(normed2, w_up, preferred_element_type=f32)
    sigmoid_g = jax.nn.sigmoid(gate_pre)
    act_gate = gate_pre * sigmoid_g
    hidden = (act_gate * up_pre).astype(b16)
    down_sum = lax.psum(jnp.dot(hidden, w_down, preferred_element_type=f32), "tensor")
    output = (resid + down_sum).astype(b16)
    grad_down = jnp.dot(hidden.T, cotangent, preferred_element_type=f32)
    d_hidden = jnp.dot(cotangent, w_down.T, preferred_element_type=f32)
    d_up = (d_hidden * act_gate).astype(b16)
    d_gate = (d_hidden * up_pre * (sigmoid_g * (1.0 + gate_pre * (1.0 - sigmoid_g)))).astype(b16)
    grad_gate = jnp.dot(normed2.T, d_gate, preferred_element_type=f32)
    grad_up = jnp.dot(normed2.T, d_up, preferred_element_type=f32)
    d_norm2 = lax.psum(
        jnp.dot(d_gate, w_gate.T, preferred_element_type=f32)
        + jnp.dot(d_up, w_up.T, preferred_element_type=f32),
        "tensor",
    )
    mlp_gain_term = own_rows(d_norm2 * unit2)
    d_resid = cotangent.astype(f32) + rms_back(d_norm2, g_mlp, unit2, rms2)
    d_resid_b = d_resid.astype(b16)
    grad_out = jnp.dot(attended.T, d_resid_b, preferred_element_type=f32)
    d_att = jnp.dot(d_resid_b, w_out.T, preferred_element_type=f32).astype(b16)
    d_att_five = d_att.reshape(seqs, SEQ_LEN, kv_heads, group, head_dim)
    probs = jnp.exp(causal_scores(q_group, k_rot, scale) - log_total)
    d_prob = jnp.einsum("sqkgd,spkd->skgqp", d_att_five, values, preferred_element_type=f32)
    delta = jnp.sum(d_att_five.astype(f32) * att_five.astype(f32), axis=-1)
    delta = jnp.transpose(delta, (0, 2, 3, 1))[..., None]
    d_score = (probs * (d_prob - delta) * scale).astype(b16)
    d_qrot = jnp.einsum("skgqp,spkd->sqkgd", d_score, k_rot, preferred_element_type=f32).reshape(
        seqs, SEQ_LEN, heads, head_dim
    )
    d_krot = jnp.einsum("skgqp,sqkgd->spkd", d_score, q_group, preferred_element_type=f32)
    d_values = jnp.einsum(
        "skgqp,sqkgd->spkd", probs.astype(b16), d_att_five, preferred_element_type=f32
    )
    d_qn = rotate_back(d_qrot, cosine, sine)
    d_kn = rotate_back(d_krot, cosine, sine)
    q_gain_term = jnp.sum(d_qn * q_unit, axis=(0, 1, 2))
    k_gain_term = jnp.sum(d_kn * k_unit, axis=(0, 1, 2))
    d_query_b = rms_back(d_qn, q_gain, q_unit, q_inv).astype(b16).reshape(rows, heads * head_dim)
    d_keys_b = rms_back(d_kn, k_gain, k_unit, k_inv).astype(b16).reshape(rows, kv_heads * head_dim)
    d_values_b = d_values.astype(b16).reshape(rows, kv_heads * head_dim)
    grad_query = jnp.dot(normed1.T, d_query_b, preferred_element_type=f32)
    grad_key = jnp.dot(normed1.T, d_keys_b, preferred_element_type=f32)
    grad_value = jnp.dot(normed1.T, d_values_b, preferred_element_type=f32)
    summed_query, summed_key, summed_value, summed_gate, summed_up = (
        lax.psum_scatter(grad_query, "dp", scatter_dimension=0, tiled=True),
        lax.psum_scatter(grad_key, "dp", scatter_dimension=0, tiled=True),
        lax.psum_scatter(grad_value, "dp", scatter_dimension=0, tiled=True),
        lax.psum_scatter(grad_gate, "dp", scatter_dimension=0, tiled=True),
        lax.psum_scatter(grad_up, "dp", scatter_dimension=0, tiled=True),
    )
    summed_out, summed_down = (
        lax.psum_scatter(grad_out, "dp", scatter_dimension=1, tiled=True),
        lax.psum_scatter(grad_down, "dp", scatter_dimension=1, tiled=True),
    )
    d_norm1 = lax.psum(
        jnp.dot(d_query_b, w_query.T, preferred_element_type=f32)
        + jnp.dot(d_keys_b, w_key.T, preferred_element_type=f32)
        + jnp.dot(d_values_b, w_value.T, preferred_element_type=f32),
        "tensor",
    )
    attn_gain_term = own_rows(d_norm1 * unit1)
    grad_tokens = d_resid + rms_back(d_norm1, g_attn, unit1, rms1)
    gain_attn, gain_q, gain_k, gain_mlp = lax.psum(
        (attn_gain_term, q_gain_term, k_gain_term, mlp_gain_term), ("dp", "tensor")
    )
    return (
        output,
        grad_tokens,
        gain_attn,
        summed_query,
        summed_key,
        summed_value,
        gain_q,
        gain_k,
        summed_out,
        gain_mlp,
        summed_gate,
        summed_up,
        summed_down,
    )


def solution(mesh):
    in_specs = (
        P("dp", None),
        P(),
        P(None, "tensor"),
        P(None, "tensor"),
        P(None, "tensor"),
        P(),
        P(),
        P("tensor", None),
        P(),
        P(None, "tensor"),
        P(None, "tensor"),
        P("tensor", None),
        P("dp", None),
    )
    out_specs = (
        P("dp", None),
        P("dp", None),
        P(),
        P("dp", "tensor"),
        P("dp", "tensor"),
        P("dp", "tensor"),
        P(),
        P(),
        P("tensor", "dp"),
        P(),
        P("dp", "tensor"),
        P("dp", "tensor"),
        P("tensor", "dp"),
    )
    return jax.shard_map(body, mesh=mesh, in_specs=in_specs, out_specs=out_specs, check_vma=False)
```

profile of v0, /device:TPU:0, one launch (start us, length us, event | category | flops | bytes accessed | tf_op | source)
XLA Modules:
  0.0 1442.8 jit_solution(12172357591475566088)
XLA Ops:
  14.0 4.5 fusion.42
  26.2 2.8 reshape.219
  48.6 3.3 fusion.47
  52.2 88.0 %all-reduce.6.cloned.1.call-done = f32[512,2048]{1,0:T(8,128)} async-done(((f32[512,2048]{1,0:T(8,128)}), f32[512,2048]{1,0:T(8,128)}) %all-reduce.6.cloned.1.call-update) | async-done | bytes 4194320 | tf_op jit(solution)/shard_map/psum | solution.py:112
  140.2 3.6 multiply_reduce_fusion.2
  144.9 3.1 multiply_convert_fusion
  148.0 8.7 fusion.49
  156.7 5.1 fusion.48
  161.8 9.6 multiply_convert_fusion.2
  171.4 3.4 fusion.51
  174.9 5.0 convolution_add_fusion
  181.8 8.7 fusion.50
  190.5 75.2 %all-reduce.8.cloned.1.call-done = f32[512,2048]{1,0:T(8,128)} async-done(((f32[512,2048]{1,0:T(8,128)}), f32[512,2048]{1,0:T(8,128)}) %all-reduce.8.cloned.1.call-update) | async-done | bytes 4194320 | tf_op jit(solution)/shard_map/psum | solution.py:129
  265.8 4.1 multiply_reduce_fusion.1
  278.4 9.7 copy.195
  317.4 3.2 add_add_fusion
  327.3 5.5 fusion.17
  333.8 3.4 fusion.41
  337.2 10.2 fusion.55
  347.5 10.1 fusion.54
  357.9 10.1 fusion.53
  369.7 104.1 %all-reduce.10.cloned.1.call-done = (f32[512,2048]{1,0:T(8,128)}, f32[512,2048]{1,0:T(8,128)}) async-done(((f32[512,2048]{1,0:T(8,128)}, f32[512,2048]{1,0:T(8,128)}), (f32[512,2048]{1,0:T(8,128)}, f32[512,2048]{1,0:T(8,128)})) %all-reduce.10.cloned.1.call-update) | async-done | bytes 8388624 | tf_op jit(solution)/shard_map/psum | solution.py:121
  473.8 7.1 convert_multiply_fusion
  482.2 40.5 %all-reduce = (f32[2048]{0:T(1024)}, f32[128]{0:T(128)}, f32[128]{0:T(128)}, f32[2048]{0:T(1024)}) all-reduce(f32[2048]{0:T(1024)S(1)} %fusion.14, f32[128]{0:T(128)S(1)} %get-tuple-element.13, f32[128]{0:T(128)S(1)} %copy-done.49, f32[2048]{0:T(1024)S(1)} %fusion.13), channel_id=1, replica_groups=mesh['dp'=8,'tensor'=4] {'dp','tensor'}, use_global_device_ids=true, to_apply=%region_16.17 | all-reduce | flops 4352 | bytes 34816 | tf_op jit(solution)/shard_map/psum | solution.py:181
  522.8 7.4 multiply_add_fusion
  530.1 17.1 %reduce-scatter.10.cloned.1.call-done = f32[256,256]{1,0:T(8,128)} async-done(((f32[2048,256]{1,0:T(8,128)}), f32[256,256]{1,0:T(8,128)}) %reduce-scatter.10.cloned.1.call-update) | async-done | bytes 262160 | tf_op jit(solution)/shard_map/reduce_scatter | solution.py:164
  547.2 71.4 %reduce-scatter.12.cloned.1.call-done = f32[256,256]{1,0:T(8,128)} async-done(((f32[2048,256]{1,0:T(8,128)}), f32[256,256]{1,0:T(8,128)}) %reduce-scatter.12.cloned.1.call-update) | async-done | bytes 262160 | tf_op jit(solution)/shard_map/reduce_scatter | solution.py:165
  618.5 91.8 %reduce-scatter.14.cloned.1.call-done = f32[512,256]{1,0:T(8,128)} async-done(((f32[512,2048]{1,0:T(8,128)}), f32[512,256]{1,0:T(8,128)}) %reduce-scatter.14.cloned.1.call-update) | async-done | bytes 524304 | tf_op jit(solution)/shard_map/reduce_scatter | solution.py:170
  710.3 92.2 %reduce-scatter.8.cloned.1.call-done = f32[256,512]{1,0:T(8,128)} async-done(((f32[2048,512]{1,0:T(8,128)}), f32[256,512]{1,0:T(8,128)}) %reduce-scatter.8.cloned.1.call-update) | async-done | bytes 524304 | tf_op jit(solution)/shard_map/reduce_scatter | solution.py:163
  802.5 211.7 %reduce-scatter.20.cloned.1.call-done = f32[1536,256]{1,0:T(8,128)} async-done(((f32[1536,2048]{1,0:T(8,128)}), f32[1536,256]{1,0:T(8,128)}) %reduce-scatter.20.cloned.1.call-update) | async-done | bytes 1572880 | tf_op jit(solution)/shard_map/reduce_scatter | solution.py:171
  1014.2 210.7 %reduce-scatter.18.cloned.1.call-done = f32[256,1536]{1,0:T(8,128)} async-done(((f32[2048,1536]{1,0:T(8,128)}), f32[256,1536]{1,0:T(8,128)}) %reduce-scatter.18.cloned.1.call-update) | async-done | bytes 1572880 | tf_op jit(solution)/shard_map/reduce_scatter | solution.py:167
  1225.0 210.6 %reduce-scatter.16.cloned.1.call-done = f32[256,1536]{1,0:T(8,128)} async-done(((f32[2048,1536]{1,0:T(8,128)}), f32[256,1536]{1,0:T(8,128)}) %reduce-scatter.16.cloned.1.call-update) | async-done | bytes 1572880 | tf_op jit(solution)/shard_map/reduce_scatter | solution.py:166
  (211 shorter events, 85.5 us)
Async XLA Ops:
  7.2 41.4 %copy-start = (bf16[512,2048]{1,0:T(8,128)(2,1)S(1)}, bf16[512,2048]{1,0:T(8,128)(2,1)}, u32[]{:S(2)}) copy-start(bf16[512,2048]{1,0:T(8,128)(2,1)} %param.20) | copy-start | bytes 6291460
  7.2 133.0 %all-reduce.6.cloned.1.call-start = ((), (), s32[]{:S(2)}) async-start(), calls=%async_computation.7 | async-start | bytes 8388608 | tf_op jit(solution)/shard_map/psum | solution.py:112
  9.5 20.0 %copy-start.43 = (f32[512]{0:T(512)}, f32[512]{0:T(512)S(1)}, u32[]{:S(2)}) copy-start(f32[512]{0:T(512)S(1)} %add_rsqrt_fusion.3) | copy-start | bytes 6148
  29.6 5.7 copy-start.45
  33.2 6.9 copy-start.36
  35.2 5.0 copy-start.38
  35.3 4.8 copy-start.29
  35.3 4.8 copy-start.30
  51.8 92.0 %copy-start.40 = (f32[2048]{0:T(1024)S(1)}, f32[2048]{0:T(1024)}, u32[]{:S(2)}) copy-start(f32[2048]{0:T(1024)} %param.21) | copy-start | bytes 24580
  51.9 213.9 %all-reduce.8.cloned.1.call-start = ((), (), s32[]{:S(2)}) async-start(), calls=%async_computation.8 | async-start | bytes 8388608 | tf_op jit(solution)/shard_map/psum | solution.py:129
  144.9 11.8 slice-start
  148.0 8.7 copy-start.21
  148.0 8.7 slice-start.1
  156.7 5.1 copy-start.23
  161.8 13.1 slice-start.2
  180.0 293.8 %all-reduce.10.cloned.1.call-start = ((), (), s32[]{:S(2)}) async-start(), calls=%async_computation.16 | async-start | bytes 16777216 | tf_op jit(solution)/shard_map/psum | solution.py:121
  265.8 5.9 copy-start.9
  277.5 11.9 copy-start.3
  295.2 6.4 copy-start.31
  297.6 4.9 copy-start.37
  297.6 4.9 copy-start.48
  304.2 5.1 copy-start.11
  304.2 5.1 copy-start.39
  320.7 226.5 %reduce-scatter.10.cloned.1.call-start = ((), (), s32[]{:S(2)}) async-start(), calls=%async_computation.10 | async-start | bytes 2359296 | tf_op jit(solution)/shard_map/reduce_scatter | solution.py:164
  324.6 294.0 %reduce-scatter.12.cloned.1.call-start = ((), (), s32[]{:S(2)}) async-start(), calls=%async_computation.11 | async-start | bytes 2359296 | tf_op jit(solution)/shard_map/reduce_scatter | solution.py:165
  327.2 383.1 %reduce-scatter.14.cloned.1.call-start = ((), (), s32[]{:S(2)}) async-start(), calls=%async_computation.12 | async-start | bytes 4718592 | tf_op jit(solution)/shard_map/reduce_scatter | solution.py:170
  332.8 469.7 %reduce-scatter.8.cloned.1.call-start = ((), (), s32[]{:S(2)}) async-start(), calls=%async_computation.9 | async-start | bytes 4718592 | tf_op jit(solution)/shard_map/reduce_scatter | solution.py:163
  337.2 677.0 %reduce-scatter.20.cloned.1.call-start = ((), (), s32[]{:S(2)}) async-start(), calls=%async_computation.15 | async-start | bytes 14155776 | tf_op jit(solution)/shard_map/reduce_scatter | solution.py:171
  347.5 877.5 %reduce-scatter.18.cloned.1.call-start = ((), (), s32[]{:S(2)}) async-start(), calls=%async_computation.14 | async-start | bytes 14155776 | tf_op jit(solution)/shard_map/reduce_scatter | solution.py:167
  357.6 1077.9 %reduce-scatter.16.cloned.1.call-start = ((), (), s32[]{:S(2)}) async-start(), calls=%async_computation.13 | async-start | bytes 14155776 | tf_op jit(solution)/shard_map/reduce_scatter | solution.py:166
  473.8 8.4 copy-start.49
  522.8 912.8 %copy-start.1 = (bf16[512,2048]{1,0:T(8,128)(2,1)S(1)}, bf16[512,2048]{1,0:T(8,128)(2,1)}, u32[]{:S(2)}) copy-start(bf16[512,2048]{1,0:T(8,128)(2,1)} %param.20) | copy-start | bytes 6291460
  (34 other events, 83.6 us)
Sparse Core Ops, SparseCore 0:
  52.0 88.1 all-reduce.5
  180.1 85.6 all-reduce.7
  320.8 153.0 all-reduce.9
  477.8 69.3 reduce-scatter.9
  551.1 67.3 reduce-scatter.11
  622.6 87.6 reduce-scatter.13
  714.5 87.9 reduce-scatter.7
  806.7 207.5 reduce-scatter.19
  1018.4 206.5 reduce-scatter.17
  1229.0 206.5 reduce-scatter.15
where the time goes:
time: 1450 us; the launch traced here: 1440 us
  waiting for transfers between devices  1170 us (81%)
  matrix products  110 us (8%)
  other arithmetic  54.4 us (4%)
  local copies, waits for them, and re-layouts  48.2 us (3%)
  blocking collectives  40.5 us (3%)
  between operations  15.4 us (1%)
    reduce_scatter x1, waiting for transfers between devices, body(): lax.psum_scatter(grad_down, 'dp', scatter_dimension=1, tiled=True)  212 us
    reduce_scatter x1, waiting for transfers between devices, body(): lax.psum_scatter(grad_up, 'dp', scatter_dimension=0, tiled=True)  211 us
    reduce_scatter x1, waiting for transfers between devices, body(): lax.psum_scatter(grad_gate, 'dp', scatter_dimension=0, tiled=True)  211 us
    psum x1, waiting for transfers between devices, body(): lax.psum(jnp.dot(hidden, w_down, preferred_element_type=f32), 'tensor')  104 us
    reduce_scatter x1, waiting for transfers between devices, body(): lax.psum_scatter(grad_query, 'dp', scatter_dimension=0, tiled=True)  92.2 us
    reduce_scatter x1, waiting for transfers between devices, body(): lax.psum_scatter(grad_out, 'dp', scatter_dimension=1, tiled=True)  91.8 us
    psum x1, waiting for transfers between devices, body(): lax.psum(jnp.dot(attended, w_out, preferred_element_type=f32), 'tensor')  88 us
    psum x1, waiting for transfers between devices, body(): lax.psum(jnp.dot(d_gate, w_gate.T, preferred_element_type=f32) + jnp.dot(...  75.2 us
  transfers between devices with their start and end apart: 10, of which 10 were waited for; matrix products, arithmetic and copies ran while one was open for 5% of the time, Pallas kernels for 0%

commit v1 on v0

v1 whole, which is shorter than its diff:
```python
import jax
import jax.numpy as jnp
from jax import lax
from jax.sharding import PartitionSpec as P

SEQ_LEN = 256


EPS = 1e-06
THETA = 1000000.0

f32 = jnp.float32
b16 = jnp.bfloat16


def rope_tables(length, width):
    half = width // 2
    inverse = THETA ** (-(jnp.arange(half).astype(jnp.float32) * 2.0 / width))
    angles = jnp.arange(length).astype(jnp.float32)[:, None] * inverse[None, :]
    angles = jnp.concatenate([angles, angles], axis=1)
    return (jnp.cos(angles)[None, :, None, :], jnp.sin(angles)[None, :, None, :])


def rotate(values, cosine, sine):
    half = values.shape[-1] // 2
    turned = jnp.concatenate([-values[..., half:], values[..., :half]], axis=-1)
    return values * cosine + turned * sine


def rotate_back(grads, cosine, sine):
    half = grads.shape[-1] // 2
    sined = grads * sine
    return grads * cosine + jnp.concatenate([sined[..., half:], -sined[..., :half]], axis=-1)


def rms_norm(values, gain):
    inv_rms = lax.rsqrt(jnp.mean(values * values, axis=-1, keepdims=True) + EPS)
    unit_rows = values * inv_rms
    return (unit_rows * gain, unit_rows, inv_rms)


def rms_back(grads, gain, unit_rows, inv_rms):
    scaled = grads * gain
    return inv_rms * (scaled - unit_rows * jnp.mean(scaled * unit_rows, axis=-1, keepdims=True))


def causal_scores(query_five, keys, scale):
    length = query_five.shape[1]
    scores = (
        jnp.einsum("sqkgd,spkd->skgqp", query_five, keys, preferred_element_type=jnp.float32)
        * scale
    )
    allowed = jnp.arange(length)[:, None] >= jnp.arange(length)[None, :]
    return jnp.where(allowed, scores, -1e30)


def swap(value, axis, mask):
    size = lax.axis_size(axis)
    return lax.ppermute(value, axis, [(i, i ^ mask) for i in range(size)])


def dot(a, b):
    return jnp.dot(a, b, preferred_element_type=f32)


def dot_nt(a, b):
    return lax.dot_general(a, b, (((1,), (1,)), ((), ())), preferred_element_type=f32)


def dot_tn(a, b):
    return lax.dot_general(a, b, (((0,), (0,)), ((), ())), preferred_element_type=f32)


def tensor_masks():
    size = lax.axis_size("tensor")
    return [1 << i for i in range(1, size.bit_length() - 1)]


def halves_sum(mine, theirs):
    total = mine + swap(theirs, "tensor", 1)
    for mask in tensor_masks():
        total = total + swap(total, "tensor", mask)
    return total


def scatter_sum(parts, masks):
    for mask in masks:
        half = len(parts) // 2
        received = [swap(p, "dp", mask) for p in parts[half:]]
        parts = [a + b for a, b in zip(parts[:half], received)]
    return parts[0]


def relative(masks):
    offsets = [0]
    for mask in reversed(masks):
        offsets = offsets + [o ^ mask for o in offsets]
    return offsets


def body(
    tokens,
    g_attn,
    w_query,
    w_key,
    w_value,
    q_gain,
    k_gain,
    w_out,
    g_mlp,
    w_gate,
    w_up,
    w_down,
    cotangent,
):
    rows, width = tokens.shape
    head_dim = q_gain.shape[0]
    heads = w_query.shape[1] // head_dim
    kv_heads = w_key.shape[1] // head_dim
    group = heads // kv_heads
    seqs = rows // SEQ_LEN
    scale = head_dim ** (-0.5)
    cosine, sine = rope_tables(SEQ_LEN, head_dim)

    n_dp = lax.axis_size("dp")
    me = lax.axis_index("dp")
    core = lax.axis_index("tensor") % 2
    half = rows // 2
    block = width // n_dp
    bits = [1 << i for i in range(n_dp.bit_length() - 1)]
    near, far = bits[0], bits[-1]
    middle = bits[1:-1]

    def mine_of(a):
        return lax.dynamic_slice_in_dim(a, core * half, half, 0)

    def theirs_of(a):
        return lax.dynamic_slice_in_dim(a, (1 - core) * half, half, 0)

    def in_order(mine, theirs):
        out = jnp.zeros((rows,) + mine.shape[1:], mine.dtype)
        out = lax.dynamic_update_slice_in_dim(out, mine, core * half, 0)
        return lax.dynamic_update_slice_in_dim(out, theirs, (1 - core) * half, 0)

    def columns(a, offset):
        return lax.dynamic_slice_in_dim(a, (me ^ offset) * block, block, 1)

    cot_mine, cot_theirs = mine_of(cotangent), theirs_of(cotangent)
    cot_own = jnp.concatenate([cot_mine, cot_theirs])
    c0 = cot_mine.astype(f32) * 2.0
    c1 = swap(c0, "dp", near)
    c2 = swap(c0, "dp", far)
    c3 = swap(c2, "dp", near)
    cot_near = (jnp.concatenate([c1, swap(c1, "tensor", 1)]) * 0.5).astype(b16)
    c23 = jnp.concatenate([c2, c3])
    cot_far = (jnp.concatenate([c23, swap(c23, "tensor", 1)]) * 0.5).astype(b16)

    tok = jnp.concatenate([mine_of(tokens), theirs_of(tokens)])
    x_full = tok.astype(f32)
    normed1, unit1, rms1 = rms_norm(x_full, g_attn)
    normed1 = normed1.astype(b16)
    query = dot(normed1, w_query).reshape(seqs, SEQ_LEN, heads, head_dim)
    keyvec = dot(normed1, w_key).reshape(seqs, SEQ_LEN, kv_heads, head_dim)
    values = dot(normed1, w_value).astype(b16).reshape(seqs, SEQ_LEN, kv_heads, head_dim)
    q_normed, q_unit, q_inv = rms_norm(query, q_gain)
    k_normed, k_unit, k_inv = rms_norm(keyvec, k_gain)
    q_rot = rotate(q_normed, cosine, sine).astype(b16)
    k_rot = rotate(k_normed, cosine, sine).astype(b16)
    q_group = q_rot.reshape(seqs, SEQ_LEN, kv_heads, group, head_dim)
    scores = causal_scores(q_group, k_rot, scale)
    row_top = jnp.max(scores, axis=-1, keepdims=True)
    log_total = row_top + jnp.log(jnp.sum(jnp.exp(scores - row_top), axis=-1, keepdims=True))
    probs = jnp.exp(scores - log_total)
    probs_b = probs.astype(b16)
    att_five = jnp.einsum("skgqp,spkd->sqkgd", probs_b, values, preferred_element_type=f32).astype(
        b16
    )
    attended = att_five.reshape(rows, heads * head_dim)
    mixed = dot(attended, w_out)
    resid_mine = x_full[:half] + halves_sum(mixed[:half], mixed[half:])
    _, n0, _ = rms_norm(resid_mine, g_mlp)
    n1 = swap(n0, "dp", near)
    n2 = swap(n0, "dp", far)
    n3 = swap(n2, "dp", near)
    resid = jnp.concatenate([resid_mine, swap(resid_mine, "tensor", 1)])
    normed2, unit2, rms2 = rms_norm(resid, g_mlp)
    normed2 = normed2.astype(b16)

    def feed(normed, cot):
        gate_pre = dot(normed, w_gate)
        up_pre = dot(normed, w_up)
        d_hidden = dot_nt(cot, w_down)
        sigmoid_g = jax.nn.sigmoid(gate_pre)
        act_gate = gate_pre * sigmoid_g
        hidden = (act_gate * up_pre).astype(b16)
        d_up = (d_hidden * act_gate).astype(b16)
        d_gate = (
            d_hidden * up_pre * (sigmoid_g * (1.0 + gate_pre * (1.0 - sigmoid_g)))
        ).astype(b16)
        return hidden, d_gate, d_up

    hidden, d_gate, d_up = feed(normed2, cot_own)
    dn_part = dot_nt(d_gate, w_gate) + dot_nt(d_up, w_up)
    down_part = dot(hidden, w_down)
    mlp_gain_term = jnp.sum(dn_part * unit2, axis=0)
    dn_mine = halves_sum(dn_part[:half], dn_part[half:])
    down_mine = halves_sum(down_part[:half], down_part[half:])

    normed2_near = (jnp.concatenate([n1, swap(n1, "tensor", 1)]) * g_mlp).astype(b16)
    n23 = jnp.concatenate([n2, n3])
    normed2_far = (jnp.concatenate([n23, swap(n23, "tensor", 1)]) * g_mlp).astype(b16)
    near_parts = feed(normed2_near, cot_near)
    far_parts = feed(normed2_far, cot_far)
    all_hidden, all_gate, all_up = (
        jnp.concatenate(list(three)) for three in zip((hidden, d_gate, d_up), near_parts, far_parts)
    )
    all_cot = jnp.concatenate([cot_own, cot_near, cot_far])
    all_normed = jnp.concatenate([normed2, normed2_near, normed2_far])
    offsets = relative(middle)
    summed_down = scatter_sum([dot_tn(all_hidden, columns(all_cot, o)) for o in offsets], middle)
    summed_gate = scatter_sum([dot_tn(columns(all_normed, o), all_gate) for o in offsets], middle)
    summed_up = scatter_sum([dot_tn(columns(all_normed, o), all_up) for o in offsets], middle)

    d_norm2 = jnp.concatenate([dn_mine, swap(dn_mine, "tensor", 1)])
    d_resid = cot_own.astype(f32) + rms_back(d_norm2, g_mlp, unit2, rms2)
    d_resid_b = d_resid.astype(b16)
    down_sum = jnp.concatenate([down_mine, swap(down_mine, "tensor", 1)])
    out_own = (resid + down_sum).astype(b16)
    output = in_order(out_own[:half], out_own[half:])

    every = [near] + middle + [far]
    blocks = relative(every)
    summed_out = scatter_sum([dot_tn(attended, columns(d_resid_b, o)) for o in blocks], every)
    d_att = dot_nt(d_resid_b, w_out).astype(b16)
    d_att_five = d_att.reshape(seqs, SEQ_LEN, kv_heads, group, head_dim)
    d_prob = jnp.einsum("sqkgd,spkd->skgqp", d_att_five, values, preferred_element_type=f32)
    delta = jnp.sum(d_att_five.astype(f32) * att_five.astype(f32), axis=-1)
    delta = jnp.transpose(delta, (0, 2, 3, 1))[..., None]
    d_score = (probs * (d_prob - delta) * scale).astype(b16)
    d_qrot = jnp.einsum("skgqp,spkd->sqkgd", d_score, k_rot, preferred_element_type=f32).reshape(
        seqs, SEQ_LEN, heads, head_dim
    )
    d_krot = jnp.einsum("skgqp,sqkgd->spkd", d_score, q_group, preferred_element_type=f32)
    d_values = jnp.einsum("skgqp,sqkgd->spkd", probs_b, d_att_five, preferred_element_type=f32)
    d_qn = rotate_back(d_qrot, cosine, sine)
    d_kn = rotate_back(d_krot, cosine, sine)
    q_gain_term = jnp.sum(d_qn * q_unit, axis=(0, 1, 2))
    k_gain_term = jnp.sum(d_kn * k_unit, axis=(0, 1, 2))
    d_query_b = rms_back(d_qn, q_gain, q_unit, q_inv).astype(b16).reshape(rows, heads * head_dim)
    d_keys_b = rms_back(d_kn, k_gain, k_unit, k_inv).astype(b16).reshape(rows, kv_heads * head_dim)
    d_values_b = d_values.astype(b16).reshape(rows, kv_heads * head_dim)
    d1_part = dot_nt(d_query_b, w_query) + dot_nt(d_keys_b, w_key) + dot_nt(d_values_b, w_value)
    attn_gain_term = jnp.sum(d1_part * unit1, axis=0)
    gains = jnp.concatenate([attn_gain_term, q_gain_term, k_gain_term, mlp_gain_term])
    for mask in [1] + tensor_masks():
        gains = gains + swap(gains, "tensor", mask)
    for mask in bits:
        gains = gains + swap(gains, "dp", mask)
    hd = head_dim
    gain_attn, gain_q, gain_k, gain_mlp = (
        gains[:width],
        gains[width : width + hd],
        gains[width + hd : width + 2 * hd],
        gains[width + 2 * hd :],
    )
    d_qkv = jnp.concatenate([d_query_b, d_keys_b, d_values_b], axis=1)
    summed_qkv = scatter_sum([dot_tn(columns(normed1, o), d_qkv) for o in blocks], every)
    nq, nk = heads * head_dim, kv_heads * head_dim
    summed_query, summed_key, summed_value = (
        summed_qkv[:, :nq],
        summed_qkv[:, nq : nq + nk],
        summed_qkv[:, nq + nk :],
    )
    d1_mine = halves_sum(d1_part[:half], d1_part[half:])
    gt_mine = d_resid[:half] + rms_back(d1_mine, g_attn, unit1[:half], rms1[:half])
    grad_tokens = in_order(gt_mine, swap(gt_mine, "tensor", 1))
    return (
        output,
        grad_tokens,
        gain_attn,
        summed_query,
        summed_key,
        summed_value,
        gain_q,
        gain_k,
        summed_out,
        gain_mlp,
        summed_gate,
        summed_up,
        summed_down,
    )


def solution(mesh):
    in_specs = (
        P("dp", None),
        P(),
        P(None, "tensor"),
        P(None, "tensor"),
        P(None, "tensor"),
        P(),
        P(),
        P("tensor", None),
        P(),
        P(None, "tensor"),
        P(None, "tensor"),
        P("tensor", None),
        P("dp", None),
    )
    out_specs = (
        P("dp", None),
        P("dp", None),
        P(),
        P("dp", "tensor"),
        P("dp", "tensor"),
        P("dp", "tensor"),
        P(),
        P(),
        P("tensor", "dp"),
        P(),
        P("dp", "tensor"),
        P("dp", "tensor"),
        P("tensor", "dp"),
    )
    return jax.shard_map(body, mesh=mesh, in_specs=in_specs, out_specs=out_specs, check_vma=False)
```

time: 1450 us -> 755 us (0.52)
  waiting for transfers between devices: 1170 us -> 412 us
  matrix products: 110 us -> 177 us
  blocking collectives: 40.5 us -> 0 us
  starting transfers between devices: 1.13 us -> 39.6 us
    reduce_scatter x7 -> x0, waiting for transfers between devices: 905 us -> none  [the longest x1 212 us: body(): lax.psum_scatter(grad_down, 'dp', scatter_dimension=1, tiled=True)]
    ppermute x0 -> x44, waiting for transfers between devices: none -> 412 us  [swap(): return lax.ppermute(value, axis, [(i, i ^ mask) for i in range(size)])]
    psum x3 -> x0, waiting for transfers between devices: 267 us -> none  [the longest x1 104 us: body(): lax.psum(jnp.dot(hidden, w_down, preferred_element_type=f32), 'tensor')]
    dot_general x22 -> x43, matrix products: 106 us -> 173 us  [the longest x11 74.4 us: dot(): return jnp.dot(a, b, preferred_element_type=f32)]
    psum x1 -> x0, blocking collectives: 40.5 us -> none  [body(): lax.psum((attn_gain_term, q_gain_term, k_gain_term, mlp_gain_term), ('dp'...]
    ppermute x0 -> x44, starting transfers between devices: none -> 39.6 us  [swap(): return lax.ppermute(value, axis, [(i, i ^ mask) for i in range(size)])]
    convert_element_type x0 -> x6, other arithmetic: none -> 16.3 us  [the longest x1 5.48 us: body(): d_resid_b = d_resid.astype(b16)]
    concatenate x0 -> x5, other arithmetic: none -> 15.1 us  [the longest x1 4.17 us: body(): all_cot = jnp.concatenate([cot_own, cot_near, cot_far])]
  transfers between devices with their start and end apart: 10 -> 44, of which waited for: 10 -> 16; matrix products, arithmetic and copies ran while one was open for 5% -> 28% of each run, Pallas kernels for 0% -> 0%
where the time goes in v1:
time: 755 us; the launch traced here: 750 us
  waiting for transfers between devices  412 us (55%)
  matrix products  177 us (23%)
  other arithmetic  66.6 us (9%)
  local copies, waits for them, and re-layouts  52.6 us (7%)
  starting transfers between devices  39.6 us (5%)
    ppermute x44, waiting for transfers between devices, swap(): return lax.ppermute(value, axis, [(i, i ^ mask) for i in range(size)])  412 us
    dot_general x11, matrix products, dot(): return jnp.dot(a, b, preferred_element_type=f32)  74.4 us
    dot_general x22, matrix products, dot_tn(): lax.dot_general(a, b, (((0,), (0,)), ((), ())), preferred_element_type=f32)  51 us
    dot_general x9, matrix products, dot_nt(): lax.dot_general(a, b, (((1,), (1,)), ((), ())), preferred_element_type=f32)  45.1 us
    ppermute x44, starting transfers between devices, swap(): return lax.ppermute(value, axis, [(i, i ^ mask) for i in range(size)])  39.6 us
    unnamed x195, local copies, waits for them, and re-layouts  21.8 us
  transfers between devices with their start and end apart: 44, of which 16 were waited for; matrix products, arithmetic and copies ran while one was open for 28% of the time, Pallas kernels for 0%

profile of v1, /device:TPU:0, one launch (start us, length us, event | category | flops | bytes accessed | tf_op | source)
XLA Modules:
  0.0 749.6 jit_solution(10373548526850726667)
XLA Ops:
  54.7 80.1 %collective-permute-done.38 = f32[256,2048]{1,0:T(8,128)} collective-permute-done((f32[256,2048]{1,0:T(8,128)}, f32[256,2048]{1,0:T(8,128)}, u32[]{:S(2)}, u32[]{:S(2)}) %collective-permute-start.38) | collective-permute-done | bytes 2097184 | tf_op jit(solution)/shard_map/ppermute | solution.py:59
  139.6 5.8 fusion.18
  148.0 35.5 %collective-permute-done.39 = f32[256,2048]{1,0:T(8,128)S(1)} collective-permute-done((f32[256,2048]{1,0:T(8,128)}, f32[256,2048]{1,0:T(8,128)S(1)}, u32[]{:S(2)}, u32[]{:S(2)}) %collective-permute-start.39) | collective-permute-done | bytes 2097184 | tf_op jit(solution)/shard_map/ppermute | solution.py:59
  188.7 8.6 %fusion.107 = f32[512,1536]{1,0:T(8,128)} fusion(bf16[512,2048]{1,0:T(8,128)(2,1)S(1)} %multiply_convert_fusion.3, bf16[2048,1536]{1,0:T(8,128)(2,1)} %param.23), kind=kOutput, calls=%fused_computation.224 | convolution fusion | flops 3221225472 | bytes 11534336 | tf_op jit(solution)/shard_map/dot_general | solution.py:63
  197.3 9.0 %multiply_convert_fusion.8 = (bf16[512,1536]{1,0:T(8,128)(2,1)S(1)}, bf16[512,1536]{1,0:T(8,128)(2,1)S(1)}, bf16[512,1536]{1,0:T(8,128)(2,1)}) fusion(f32[512,1536]{1,0:T(8,128)S(1)} %fusion.18, f32[512,1536]{1,0:T(8,128)} %fusion.107, bf16[512,2048]{1,0:T(8,128)(2,1)S(1)} %multiply_convert_fusion.3, bf16[2048,1536]{1,0:T(8,128)(2,1)} %param.22), kind=kOutput, calls=%fused_computation.38 | convolution fusion | flops 3233021952 | bytes 19398656 | tf_op jit(solution)/shard_map/dot_general | solution.py:63
  206.3 8.9 %fusion.109 = f32[512,2048]{1,0:T(8,128)} fusion(bf16[512,1536]{1,0:T(8,128)(2,1)S(1)} %get-tuple-element.35, bf16[2048,1536]{1,0:T(8,128)(2,1)} %param.22), kind=kOutput, calls=%fused_computation.226 | convolution fusion | flops 3221225472 | bytes 12058624 | tf_op jit(solution)/shard_map/dot_general | solution.py:67
  215.2 26.1 %collective-permute-done.33 = f32[256,2048]{1,0:T(8,128)S(1)} collective-permute-done((f32[256,2048]{1,0:T(8,128)}, f32[256,2048]{1,0:T(8,128)S(1)}, u32[]{:S(2)}, u32[]{:S(2)}) %collective-permute-start.33) | collective-permute-done | bytes 2097184 | tf_op jit(solution)/shard_map/ppermute | solution.py:59
  242.9 7.3 convolution_add_fusion
  252.3 5.8 fusion.108
  263.7 7.9 %fusion.113 = f32[512,1536]{1,0:T(8,128)} fusion(bf16[512,2048]{1,0:T(8,128)(2,1)S(1)} %fusion.5, bf16[1536,2048]{1,0:T(8,128)(2,1)} %param.24), kind=kOutput, calls=%fused_computation.230 | convolution fusion | flops 3221225472 | bytes 11534336 | tf_op jit(solution)/shard_map/dot_general | solution.py:67
  272.1 15.9 %collective-permute-done.34 = f32[256,2048]{1,0:T(8,128)S(1)} collective-permute-done((f32[256,2048]{1,0:T(8,128)S(1)}, f32[256,2048]{1,0:T(8,128)S(1)}, u32[]{:S(2)}, u32[]{:S(2)}) %collective-permute-start.34) | collective-permute-done | bytes 2097184 | tf_op jit(solution)/shard_map/ppermute | solution.py:59
  303.2 10.5 %fusion.115 = f32[1024,1536]{1,0:T(8,128)} fusion(bf16[1024,2048]{1,0:T(8,128)(2,1)S(1)} %fusion.1, bf16[1536,2048]{1,0:T(8,128)(2,1)} %param.24), kind=kOutput, calls=%fused_computation.232 | convolution fusion | flops 6442450944 | bytes 16777216 | tf_op jit(solution)/shard_map/dot_general | solution.py:67
  313.7 27.5 %collective-permute-done.7 = f32[256,2048]{1,0:T(8,128)} collective-permute-done((f32[256,2048]{1,0:T(8,128)S(1)}, f32[256,2048]{1,0:T(8,128)}, u32[]{:S(2)}, u32[]{:S(2)}) %collective-permute-start.7) | collective-permute-done | bytes 2097184 | tf_op jit(solution)/shard_map/ppermute | solution.py:59
  343.2 42.5 %collective-permute-done.4 = f32[256,2048]{1,0:T(8,128)} collective-permute-done((f32[256,2048]{1,0:T(8,128)S(1)}, f32[256,2048]{1,0:T(8,128)}, u32[]{:S(2)}, u32[]{:S(2)}) %collective-permute-start.4) | collective-permute-done | bytes 2097184 | tf_op jit(solution)/shard_map/ppermute | solution.py:59
  392.2 8.7 %fusion.116 = f32[1024,1536]{1,0:T(8,128)} fusion(bf16[1024,2048]{1,0:T(8,128)(2,1)S(1)} %fusion, bf16[2048,1536]{1,0:T(8,128)(2,1)S(1)} %bitcast.187), kind=kOutput, calls=%fused_computation.233 | convolution fusion | flops 6442450944 | bytes 16777216 | tf_op jit(solution)/shard_map/dot_general | solution.py:63
  400.8 16.0 %multiply_convert_fusion = (bf16[1024,1536]{1,0:T(8,128)(2,1)}, bf16[1024,1536]{1,0:T(8,128)(2,1)}, bf16[1024,1536]{1,0:T(8,128)(2,1)}) fusion(f32[1024,1536]{1,0:T(8,128)} %fusion.116, f32[1024,1536]{1,0:T(8,128)} %fusion.115, bf16[1024,2048]{1,0:T(8,128)(2,1)S(1)} %fusion, bf16[2048,1536]{1,0:T(8,128)(2,1)} %param.23), kind=kOutput, calls=%fused_computation.9 | convolution fusion | flops 6466043904 | bytes 32505856 | tf_op jit(solution)/shard_map/dot_general | solution.py:63
  416.8 4.7 multiply_reduce_fusion
  421.6 5.5 fusion.97
  438.5 8.0 %fusion.114 = f32[512,1536]{1,0:T(8,128)} fusion(bf16[512,2048]{1,0:T(8,128)(2,1)S(1)} %copy-done.27, bf16[2048,1536]{1,0:T(8,128)(2,1)} %param.22), kind=kOutput, calls=%fused_computation.231 | convolution fusion | flops 3221225472 | bytes 11534336 | tf_op jit(solution)/shard_map/dot_general | solution.py:63
  465.8 10.0 %multiply_convert_fusion.5 = (bf16[512,1536]{1,0:T(8,128)(2,1)}, bf16[512,1536]{1,0:T(8,128)(2,1)}, bf16[512,1536]{1,0:T(8,128)(2,1)}) fusion(f32[512,1536]{1,0:T(8,128)} %fusion.114, f32[512,1536]{1,0:T(8,128)} %fusion.113, bf16[512,2048]{1,0:T(8,128)(2,1)S(1)} %copy-done.27, bf16[2048,1536]{1,0:T(8,128)(2,1)} %param.23), kind=kOutput, calls=%fused_computation.33 | convolution fusion | flops 3233021952 | bytes 19398656 | tf_op jit(solution)/shard_map/dot_general | solution.py:63
  475.8 5.8 fusion.8
  502.6 5.0 fusion.9
  511.9 52.9 %collective-permute-done.25 = f32[512,256]{1,0:T(8,128)S(1)} collective-permute-done((f32[512,256]{1,0:T(8,128)S(1)}, f32[512,256]{1,0:T(8,128)S(1)}, u32[]{:S(2)}, u32[]{:S(2)}) %collective-permute-start.25) | collective-permute-done | bytes 524320 | tf_op jit(solution)/shard_map/ppermute | solution.py:59
  577.7 4.9 collective-permute-done.27
  587.2 4.9 convolution_add_fusion.3
  592.1 17.8 %collective-permute-done.10 = f32[256,2048]{1,0:T(8,128)S(1)} collective-permute-done((f32[256,2048]{1,0:T(8,128)S(1)}, f32[256,2048]{1,0:T(8,128)S(1)}, u32[]{:S(2)}, u32[]{:S(2)}) %collective-permute-start.10) | collective-permute-done | bytes 2097184 | tf_op jit(solution)/shard_map/ppermute | solution.py:59
  618.6 8.6 %collective-permute-done.42 = f32[256,1536]{1,0:T(8,128)} collective-permute-done((f32[256,1536]{1,0:T(8,128)}, f32[256,1536]{1,0:T(8,128)}, u32[]{:S(2)}, u32[]{:S(2)}) %collective-permute-start.42) | collective-permute-done | bytes 1572896 | tf_op jit(solution)/shard_map/ppermute | solution.py:59
  627.4 59.5 %collective-permute-done.22 = f32[256,1024]{1,0:T(8,128)} collective-permute-done((f32[256,1024]{1,0:T(8,128)}, f32[256,1024]{1,0:T(8,128)}, u32[]{:S(2)}, u32[]{:S(2)}) %collective-permute-start.22) | collective-permute-done | bytes 1048608 | tf_op jit(solution)/shard_map/ppermute | solution.py:59
  687.0 6.4 convolution_add_fusion.2
  701.0 4.9 convolution_add_fusion.1
  706.0 15.0 %collective-permute-done.17 = f32[256,1024]{1,0:T(8,128)S(1)} collective-permute-done((f32[256,1024]{1,0:T(8,128)S(1)}, f32[256,1024]{1,0:T(8,128)S(1)}, u32[]{:S(2)}, u32[]{:S(2)}) %collective-permute-start.17) | collective-permute-done | bytes 1048608 | tf_op jit(solution)/shard_map/ppermute | solution.py:59
  720.9 22.4 %collective-permute-done.19 = f32[256,1024]{1,0:T(8,128)S(1)} collective-permute-done((f32[256,1024]{1,0:T(8,128)S(1)}, f32[256,1024]{1,0:T(8,128)S(1)}, u32[]{:S(2)}, u32[]{:S(2)}) %collective-permute-start.19) | collective-permute-done | bytes 1048608 | tf_op jit(solution)/shard_map/ppermute | solution.py:59
  (406 shorter events, 195.0 us)
Async XLA Ops:
  39.8 94.9 %collective-permute-start.38 = (f32[256,2048]{1,0:T(8,128)}, f32[256,2048]{1,0:T(8,128)}, u32[]{:S(2)}, u32[]{:S(2)}) collective-permute-start(f32[256,2048]{1,0:T(8,128)} %get-tuple-element.19), channel_id=1, source_target_pairs={{0,16},{4,20},{8,24},{12,28},{16,0},{20,4},{24,8},{28,12},{1,17},{... | collective-permute-start | bytes 6291464 | tf_op jit(solution)/shard_map/ppermute | solution.py:59
  45.5 90.9 %collective-permute-start.1 = (f32[256,2048]{1,0:T(8,128)}, f32[256,2048]{1,0:T(8,128)}, u32[]{:S(2)}, u32[]{:S(2)}) collective-permute-start(f32[256,2048]{1,0:T(8,128)} %slice_add_fusion.4), channel_id=1, source_target_pairs={{0,2},{1,3},{2,0},{3,1},{4,6},{5,7},{6,4},{7,5},{8,10},{9,11},{10,... | collective-permute-start | bytes 6291464 | tf_op jit(solution)/shard_map/ppermute | solution.py:59
  46.9 98.4 %collective-permute-start.36 = (f32[256,2048]{1,0:T(8,128)}, f32[256,2048]{1,0:T(8,128)}, u32[]{:S(2)}, u32[]{:S(2)}) collective-permute-start(f32[256,2048]{1,0:T(8,128)} %get-tuple-element.19), channel_id=1, source_target_pairs={{0,4},{4,0},{8,12},{12,8},{16,20},{20,16},{24,28},{28,24},{1,5},{5... | collective-permute-start | bytes 6291464 | tf_op jit(solution)/shard_map/ppermute | solution.py:59
  134.8 48.7 %collective-permute-start.39 = (f32[256,2048]{1,0:T(8,128)}, f32[256,2048]{1,0:T(8,128)S(1)}, u32[]{:S(2)}, u32[]{:S(2)}) collective-permute-start(f32[256,2048]{1,0:T(8,128)} %collective-permute-done.38), channel_id=1, source_target_pairs={{0,4},{4,0},{8,12},{12,8},{16,20},{20,16},{24,28},{28,24},{1,5},{5... | collective-permute-start | bytes 6291464 | tf_op jit(solution)/shard_map/ppermute | solution.py:59
  138.9 48.7 %collective-permute-start.2 = (f32[256,2048]{1,0:T(8,128)S(1)}, f32[256,2048]{1,0:T(8,128)S(1)}, u32[]{:S(2)}, u32[]{:S(2)}) collective-permute-start(f32[256,2048]{1,0:T(8,128)S(1)} %get-tuple-element.22), channel_id=1, source_target_pairs={{0,1},{1,0},{2,3},{3,2},{4,5},{5,4},{6,7},{7,6},{8,9},{9,8},{10,11... | collective-permute-start | bytes 6291464 | tf_op jit(solution)/shard_map/ppermute | solution.py:59
  145.4 114.2 %collective-permute-start.37 = (f32[256,2048]{1,0:T(8,128)}, f32[256,2048]{1,0:T(8,128)S(1)}, u32[]{:S(2)}, u32[]{:S(2)}) collective-permute-start(f32[256,2048]{1,0:T(8,128)} %collective-permute-done.36), channel_id=1, source_target_pairs={{0,1},{1,0},{2,3},{3,2},{4,5},{5,4},{6,7},{7,6},{8,9},{9,8},{10,11... | collective-permute-start | bytes 6291464 | tf_op jit(solution)/shard_map/ppermute | solution.py:59
  147.5 124.0 %collective-permute-start.31 = (f32[256,2048]{1,0:T(8,128)}, f32[256,2048]{1,0:T(8,128)}, u32[]{:S(2)}, u32[]{:S(2)}) collective-permute-start(f32[256,2048]{1,0:T(8,128)} %broadcast_multiply_fusion.1), channel_id=1, source_target_pairs={{0,4},{4,0},{8,12},{12,8},{16,20},{20,16},{24,28},{28,24},{1,5},{5... | collective-permute-start | bytes 6291464 | tf_op jit(solution)/shard_map/ppermute | solution.py:59
  148.0 93.3 %collective-permute-start.33 = (f32[256,2048]{1,0:T(8,128)}, f32[256,2048]{1,0:T(8,128)S(1)}, u32[]{:S(2)}, u32[]{:S(2)}) collective-permute-start(f32[256,2048]{1,0:T(8,128)} %broadcast_multiply_fusion.1), channel_id=1, source_target_pairs={{0,16},{4,20},{8,24},{12,28},{16,0},{20,4},{24,8},{28,12},{1,17},{... | collective-permute-start | bytes 6291464 | tf_op jit(solution)/shard_map/ppermute | solution.py:59
  187.6 109.0 %collective-permute-start.40 = (f32[512,2048]{1,0:T(8,128)}, f32[512,2048]{1,0:T(8,128)S(1)}, u32[]{:S(2)}, u32[]{:S(2)}) collective-permute-start(f32[512,2048]{1,0:T(8,128)} %pad_maximum_fusion.7), channel_id=1, source_target_pairs={{0,1},{1,0},{2,3},{3,2},{4,5},{5,4},{6,7},{7,6},{8,9},{9,8},{10,11... | collective-permute-start | bytes 12582920 | tf_op jit(solution)/shard_map/ppermute | solution.py:59
  241.3 46.6 %collective-permute-start.34 = (f32[256,2048]{1,0:T(8,128)S(1)}, f32[256,2048]{1,0:T(8,128)S(1)}, u32[]{:S(2)}, u32[]{:S(2)}) collective-permute-start(f32[256,2048]{1,0:T(8,128)S(1)} %collective-permute-done.33), channel_id=1, source_target_pairs={{0,4},{4,0},{8,12},{12,8},{16,20},{20,16},{24,28},{28,24},{1,5},{5... | collective-permute-start | bytes 6291464 | tf_op jit(solution)/shard_map/ppermute | solution.py:59
  271.5 145.3 %collective-permute-start.32 = (f32[256,2048]{1,0:T(8,128)}, f32[256,2048]{1,0:T(8,128)}, u32[]{:S(2)}, u32[]{:S(2)}) collective-permute-start(f32[256,2048]{1,0:T(8,128)} %collective-permute-done.31), channel_id=1, source_target_pairs={{0,1},{1,0},{2,3},{3,2},{4,5},{5,4},{6,7},{7,6},{8,9},{9,8},{10,11... | collective-permute-start | bytes 6291464 | tf_op jit(solution)/shard_map/ppermute | solution.py:59
  290.6 98.5 %collective-permute-start.35 = (f32[512,2048]{1,0:T(8,128)}, f32[512,2048]{1,0:T(8,128)}, u32[]{:S(2)}, u32[]{:S(2)}) collective-permute-start(f32[512,2048]{1,0:T(8,128)} %pad_maximum_fusion.6), channel_id=1, source_target_pairs={{0,1},{1,0},{2,3},{3,2},{4,5},{5,4},{6,7},{7,6},{8,9},{9,8},{10,11... | collective-permute-start | bytes 12582920 | tf_op jit(solution)/shard_map/ppermute | solution.py:59
  292.5 48.7 %collective-permute-start.7 = (f32[256,2048]{1,0:T(8,128)S(1)}, f32[256,2048]{1,0:T(8,128)}, u32[]{:S(2)}, u32[]{:S(2)}) collective-permute-start(f32[256,2048]{1,0:T(8,128)S(1)} %slice_add_fusion.2), channel_id=1, source_target_pairs={{0,2},{1,3},{2,0},{3,1},{4,6},{5,7},{6,4},{7,5},{8,10},{9,11},{10,... | collective-permute-start | bytes 6291464 | tf_op jit(solution)/shard_map/ppermute | solution.py:59
  296.1 89.6 %collective-permute-start.4 = (f32[256,2048]{1,0:T(8,128)S(1)}, f32[256,2048]{1,0:T(8,128)}, u32[]{:S(2)}, u32[]{:S(2)}) collective-permute-start(f32[256,2048]{1,0:T(8,128)S(1)} %slice_add_fusion.3), channel_id=1, source_target_pairs={{0,2},{1,3},{2,0},{3,1},{4,6},{5,7},{6,4},{7,5},{8,10},{9,11},{10,... | collective-permute-start | bytes 6291464 | tf_op jit(solution)/shard_map/ppermute | solution.py:59
  343.1 73.7 %collective-permute-start.8 = (f32[256,2048]{1,0:T(8,128)S(1)}, f32[256,2048]{1,0:T(8,128)}, u32[]{:S(2)}, u32[]{:S(2)}) collective-permute-start(f32[256,2048]{1,0:T(8,128)S(1)} %add.287), channel_id=1, source_target_pairs={{0,1},{1,0},{2,3},{3,2},{4,5},{5,4},{6,7},{7,6},{8,9},{9,8},{10,11... | collective-permute-start | bytes 6291464 | tf_op jit(solution)/shard_map/ppermute | solution.py:59
  463.3 45.3 %collective-permute-start.9 = (f32[256,2048]{1,0:T(8,128)}, f32[256,2048]{1,0:T(8,128)S(1)}, u32[]{:S(2)}, u32[]{:S(2)}) collective-permute-start(f32[256,2048]{1,0:T(8,128)} %slice.136), channel_id=1, source_target_pairs={{0,1},{1,0},{2,3},{3,2},{4,5},{5,4},{6,7},{7,6},{8,9},{9,8},{10,11... | collective-permute-start | bytes 6291464 | tf_op jit(solution)/shard_map/ppermute | solution.py:59
  496.2 73.4 %collective-permute-start.21 = (f32[256,1024]{1,0:T(8,128)}, f32[256,1024]{1,0:T(8,128)}, u32[]{:S(2)}, u32[]{:S(2)}) collective-permute-start(f32[256,1024]{1,0:T(8,128)} %fusion.51), channel_id=1, source_target_pairs={{0,4},{4,0},{8,12},{12,8},{16,20},{20,16},{24,28},{28,24},{1,5},{5... | collective-permute-start | bytes 3145736 | tf_op jit(solution)/shard_map/ppermute | solution.py:59
  497.8 76.3 %collective-permute-start.18 = (f32[256,1024]{1,0:T(8,128)}, f32[256,1024]{1,0:T(8,128)}, u32[]{:S(2)}, u32[]{:S(2)}) collective-permute-start(f32[256,1024]{1,0:T(8,128)} %fusion.57), channel_id=1, source_target_pairs={{0,4},{4,0},{8,12},{12,8},{16,20},{20,16},{24,28},{28,24},{1,5},{5... | collective-permute-start | bytes 3145736 | tf_op jit(solution)/shard_map/ppermute | solution.py:59
  498.2 69.6 %collective-permute-start.28 = (f32[512,256]{1,0:T(8,128)S(1)}, f32[512,256]{1,0:T(8,128)S(1)}, u32[]{:S(2)}, u32[]{:S(2)}) collective-permute-start(f32[512,256]{1,0:T(8,128)S(1)} %fusion.39), channel_id=1, source_target_pairs={{0,4},{4,0},{8,12},{12,8},{16,20},{20,16},{24,28},{28,24},{1,5},{5... | collective-permute-start | bytes 1572872 | tf_op jit(solution)/shard_map/ppermute | solution.py:59
  507.5 57.3 %collective-permute-start.25 = (f32[512,256]{1,0:T(8,128)S(1)}, f32[512,256]{1,0:T(8,128)S(1)}, u32[]{:S(2)}, u32[]{:S(2)}) collective-permute-start(f32[512,256]{1,0:T(8,128)S(1)} %fusion.45), channel_id=1, source_target_pairs={{0,4},{4,0},{8,12},{12,8},{16,20},{20,16},{24,28},{28,24},{1,5},{5... | collective-permute-start | bytes 1572872 | tf_op jit(solution)/shard_map/ppermute | solution.py:59
  509.9 77.0 %collective-permute-start.41 = (f32[256,1536]{1,0:T(8,128)S(1)}, f32[256,1536]{1,0:T(8,128)S(1)}, u32[]{:S(2)}, u32[]{:S(2)}) collective-permute-start(f32[256,1536]{1,0:T(8,128)S(1)} %fusion.10), channel_id=1, source_target_pairs={{0,8},{4,12},{8,0},{12,4},{16,24},{20,28},{24,16},{28,20},{1,9},{5... | collective-permute-start | bytes 4718600 | tf_op jit(solution)/shard_map/ppermute | solution.py:59
  564.8 45.0 %collective-permute-start.10 = (f32[256,2048]{1,0:T(8,128)S(1)}, f32[256,2048]{1,0:T(8,128)S(1)}, u32[]{:S(2)}, u32[]{:S(2)}) collective-permute-start(f32[256,2048]{1,0:T(8,128)S(1)} %slice_add_fusion), channel_id=1, source_target_pairs={{0,2},{1,3},{2,0},{3,1},{4,6},{5,7},{6,4},{7,5},{8,10},{9,11},{10,... | collective-permute-start | bytes 6291464 | tf_op jit(solution)/shard_map/ppermute | solution.py:59
  574.1 44.0 %collective-permute-start.20 = (f32[256,1024]{1,0:T(8,128)}, f32[256,1024]{1,0:T(8,128)S(1)}, u32[]{:S(2)}, u32[]{:S(2)}) collective-permute-start(f32[256,1024]{1,0:T(8,128)} %fusion.54), channel_id=1, source_target_pairs={{0,4},{4,0},{8,12},{12,8},{16,20},{20,16},{24,28},{28,24},{1,5},{5... | collective-permute-start | bytes 3145736 | tf_op jit(solution)/shard_map/ppermute | solution.py:59
  582.7 112.6 %collective-permute-start.24 = (f32[512,256]{1,0:T(8,128)S(1)}, f32[512,256]{1,0:T(8,128)}, u32[]{:S(2)}, u32[]{:S(2)}) collective-permute-start(f32[512,256]{1,0:T(8,128)S(1)} %fusion.48), channel_id=1, source_target_pairs={{0,4},{4,0},{8,12},{12,8},{16,20},{20,16},{24,28},{28,24},{1,5},{5... | collective-permute-start | bytes 1572872 | tf_op jit(solution)/shard_map/ppermute | solution.py:59
  584.0 43.2 %collective-permute-start.42 = (f32[256,1536]{1,0:T(8,128)}, f32[256,1536]{1,0:T(8,128)}, u32[]{:S(2)}, u32[]{:S(2)}) collective-permute-start(f32[256,1536]{1,0:T(8,128)} %fusion.9), channel_id=1, source_target_pairs={{0,8},{4,12},{8,0},{12,4},{16,24},{20,28},{24,16},{28,20},{1,9},{5... | collective-permute-start | bytes 4718600 | tf_op jit(solution)/shard_map/ppermute | solution.py:59
  586.9 114.1 %collective-permute-start.43 = (f32[1536,256]{1,0:T(8,128)}, f32[1536,256]{1,0:T(8,128)}, u32[]{:S(2)}, u32[]{:S(2)}) collective-permute-start(f32[1536,256]{1,0:T(8,128)} %fusion.8), channel_id=1, source_target_pairs={{0,8},{4,12},{8,0},{12,4},{16,24},{20,28},{24,16},{28,20},{1,9},{5... | collective-permute-start | bytes 4718600 | tf_op jit(solution)/shard_map/ppermute | solution.py:59
  609.8 77.1 %collective-permute-start.22 = (f32[256,1024]{1,0:T(8,128)}, f32[256,1024]{1,0:T(8,128)}, u32[]{:S(2)}, u32[]{:S(2)}) collective-permute-start(f32[256,1024]{1,0:T(8,128)} %convolution_add_fusion.4), channel_id=1, source_target_pairs={{0,8},{4,12},{8,0},{12,4},{16,24},{20,28},{24,16},{28,20},{1,9},{5... | collective-permute-start | bytes 3145736 | tf_op jit(solution)/shard_map/ppermute | solution.py:59
  618.1 78.0 %collective-permute-start.26 = (f32[512,256]{1,0:T(8,128)}, f32[512,256]{1,0:T(8,128)S(1)}, u32[]{:S(2)}, u32[]{:S(2)}) collective-permute-start(f32[512,256]{1,0:T(8,128)} %convolution_add_fusion.10), channel_id=1, source_target_pairs={{0,8},{4,12},{8,0},{12,4},{16,24},{20,28},{24,16},{28,20},{1,9},{5... | collective-permute-start | bytes 1572872 | tf_op jit(solution)/shard_map/ppermute | solution.py:59
  627.2 68.9 %collective-permute-start.30 = (f32[512,256]{1,0:T(8,128)}, f32[512,256]{1,0:T(8,128)S(1)}, u32[]{:S(2)}, u32[]{:S(2)}) collective-permute-start(f32[512,256]{1,0:T(8,128)} %fusion.20), channel_id=1, source_target_pairs={{0,16},{4,20},{8,24},{12,28},{16,0},{20,4},{24,8},{28,12},{1,17},{... | collective-permute-start | bytes 1572872 | tf_op jit(solution)/shard_map/ppermute | solution.py:59
  687.0 60.1 %collective-permute-start.11 = (f32[256,2048]{1,0:T(8,128)}, f32[256,2048]{1,0:T(8,128)S(1)}, u32[]{:S(2)}, u32[]{:S(2)}) collective-permute-start(f32[256,2048]{1,0:T(8,128)} %get-tuple-element.24), channel_id=1, source_target_pairs={{0,1},{1,0},{2,3},{3,2},{4,5},{5,4},{6,7},{7,6},{8,9},{9,8},{10,11... | collective-permute-start | bytes 6291464 | tf_op jit(solution)/shard_map/ppermute | solution.py:59
  696.1 47.2 %collective-permute-start.19 = (f32[256,1024]{1,0:T(8,128)S(1)}, f32[256,1024]{1,0:T(8,128)S(1)}, u32[]{:S(2)}, u32[]{:S(2)}) collective-permute-start(f32[256,1024]{1,0:T(8,128)S(1)} %copy-done.77), channel_id=1, source_target_pairs={{0,8},{4,12},{8,0},{12,4},{16,24},{20,28},{24,16},{28,20},{1,9},{5... | collective-permute-start | bytes 3145736 | tf_op jit(solution)/shard_map/ppermute | solution.py:59
  696.1 48.8 %collective-permute-start.23 = (f32[256,1024]{1,0:T(8,128)S(1)}, f32[256,1024]{1,0:T(8,128)S(1)}, u32[]{:S(2)}, u32[]{:S(2)}) collective-permute-start(f32[256,1024]{1,0:T(8,128)S(1)} %fusion.15), channel_id=1, source_target_pairs={{0,16},{4,20},{8,24},{12,28},{16,0},{20,4},{24,8},{28,12},{1,17},{... | collective-permute-start | bytes 3145736 | tf_op jit(solution)/shard_map/ppermute | solution.py:59
  (107 other events, 1202.0 us)

commit v2 on v1

v2 whole, which is shorter than its diff:
```python
import functools

import jax
import jax.numpy as jnp
from jax import lax
from jax.experimental import pallas as pl
from jax.experimental.pallas import tpu as pltpu
from jax.sharding import PartitionSpec as P

SEQ_LEN = 256


EPS = 1e-06
THETA = 1000000.0

f32 = jnp.float32
b16 = jnp.bfloat16


def rms_norm(values, gain):
    inv_rms = lax.rsqrt(jnp.mean(values * values, axis=-1, keepdims=True) + EPS)
    unit_rows = values * inv_rms
    return (unit_rows * gain, unit_rows, inv_rms)


def rms_back(grads, gain, unit_rows, inv_rms):
    scaled = grads * gain
    return inv_rms * (scaled - unit_rows * jnp.mean(scaled * unit_rows, axis=-1, keepdims=True))


def swap(value, axis, mask):
    size = lax.axis_size(axis)
    return lax.ppermute(value, axis, [(i, i ^ mask) for i in range(size)])


class Sequence:
    def __init__(self):
        self.token = None

    def __call__(self, *values):
        if self.token is None:
            out = lax.optimization_barrier(values)
        else:
            *out, self.token = lax.optimization_barrier((*values, self.token))
        self.token = out[0].reshape(-1)[:1] if self.token is None else self.token
        return out[0] if len(out) == 1 else tuple(out)


def dot(a, b):
    return jnp.dot(a, b, preferred_element_type=f32)


def dot_nt(a, b):
    return lax.dot_general(a, b, (((1,), (1,)), ((), ())), preferred_element_type=f32)


def dot_tn(a, b):
    return lax.dot_general(a, b, (((0,), (0,)), ((), ())), preferred_element_type=f32)


TILE = 512
PIECES = 4


def vmem(mib=60):
    return pltpu.CompilerParams(vmem_limit_bytes=mib << 20)


def whole(shape):
    return pl.BlockSpec(shape, lambda *_: (0,) * len(shape))


def gated(nb, cb, wg_ref, wu_ref, wd_ref):
    gate_pre = dot(nb[...], wg_ref[...])
    up_pre = dot(nb[...], wu_ref[...])
    d_hidden = dot_nt(cb[...], wd_ref[...])
    sig = jax.nn.sigmoid(gate_pre)
    act = gate_pre * sig
    hidden = (act * up_pre).astype(b16)
    d_up = (d_hidden * act).astype(b16)
    d_gate = (d_hidden * up_pre * (sig * (1.0 + gate_pre * (1.0 - sig)))).astype(b16)
    return hidden, d_gate, d_up


def own_kernel(ra_ref, *refs):
    rb_refs, refs = refs[:PIECES], refs[PIECES:]
    cot_ref, g_ref, wg_ref, wu_ref, wd_ref, normed_ref, hid_ref, dg_ref, du_ref, dna_ref = refs[:10]
    dnb_refs, (gain_ref, rms_ref) = refs[10:-2], refs[-2:]
    step = pl.program_id(0)
    half = ra_ref.shape[0]
    part = half // PIECES

    @pl.when(step == 0)
    def _():
        for i, ref in enumerate((ra_ref, *rb_refs)):
            r = ref[...]
            at = 0 if i == 0 else half + (i - 1) * part
            inv = lax.rsqrt(jnp.mean(r * r, axis=-1, keepdims=True) + EPS)
            rms_ref[at : at + r.shape[0], :] = inv
            normed_ref[at : at + r.shape[0], :] = (r * inv * g_ref[...]).astype(b16)
        dna_ref[...] = jnp.zeros_like(dna_ref)
        for ref in dnb_refs:
            ref[...] = jnp.zeros_like(ref)

    hidden, d_gate, d_up = gated(normed_ref, cot_ref, wg_ref, wu_ref, wd_ref)
    hid_ref[...] = hidden
    dg_ref[...] = d_gate
    du_ref[...] = d_up
    dna_ref[...] += dot_nt(d_gate[:half], wg_ref[...]) + dot_nt(d_up[:half], wu_ref[...])
    far = dot_nt(d_gate[half:], wg_ref[...]) + dot_nt(d_up[half:], wu_ref[...])
    for i, ref in enumerate(dnb_refs):
        ref[...] += far[i * part : (i + 1) * part]

    @pl.when(step == pl.num_programs(0) - 1)
    def _():
        total = jnp.sum(dna_ref[...] * (ra_ref[...] * rms_ref[:half, :]), axis=0, keepdims=True)
        for i, (r_ref, d_ref) in enumerate(zip(rb_refs, dnb_refs)):
            at = half + i * part
            unit = r_ref[...] * rms_ref[at : at + part, :]
            total += jnp.sum(d_ref[...] * unit, axis=0, keepdims=True)
        gain_ref[...] = total


def own_feed(r_a, r_b, cot, g, w_gate, w_up, w_down):
    half, width = r_a.shape
    rows, hidden = 2 * half, w_gate.shape[1]
    col = pl.BlockSpec((rows, TILE), lambda i: (0, i))
    wide = jax.ShapeDtypeStruct((rows, hidden), b16)
    piece = (half // PIECES, width)
    return pl.pallas_call(
        own_kernel,
        grid=(hidden // TILE,),
        in_specs=[whole((half, width))]
        + [whole(piece)] * PIECES
        + [
            whole((rows, width)),
            whole((1, width)),
            pl.BlockSpec((width, TILE), lambda i: (0, i)),
            pl.BlockSpec((width, TILE), lambda i: (0, i)),
            pl.BlockSpec((TILE, width), lambda i: (i, 0)),
        ],
        out_specs=[
            whole((rows, width)),
            col,
            col,
            col,
            whole((half, width)),
        ]
        + [whole(piece)] * PIECES
        + [whole((1, width))],
        out_shape=[
            jax.ShapeDtypeStruct((rows, width), b16),
            wide,
            wide,
            wide,
            jax.ShapeDtypeStruct((half, width), f32),
        ]
        + [jax.ShapeDtypeStruct(piece, f32)] * PIECES
        + [jax.ShapeDtypeStruct((1, width), f32)],
        scratch_shapes=[pltpu.VMEM((rows, 1), f32)],
        compiler_params=vmem(),
        name="own_feed",
    )(r_a, *r_b, cot, g.reshape(1, -1), w_gate, w_up, w_down)


def put_columns(at_ref, cc_ref, nb_ref, cb_ref, where_ref, count, block):
    for j in range(count):
        here = pl.ds(pl.multiple_of(where_ref[j] * block, 128), block)
        at_ref[j * block : (j + 1) * block, :] = nb_ref[:, here].T
        cc_ref[:, j * block : (j + 1) * block] = cb_ref[:, here]


def put_grads(sums, at_ref, cc_ref, hidden, d_gate, d_up, block, before=None):
    down = dot_tn(hidden, cc_ref[...])
    gate = dot(at_ref[...], d_gate)
    up = dot(at_ref[...], d_up)
    count = len(sums) // 2
    for j in range(count):
        part = slice(j * block, (j + 1) * block)
        for k, rows, fresh in (
            (j, slice(None), down[:, part]),
            (count + j, slice(0, block), gate[part]),
            (count + j, slice(block, 2 * block), up[part]),
        ):
            old = 0.0 if before is None else before[k][rows, :]
            sums[k][rows, :] = fresh + old


def rest_kernel(where_ref, nb_ref, cb_ref, hid_ref, dg_ref, du_ref, wd_ref, *rest):
    count = (len(rest) - 4) // 2
    ya_ref, yb_ref, *sums = rest[:-2]
    at_ref, cc_ref = rest[-2:]
    half = ya_ref.shape[0]
    block = cc_ref.shape[1] // count

    @pl.when(pl.program_id(0) == 0)
    def _():
        put_columns(at_ref, cc_ref, nb_ref, cb_ref, where_ref, count, block)
        ya_ref[...] = jnp.zeros_like(ya_ref)
        yb_ref[...] = jnp.zeros_like(yb_ref)

    hidden = hid_ref[...]
    ya_ref[...] += dot(hidden[:half], wd_ref[...])
    yb_ref[...] += dot(hidden[half:], wd_ref[...])
    put_grads(sums, at_ref, cc_ref, hidden, dg_ref[...], du_ref[...], block)


def sum_specs(count, block, hidden):
    specs = [pl.BlockSpec((TILE, block), lambda i, *_: (i, 0))] * count
    specs += [pl.BlockSpec((2 * block, TILE), lambda i, *_: (0, i))] * count
    shapes = [jax.ShapeDtypeStruct((hidden, block), f32)] * count
    shapes += [jax.ShapeDtypeStruct((2 * block, hidden), f32)] * count
    return specs, shapes


def own_rest(where, nb, cb, hidden, d_gate, d_up, w_down, block):
    rows, width = nb.shape
    count = where.shape[0]
    half, ff = rows // 2, hidden.shape[1]
    specs, shapes = sum_specs(count, block, ff)
    col = pl.BlockSpec((rows, TILE), lambda i, *_: (0, i))
    part = jax.ShapeDtypeStruct((half, width), f32)
    out = pl.pallas_call(
        rest_kernel,
        grid_spec=pltpu.PrefetchScalarGridSpec(
            num_scalar_prefetch=1,
            grid=(ff // TILE,),
            in_specs=[
                whole((rows, width)),
                whole((rows, width)),
                col,
                col,
                col,
                pl.BlockSpec((TILE, width), lambda i, *_: (i, 0)),
            ],
            out_specs=[whole((half, width)), whole((half, width))] + specs,
            scratch_shapes=[
                pltpu.VMEM((count * block, rows), b16),
                pltpu.VMEM((rows, count * block), b16),
            ],
        ),
        out_shape=[part, part] + shapes,
        compiler_params=vmem(),
        name="own_rest",
    )(where, nb, cb, hidden, d_gate, d_up, w_down)
    return out[0], out[1], list(out[2:])


def group_kernel(pieces, count, where_ref, *refs):
    n_refs, refs = refs[:pieces], refs[pieces:]
    c_refs, refs = refs[:pieces], refs[pieces:]
    g_ref, wg_ref, wu_ref, wd_ref = refs[:4]
    before = refs[4 : 4 + 2 * count]
    sums = refs[4 + 2 * count : 4 + 4 * count]
    nb_ref, cb_ref, at_ref, cc_ref = refs[4 + 4 * count :]
    block = cc_ref.shape[1] // count

    @pl.when(pl.program_id(0) == 0)
    def _():
        at = 0
        for n_ref, c_ref in zip(n_refs, c_refs):
            size = n_ref.shape[0]
            nb_ref[at : at + size, :] = (n_ref[...] * g_ref[...]).astype(b16)
            cb_ref[at : at + size, :] = (c_ref[...] * 0.5).astype(b16)
            at += size
        put_columns(at_ref, cc_ref, nb_ref, cb_ref, where_ref, count, block)

    hidden, d_gate, d_up = gated(nb_ref, cb_ref, wg_ref, wu_ref, wd_ref)
    put_grads(sums, at_ref, cc_ref, hidden, d_gate, d_up, block, before)


def group_feed(where, ns, cs, g, w_gate, w_up, w_down, before, block):
    width, ff = w_gate.shape
    count = where.shape[0]
    rows = sum(n.shape[0] for n in ns)
    specs, shapes = sum_specs(count, block, ff)
    return list(
        pl.pallas_call(
            functools.partial(group_kernel, len(ns), count),
            grid_spec=pltpu.PrefetchScalarGridSpec(
                num_scalar_prefetch=1,
                grid=(ff // TILE,),
                in_specs=[whole(a.shape) for a in (*ns, *cs)]
                + [
                    whole((1, width)),
                    pl.BlockSpec((width, TILE), lambda i, *_: (0, i)),
                    pl.BlockSpec((width, TILE), lambda i, *_: (0, i)),
                    pl.BlockSpec((TILE, width), lambda i, *_: (i, 0)),
                ]
                + specs,
                out_specs=specs,
                scratch_shapes=[
                    pltpu.VMEM((rows, width), b16),
                    pltpu.VMEM((rows, width), b16),
                    pltpu.VMEM((count * block, rows), b16),
                    pltpu.VMEM((rows, count * block), b16),
                ],
            ),
            out_shape=shapes,
            compiler_params=vmem(),
            name="group_feed",
        )(where, *ns, *cs, g.reshape(1, -1), w_gate, w_up, w_down, *before)
    )


def sum_kernel(count, *refs):
    a_ref, b_refs, outs = refs[0], refs[1 : 1 + count], refs[1 + count :]
    size = a_ref.shape[0] // count
    for i, b_ref in enumerate(b_refs):
        at = slice(i * size, (i + 1) * size)
        total = a_ref[at, :] + b_ref[...]
        outs[0][at, :] = total
        if len(outs) == 1 + count:
            outs[1 + i][...] = total
        elif len(outs) > 1:
            small = outs[1].shape[0]
            for j in range(size // small):
                outs[1 + i * (size // small) + j][...] = total[j * small : (j + 1) * small]


def sum_of(a, bs, split=False):
    shapes = [jax.ShapeDtypeStruct(a.shape, f32)]
    if split:
        shapes += [jax.ShapeDtypeStruct((a.shape[0] // PIECES, a.shape[1]), f32)] * PIECES
    return pl.pallas_call(
        functools.partial(sum_kernel, len(bs)),
        in_specs=[whole(x.shape) for x in (a, *bs)],
        out_specs=[whole(x.shape) for x in shapes],
        out_shape=shapes,
        grid=(1,),
        compiler_params=vmem(),
        name="sum_of",
    )(a, *bs)


def resid_kernel(x_at_ref, tok_ref, a_ref, b_ref, r_ref, n_ref, quarter_ref, *pieces):
    size = pieces[0].shape[0]
    for i, piece in enumerate(pieces):
        at = slice(i * size, (i + 1) * size)
        resid = tok_ref[at, :].astype(f32) + (a_ref[at, :] + b_ref[at, :])
        r_ref[at, :] = resid
        piece[...] = resid
        n_ref[at, :] = resid * lax.rsqrt(jnp.mean(resid * resid, axis=-1, keepdims=True) + EPS)
    small = quarter_ref.shape[0]
    quarter_ref[...] = n_ref[pl.ds(pl.multiple_of(x_at_ref[0] * small, small), small), :]


def resid_of(x_at, tok, a, b):
    rows, width = a.shape
    shapes = [(rows, width), (rows, width), (rows // 2, width)] + [(rows // PIECES, width)] * PIECES
    return pl.pallas_call(
        resid_kernel,
        grid_spec=pltpu.PrefetchScalarGridSpec(
            num_scalar_prefetch=1,
            grid=(1,),
            in_specs=[whole(a.shape)] * 3,
            out_specs=[whole(s) for s in shapes],
        ),
        out_shape=[jax.ShapeDtypeStruct(s, f32) for s in shapes],
        compiler_params=vmem(),
        name="resid_of",
    )(x_at, tok, a, b)


def feed(normed, cot, w_gate, w_up, w_down):
    gate_pre = dot(normed, w_gate)
    up_pre = dot(normed, w_up)
    d_hidden = dot_nt(cot, w_down)
    sigmoid_g = jax.nn.sigmoid(gate_pre)
    act_gate = gate_pre * sigmoid_g
    hidden = (act_gate * up_pre).astype(b16)
    d_up = (d_hidden * act_gate).astype(b16)
    d_gate = (d_hidden * up_pre * (sigmoid_g * (1.0 + gate_pre * (1.0 - sigmoid_g)))).astype(b16)
    return hidden, d_gate, d_up


def plain_grads(where, normed, cot, parts, block):
    hidden, d_gate, d_up = parts
    takes = [functools.partial(lax.dynamic_slice_in_dim, start_index=w * block, slice_size=block, axis=1) for w in where]
    pair = jnp.concatenate([d_gate, d_up], axis=1)
    both = [dot_tn(take(normed), pair) for take in takes]
    ff = hidden.shape[1]
    return [dot_tn(hidden, take(cot)) for take in takes] + [
        jnp.concatenate([b[:, :ff], b[:, ff:]]) for b in both
    ]


def plain_own_feed(r_a, r_b, cot, g, w_gate, w_up, w_down):
    resid = jnp.concatenate([r_a, *r_b])
    normed, unit, _ = rms_norm(resid, g)
    normed = normed.astype(b16)
    parts = feed(normed, cot, w_gate, w_up, w_down)
    total = dot_nt(parts[1], w_gate) + dot_nt(parts[2], w_up)
    half = r_a.shape[0]
    gain = jnp.sum(total * unit, axis=0, keepdims=True)
    return (normed, *parts, total[:half], *jnp.split(total[half:], PIECES), gain)


def plain_own_rest(where, nb, cb, hidden, d_gate, d_up, w_down, block):
    down = dot(hidden, w_down)
    half = nb.shape[0] // 2
    return down[:half], down[half:], plain_grads(where, nb, cb, (hidden, d_gate, d_up), block)


def plain_group_feed(where, ns, cs, g, w_gate, w_up, w_down, before, block):
    normed = (jnp.concatenate(ns) * g).astype(b16)
    cot = (jnp.concatenate(cs) * 0.5).astype(b16)
    parts = feed(normed, cot, w_gate, w_up, w_down)
    return [old + new for old, new in zip(before, plain_grads(where, normed, cot, parts, block))]


def rope_tables(length, width):
    half = width // 2
    inverse = THETA ** (-(jnp.arange(half).astype(f32) * 2.0 / width))
    angles = jnp.arange(length).astype(f32)[:, None] * inverse[None, :]
    angles = jnp.concatenate([angles, angles], axis=1)
    sign = jnp.where(jnp.arange(width) < half, -1.0, 1.0).astype(f32)
    return jnp.cos(angles), jnp.sin(angles) * sign[None, :]


def turn(values, cosine, sine):
    return values * cosine + pltpu.roll(values, values.shape[-1] // 2, 1) * sine


def turn_back(grads, cosine, sine):
    return grads * cosine + pltpu.roll(grads * sine, grads.shape[-1] // 2, 1)


def norm_of(values):
    inv = lax.rsqrt(jnp.mean(values * values, axis=-1, keepdims=True) + EPS)
    return values * inv, inv


def norm_back(scaled, unit, inv):
    return inv * (scaled - unit * jnp.mean(scaled * unit, axis=-1, keepdims=True))


def softmax_of(q_rot, k_rot):
    length, width = q_rot.shape
    scores = dot_nt(q_rot, k_rot) * (width**-0.5)
    at = lax.broadcasted_iota(jnp.int32, (length, length), 0)
    to = lax.broadcasted_iota(jnp.int32, (length, length), 1)
    scores = jnp.where(at >= to, scores, -1e30)
    grown = jnp.exp(scores - jnp.max(scores, axis=-1, keepdims=True))
    return grown * (1.0 / jnp.sum(grown, axis=-1, keepdims=True))


def attend_kernel(half, core_ref, tok_ref, g_ref, wq_ref, wk_ref, wv_ref, qg_ref, kg_ref, wo_ref, cos_ref, sin_ref, *outs):
    n_ref, q_ref, k_ref, v_ref, att_ref, mine_ref = outs[:6]
    width = qg_ref.shape[1]
    cosine, sine = cos_ref[...], sin_ref[...]
    unit, _ = norm_of(tok_ref[...].astype(f32))
    normed = (unit * g_ref[...]).astype(b16)
    n_ref[...] = normed
    query = dot(normed, wq_ref[...])
    keys = dot(normed, wk_ref[...])
    values = dot(normed, wv_ref[...]).astype(b16)
    q_ref[...] = query
    k_ref[...] = keys
    v_ref[...] = values
    kv_heads = keys.shape[1] // width
    share = query.shape[1] // keys.shape[1]
    for kv in range(kv_heads):
        at = slice(kv * width, (kv + 1) * width)
        k_unit, _ = norm_of(keys[:, at])
        k_rot = turn(k_unit * kg_ref[...], cosine, sine).astype(b16)
        for h in range(kv * share, (kv + 1) * share):
            to = slice(h * width, (h + 1) * width)
            q_unit, _ = norm_of(query[:, to])
            q_rot = turn(q_unit * qg_ref[...], cosine, sine).astype(b16)
            probs = softmax_of(q_rot, k_rot).astype(b16)
            att_ref[:, to] = dot(probs, values[:, at]).astype(b16)
    mixed = dot(att_ref[...], wo_ref[...])

    @pl.when(pl.program_id(0) < half)
    def _():
        for i, ref in enumerate(outs[6:]):
            ref[...] = mixed[i * ref.shape[0] : (i + 1) * ref.shape[0]]

    @pl.when(pl.program_id(0) >= half)
    def _():
        mine_ref[...] = mixed


def attend(core, tokens, g, wq, wk, wv, qg, kg, wo, cosine, sine):
    rows, width = tokens.shape
    seqs = rows // SEQ_LEN
    half = seqs // 2

    def source(i, core_ref):
        mine = core_ref[0]
        return (jnp.where(i < half, (1 - mine) * half + i, mine * half + i - half), 0)

    def place(i, _):
        return ((i + half) % seqs, 0)

    def out(columns, dtype):
        return pl.BlockSpec((SEQ_LEN, columns), place), jax.ShapeDtypeStruct((rows, columns), dtype)

    nq, nk = wq.shape[1], wk.shape[1]
    outs = [out(width, b16), out(nq, f32), out(nk, f32), out(nk, b16), out(nq, b16)]
    part = jax.ShapeDtypeStruct((rows // 2, width), f32)
    piece = SEQ_LEN // PIECES
    return pl.pallas_call(
        functools.partial(attend_kernel, half),
        grid_spec=pltpu.PrefetchScalarGridSpec(
            num_scalar_prefetch=1,
            grid=(seqs,),
            in_specs=[pl.BlockSpec((SEQ_LEN, width), source)]
            + [whole(a.shape) for a in (g, wq, wk, wv, qg, kg, wo, cosine, sine)],
            out_specs=[o[0] for o in outs]
            + [
                pl.BlockSpec((SEQ_LEN, width), lambda i, _: (jnp.maximum(i - half, 0), 0)),
            ]
            + [pl.BlockSpec((piece, width), lambda i, _: (jnp.minimum(i, half - 1), 0))] * PIECES,
        ),
        out_shape=[o[1] for o in outs]
        + [part]
        + [jax.ShapeDtypeStruct((piece * half, width), f32)] * PIECES,
        compiler_params=vmem(),
        name="attend",
    )(core, tokens, g, wq, wk, wv, qg, kg, wo, cosine, sine)


def attend_back_kernel(half, core_ref, *refs):
    dnb_refs, rb_refs, refs = refs[:PIECES], refs[PIECES : 2 * PIECES], refs[2 * PIECES :]
    ins, outs = refs[:18], refs[18:]
    dna_ref, ra_ref, cot_ref, tok_ref, q_ref, k_ref, v_ref, att_ref = ins[:8]
    gm_ref, ga_ref, qg_ref, kg_ref, wq_ref, wk_ref, wv_ref, wo_ref, cos_ref, sin_ref = ins[8:]
    dr_ref, drm_ref, dqkv_ref, d1a_ref, ga_out, gq_out, gk_out = outs[:7]
    d1b_refs, (r_ref, dn_ref) = outs[7:-2], outs[-2:]
    step = pl.program_id(0)
    width = qg_ref.shape[1]
    cosine, sine = cos_ref[...], sin_ref[...]

    @pl.when(step == 0)
    def _():
        ga_out[...] = jnp.zeros_like(ga_out)
        gq_out[...] = jnp.zeros_like(gq_out)
        gk_out[...] = jnp.zeros_like(gk_out)

    mine = step < half

    @pl.when(mine)
    def _():
        r_ref[...] = ra_ref[...]
        dn_ref[...] = dna_ref[...]

    @pl.when(step >= half)
    def _():
        for i, (r_piece, dn_piece) in enumerate(zip(rb_refs, dnb_refs)):
            at = slice(i * r_piece.shape[0], (i + 1) * r_piece.shape[0])
            r_ref[at, :] = r_piece[...]
            dn_ref[at, :] = dn_piece[...]

    unit2, inv2 = norm_of(r_ref[...])
    scaled = dn_ref[...] * gm_ref[...]
    d_resid = cot_ref[...].astype(f32) + norm_back(scaled, unit2, inv2)
    d_resid_b = d_resid.astype(b16)
    dr_ref[...] = d_resid_b

    @pl.when(mine)
    def _():
        drm_ref[...] = d_resid

    d_att = dot_nt(d_resid_b, wo_ref[...]).astype(b16)
    nq, nk = q_ref.shape[1], k_ref.shape[1]
    share = nq // nk
    for kv in range(nk // width):
        at = slice(kv * width, (kv + 1) * width)
        k_unit, k_inv = norm_of(k_ref[:, at])
        k_rot = turn(k_unit * kg_ref[...], cosine, sine).astype(b16)
        values = v_ref[:, at]
        d_krot = d_values = 0.0
        for h in range(kv * share, (kv + 1) * share):
            to = slice(h * width, (h + 1) * width)
            q_unit, q_inv = norm_of(q_ref[:, to])
            q_rot = turn(q_unit * qg_ref[...], cosine, sine).astype(b16)
            probs = softmax_of(q_rot, k_rot)
            d_head = d_att[:, to]
            d_prob = dot_nt(d_head, values)
            delta = jnp.sum(d_head.astype(f32) * att_ref[:, to].astype(f32), axis=-1, keepdims=True)
            d_score = (probs * (d_prob - delta) * (width**-0.5)).astype(b16)
            d_krot += dot_tn(d_score, q_rot)
            d_values += dot_tn(probs.astype(b16), d_head)
            d_qn = turn_back(dot(d_score, k_rot), cosine, sine)
            gq_out[...] += jnp.sum(d_qn * q_unit, axis=0, keepdims=True)
            dqkv_ref[:, to] = norm_back(d_qn * qg_ref[...], q_unit, q_inv).astype(b16)
        d_kn = turn_back(d_krot, cosine, sine)
        gk_out[...] += jnp.sum(d_kn * k_unit, axis=0, keepdims=True)
        here = slice(nq + kv * width, nq + (kv + 1) * width)
        dqkv_ref[:, here] = norm_back(d_kn * kg_ref[...], k_unit, k_inv).astype(b16)
        here = slice(nq + nk + kv * width, nq + nk + (kv + 1) * width)
        dqkv_ref[:, here] = d_values.astype(b16)
    d_norm1 = (
        dot_nt(dqkv_ref[:, :nq], wq_ref[...])
        + dot_nt(dqkv_ref[:, nq : nq + nk], wk_ref[...])
        + dot_nt(dqkv_ref[:, nq + nk :], wv_ref[...])
    )
    unit1, _ = norm_of(tok_ref[...].astype(f32))
    ga_out[...] += jnp.sum(d_norm1 * unit1, axis=0, keepdims=True)

    @pl.when(mine)
    def _():
        d1a_ref[...] = d_norm1

    @pl.when(step >= half)
    def _():
        for i, ref in enumerate(d1b_refs):
            ref[...] = d_norm1[i * ref.shape[0] : (i + 1) * ref.shape[0]]


def attend_back(core, dn_a, dn_b, r_a, r_b, cot, tokens, q, k, v, att, gm, ga, qg, kg, wq, wk, wv, wo, cosine, sine):
    rows, width = tokens.shape
    seqs = rows // SEQ_LEN
    half = seqs // 2

    def source(i, core_ref):
        mine = core_ref[0]
        return (jnp.where(i < half, mine * half + i, (1 - mine) * half + i - half), 0)

    def low(i, _):
        return (jnp.minimum(i, half - 1), 0)

    def high(i, _):
        return (jnp.maximum(i - half, 0), 0)

    def same(i, _):
        return (i, 0)

    def block(columns, place):
        return pl.BlockSpec((SEQ_LEN, columns), place)

    nq, nk = wq.shape[1], wk.shape[1]
    part = jax.ShapeDtypeStruct((rows // 2, width), f32)
    consts = (gm, ga, qg, kg, wq, wk, wv, wo, cosine, sine)
    small = [(1, width), qg.shape, kg.shape]
    piece = SEQ_LEN // PIECES
    return pl.pallas_call(
        functools.partial(attend_back_kernel, half),
        grid_spec=pltpu.PrefetchScalarGridSpec(
            num_scalar_prefetch=1,
            grid=(seqs,),
            in_specs=[
                pl.BlockSpec((piece, width), high),
            ]
            * (2 * PIECES)
            + [
                block(width, low),
                block(width, low),
                block(width, same),
                block(width, source),
                block(nq, same),
                block(nk, same),
                block(nk, same),
                block(nq, same),
            ]
            + [whole(a.shape) for a in consts],
            out_specs=[
                block(width, same),
                block(width, low),
                block(nq + 2 * nk, same),
                block(width, low),
            ]
            + [whole(s) for s in small]
            + [pl.BlockSpec((piece, width), high)] * PIECES,
            scratch_shapes=[pltpu.VMEM((SEQ_LEN, width), f32)] * 2,
        ),
        out_shape=[
            jax.ShapeDtypeStruct((rows, width), b16),
            part,
            jax.ShapeDtypeStruct((rows, nq + 2 * nk), b16),
            part,
        ]
        + [jax.ShapeDtypeStruct(s, f32) for s in small]
        + [jax.ShapeDtypeStruct((piece * half, width), f32)] * PIECES,
        compiler_params=vmem(),
        name="attend_back",
    )(core, *dn_b, *r_b, dn_a, r_a, cot, tokens, q, k, v, att, *consts)


def rows_kernel(where_ref, a_ref, b_ref, out_ref):
    out_ref[...] = dot_tn(a_ref[...], b_ref[...])


def input_grads(where, a, b, block):
    rows, columns, count = a.shape[0], b.shape[1], where.shape[0]
    return pl.pallas_call(
        rows_kernel,
        grid_spec=pltpu.PrefetchScalarGridSpec(
            num_scalar_prefetch=1,
            grid=(count,),
            in_specs=[pl.BlockSpec((rows, block), lambda j, at: (0, at[j])), whole((rows, columns))],
            out_specs=pl.BlockSpec((block, columns), lambda j, _: (j, 0)),
        ),
        out_shape=jax.ShapeDtypeStruct((count * block, columns), f32),
        compiler_params=vmem(),
        name="input_grads",
    )(where, a, b)


def output_grads(where, a, b, block):
    rows, columns, count = a.shape[0], a.shape[1], where.shape[0]
    return pl.pallas_call(
        rows_kernel,
        grid_spec=pltpu.PrefetchScalarGridSpec(
            num_scalar_prefetch=1,
            grid=(count,),
            in_specs=[whole((rows, columns)), pl.BlockSpec((rows, block), lambda j, at: (0, at[j]))],
            out_specs=pl.BlockSpec((columns, block), lambda j, _: (j, 0)),
        ),
        out_shape=jax.ShapeDtypeStruct((count * columns, block), f32),
        compiler_params=vmem(),
        name="output_grads",
    )(where, a, b)


def plain_input_grads(where, a, b, block):
    return jnp.concatenate([dot_tn(lax.dynamic_slice_in_dim(a, w * block, block, 1), b) for w in where])


def plain_output_grads(where, a, b, block):
    return jnp.concatenate([dot_tn(a, lax.dynamic_slice_in_dim(b, w * block, block, 1)) for w in where])


def tensor_masks():
    size = lax.axis_size("tensor")
    return [1 << i for i in range(1, size.bit_length() - 1)]


def scatter_sum(parts, masks):
    for mask in masks:
        half = len(parts) // 2
        received = [swap(p, "dp", mask) for p in parts[half:]]
        parts = [a + b for a, b in zip(parts[:half], received)]
    return parts[0]


def relative(masks):
    offsets = [0]
    for mask in reversed(masks):
        offsets = offsets + [o ^ mask for o in offsets]
    return offsets


def body(
    tokens,
    g_attn,
    w_query,
    w_key,
    w_value,
    q_gain,
    k_gain,
    w_out,
    g_mlp,
    w_gate,
    w_up,
    w_down,
    cotangent,
):
    rows, width = tokens.shape
    hd = q_gain.shape[0]
    cosine, sine = rope_tables(SEQ_LEN, hd)
    n_dp = lax.axis_size("dp")
    me = lax.axis_index("dp")
    core = lax.axis_index("tensor") % 2
    core_at = core.astype(jnp.int32).reshape(1)
    x_at = (lax.axis_index("tensor") // 2).astype(jnp.int32).reshape(1)
    half = rows // 2
    block = width // n_dp
    bits = [1 << i for i in range(n_dp.bit_length() - 1)]
    near, far = bits[0], bits[-1]
    middle = bits[1:-1]
    ga, gm, gq, gk = (g.reshape(1, -1) for g in (g_attn, g_mlp, q_gain, k_gain))
    seq = Sequence()

    def mine_of(a):
        return lax.dynamic_slice_in_dim(a, core * half, half, 0)

    def theirs_of(a):
        return lax.dynamic_slice_in_dim(a, (1 - core) * half, half, 0)

    def in_order(mine, theirs):
        out = jnp.zeros((rows,) + mine.shape[1:], mine.dtype)
        out = lax.dynamic_update_slice_in_dim(out, mine, core * half, 0)
        return lax.dynamic_update_slice_in_dim(out, theirs, (1 - core) * half, 0)

    def quarter_of(a):
        size = a.shape[0] // 2
        return lax.dynamic_slice_in_dim(a, (lax.axis_index("tensor") // 2) * size, size, 0)

    def one(value, count):
        return [value] if count == 1 else list(value)

    def pick(kernel, plain):
        return kernel if block % 128 == 0 else plain

    def at(offsets):
        return me ^ jnp.array(offsets, jnp.int32)

    def core_swap(a):
        return swap(a, "tensor", 1)

    def core_swaps(pieces):
        return [swap(a, "tensor", 1) for a in pieces]

    def x_swap(a):
        return swap(a, "tensor", 2)

    cot_mine, cot_theirs = mine_of(cotangent), theirs_of(cotangent)
    cot_own = jnp.concatenate([cot_mine, cot_theirs])
    c0 = cot_mine.astype(f32) * 2.0
    c0, c0_quarter, tokens_then = seq(c0, quarter_of(c0), tokens)
    c1 = swap(c0, "dp", near)
    c2 = swap(c0_quarter, "dp", far)
    tok_mine = mine_of(tokens)
    normed1, query, keys, values, attended, mixed_a, *mixed_b = seq(
        *attend(core_at, tokens_then, ga, w_query, w_key, w_value, gq, gk, w_out, cosine, sine)
    )
    mixed_got = seq(*core_swaps(mixed_b))
    (mixed_chip,) = sum_of(mixed_a, mixed_got)
    mixed_chip = seq(mixed_chip)
    mixed_x = x_swap(mixed_chip)
    c1, c2 = seq(c1, c2)
    c3 = swap(c2, "dp", near)
    c2x = x_swap(c2)
    c1t = core_swap(c1)

    mixed_x = seq(mixed_x)
    r_a, n0, n0_quarter, *r_split = seq(*resid_of(x_at, tok_mine, mixed_chip, mixed_x))
    n1 = swap(n0, "dp", near)
    n2 = swap(n0_quarter, "dp", far)
    r_b = core_swaps(r_split)
    c3, *r_b = seq(c3, *r_b)
    c3x = x_swap(c3)

    normed2, hidden, d_gate, d_up, dn_a, *dn_b, mlp_gain = seq(
        *pick(own_feed, plain_own_feed)(r_a, r_b, cot_own, gm, w_gate, w_up, w_down)
    )
    dn_got = core_swaps(dn_b)
    offsets = relative(middle)
    down_a, down_b, sums = pick(own_rest, plain_own_rest)(
        at(offsets), normed2, cot_own, hidden, d_gate, d_up, w_down, block
    )
    down_a, down_b, *sums = seq(down_a, down_b, *sums)
    n1, n2, c1t, c2x, c3x = seq(n1, n2, c1t, c2x, c3x)
    n3 = swap(n2, "dp", near)
    n2x = x_swap(n2)
    n1t = core_swap(n1)
    moved_c = core_swaps((c2, c2x, c3, c3x))
    down_got = core_swap(down_b)
    dn_got = seq(*dn_got)
    (dn_chip,) = sum_of(dn_a, dn_got)
    n1t, dn_chip = seq(n1t, dn_chip)

    def add_group(ns, cs, sums):
        group = pick(group_feed, plain_group_feed)
        return list(seq(*group(at(offsets), ns, cs, gm, w_gate, w_up, w_down, sums, block)))

    sums = add_group([n1, n1t], [c1, c1t], sums)
    n3, n2x, *moved_c = seq(n3, n2x, *moved_c)
    n3x = x_swap(n3)
    n2t, n2xt, n3t = core_swaps((n2, n2x, n3))
    n2t, n2xt = seq(n2t, n2xt)
    dn_chip = seq(dn_chip)
    dn_x = x_swap(dn_chip)
    sums = add_group([n2, n2x, n2t, n2xt], [c2, c2x, moved_c[0], moved_c[1]], sums)
    n3x, n3t, down_got = seq(n3x, n3t, down_got)
    (down_chip,) = sum_of(down_a, [down_got])
    n3xt, down_chip = seq(core_swap(n3x), down_chip)
    sums = add_group([n3, n3x, n3t, n3xt], [c3, c3x, moved_c[2], moved_c[3]], sums)
    k = len(offsets)
    h = k // 2

    def first_step(parts):
        return [swap(p, "dp", middle[0]) for p in parts[h:]]

    got_down, got_gu = first_step(sums[:k]), first_step(sums[k:])
    keep_down, keep_gu = sums[:h], sums[k : k + h]

    dn_x = seq(dn_x)
    dn_mine, *dn_split = seq(*sum_of(dn_chip, [dn_x], split=True))
    down_x = x_swap(down_chip)
    dn_theirs = seq(*core_swaps(dn_split))
    dr_b, dr_mine, d_qkv, d1_a, gain_a, gain_q, gain_k, *d1_b = seq(
        *attend_back(
            core_at, dn_mine, dn_theirs, r_a, r_b, cot_own, tokens, query, keys, values, attended,
            gm, ga, gq, gk, w_query, w_key, w_value, w_out, cosine, sine,
        )
    )
    gains = jnp.concatenate([gain_a[0], gain_q[0], gain_k[0], mlp_gain[0]])
    gains_got = swap(gains, "dp", near)
    d1_got = core_swaps(d1_b)

    every = [near] + middle + [far]
    rest = every[1:]
    blocks = relative(every)
    q = len(blocks) // 4
    of_in, of_out = pick(input_grads, plain_input_grads), pick(output_grads, plain_output_grads)

    def ins(i, count=1):
        return of_in(at(blocks[i * q : (i + count) * q]), normed1, d_qkv, block)

    def outs(i, count=1):
        return of_out(at(blocks[i * q : (i + count) * q]), attended, dr_b, block)

    in_3 = seq(ins(3))
    in_got3 = swap(in_3, "dp", near)
    out_23 = seq(outs(2, 2))
    out_got = swap(out_23, "dp", near)
    *d1_got, gains_got = seq(*d1_got, gains_got)
    (d1_chip,) = sum_of(d1_a, d1_got)
    d1_chip = seq(d1_chip)
    d1_x = x_swap(d1_chip)
    gains = gains + gains_got
    in_2 = seq(ins(2))
    in_got2 = swap(in_2, "dp", near)
    out_01, in_1, in_0 = seq(outs(0, 2), ins(1), ins(0))
    got_down = one(seq(*got_down), h)

    def finish(keep, got):
        return scatter_sum([a + b for a, b in zip(keep, got)], middle[1:])

    summed_down = finish(keep_down, got_down)
    down_x = seq(down_x)
    down_mine, *down_split = seq(*sum_of(down_chip, [down_x], split=True))
    down_theirs = core_swaps(down_split)
    in_got3, *down_theirs = seq(in_got3, *down_theirs)
    (in_1,) = sum_of(in_1, [in_got3])
    in_mid = swap(in_1, "dp", rest[0])
    down_theirs = jnp.concatenate(down_theirs)
    r_theirs = jnp.concatenate(r_b)
    output = in_order((r_a + down_mine).astype(b16), (r_theirs + down_theirs).astype(b16))
    d1_x = seq(d1_x)
    d1_mine = d1_chip + d1_x
    _, unit1, rms1 = rms_norm(tok_mine.astype(f32), ga)
    gt_mine = seq(dr_mine + rms_back(d1_mine, ga, unit1, rms1))
    gt_theirs = core_swap(gt_mine)
    got_gu = one(seq(*got_gu), h)
    summed_gu = finish(keep_gu, got_gu)
    out_got, gt_theirs = seq(out_got, gt_theirs)
    (out_01,) = sum_of(out_01, [out_got])
    at_half = out_01.shape[0] // 2
    out_mid = swap(out_01[at_half:], "dp", rest[0])
    grad_tokens = in_order(gt_mine, gt_theirs)
    gains = seq(gains + x_swap(gains))
    gains = seq(gains + core_swap(gains))
    for mask in bits[1:]:
        gains = seq(gains + swap(gains, "dp", mask))
    in_got2 = seq(in_got2)

    def split(a):
        return list(a.reshape(q, a.shape[0] // q, a.shape[1]))

    in_mid = seq(in_mid)
    summed_qkv = scatter_sum(split(in_0 + in_got2 + in_mid), rest[1:])
    out_mid = seq(out_mid)
    summed_out = scatter_sum(split(out_01[:at_half] + out_mid), rest[1:])
    summed_qkv, summed_out = seq(summed_qkv, summed_out)
    nq, nk = w_query.shape[1], w_key.shape[1]
    gains = gains + 0.0 * seq.token.astype(f32)
    return (
        output,
        grad_tokens,
        gains[:width],
        summed_qkv[:, :nq],
        summed_qkv[:, nq : nq + nk],
        summed_qkv[:, nq + nk :],
        gains[width : width + hd],
        gains[width + hd : width + 2 * hd],
        summed_out,
        gains[width + 2 * hd :],
        summed_gu[:block],
        summed_gu[block:],
        summed_down,
    )


def solution(mesh):
    in_specs = (
        P("dp", None),
        P(),
        P(None, "tensor"),
        P(None, "tensor"),
        P(None, "tensor"),
        P(),
        P(),
        P("tensor", None),
        P(),
        P(None, "tensor"),
        P(None, "tensor"),
        P("tensor", None),
        P("dp", None),
    )
    out_specs = (
        P("dp", None),
        P("dp", None),
        P(),
        P("dp", "tensor"),
        P("dp", "tensor"),
        P("dp", "tensor"),
        P(),
        P(),
        P("tensor", "dp"),
        P(),
        P("dp", "tensor"),
        P("dp", "tensor"),
        P("tensor", "dp"),
    )
    return jax.shard_map(body, mesh=mesh, in_specs=in_specs, out_specs=out_specs, check_vma=False)
```

time: 755 us -> 576 us (0.76)
  Pallas kernels: 0 us -> 216 us
  matrix products: 177 us -> 0 us
  waiting for transfers between devices: 412 us -> 251 us
  other arithmetic: 66.6 us -> 31.2 us
  local copies, waits for them, and re-layouts: 52.6 us -> 20.3 us
    pallas_call x0 -> x22, Pallas kernels: none -> 216 us  [the longest x3 72.7 us: group_feed(): pl.pallas_call(functools.partial(group_kernel, len(ns), count), grid_spec...]
    dot_general x48 -> x0, matrix products: 177 us -> none  [the longest x11 74.4 us: dot(): return jnp.dot(a, b, preferred_element_type=f32)]
    ppermute x44 -> x64, waiting for transfers between devices: 412 us -> 251 us  [swap(): return lax.ppermute(value, axis, [(i, i ^ mask) for i in range(size)])]
    convert_element_type x12 -> x1, other arithmetic: 17.7 us -> 0.01 us  [rope_tables(): angles = jnp.arange(length).astype(f32)[:, None] * inverse[None, :]]
    unnamed x195 -> x103, local copies, waits for them, and re-layouts: 21.8 us -> 9.25 us
    reshape x9 -> x0, local copies, waits for them, and re-layouts: 12.4 us -> none  [the longest x3 8.43 us: body(): query = dot(normed1, w_query).reshape(seqs, SEQ_LEN, heads, head_dim)]
    concatenate x6 -> x2, other arithmetic: 15.6 us -> 3.55 us  [the longest x1 2.84 us: body(): cot_own = jnp.concatenate([cot_mine, cot_theirs])]
    ppermute x44 -> x64, starting transfers between devices: 39.6 us -> 44.4 us  [swap(): return lax.ppermute(value, axis, [(i, i ^ mask) for i in range(size)])]
  transfers between devices with their start and end apart: 44 -> 64, of which waited for: 16 -> 25; matrix products, arithmetic and copies ran while one was open for 28% -> 6% of each run, Pallas kernels for 0% -> 35%
where the time goes in v2:
time: 576 us; the launch traced here: 565 us
  waiting for transfers between devices  251 us (44%)
  Pallas kernels  216 us (38%)
  starting transfers between devices  44.4 us (8%)
  other arithmetic  31.2 us (5%)
  local copies, waits for them, and re-layouts  20.3 us (4%)
    ppermute x64, waiting for transfers between devices, swap(): return lax.ppermute(value, axis, [(i, i ^ mask) for i in range(size)])  251 us
    pallas_call x3, Pallas kernels, group_feed(): pl.pallas_call(functools.partial(group_kernel, len(ns), count), grid_spec...  72.7 us
    ppermute x64, starting transfers between devices, swap(): return lax.ppermute(value, axis, [(i, i ^ mask) for i in range(size)])  44.4 us
    pallas_call x8, Pallas kernels, sum_of(): pl.pallas_call(functools.partial(sum_kernel, len(bs)), in_specs=[whole(x....  32.2 us
    pallas_call x1, Pallas kernels, own_feed(): pl.pallas_call(own_kernel, grid=(hidden // TILE,), in_specs=[whole((half,...  27.4 us
    pallas_call x1, Pallas kernels, attend_back(): pl.pallas_call(functools.partial(attend_back_kernel, half), grid_spec=plt...  23.7 us
    pallas_call x4, Pallas kernels, input_grads(): pl.pallas_call(rows_kernel, grid_spec=pltpu.PrefetchScalarGridSpec(num_sc...  15.7 us
    pallas_call x1, Pallas kernels, own_rest(): pl.pallas_call(rest_kernel, grid_spec=pltpu.PrefetchScalarGridSpec(num_sc...  15.1 us
  transfers between devices with their start and end apart: 64, of which 25 were waited for; matrix products, arithmetic and copies ran while one was open for 6% of the time, Pallas kernels for 35%

profile of v2, /device:TPU:0, one launch (start us, length us, event | category | flops | bytes accessed | tf_op | source)
XLA Modules:
  0.0 565.4 jit_solution(13484293735437988255)
XLA Ops:
  5.6 13.7 %attend.1 = (bf16[512,2048]{1,0:T(8,128)(2,1)}, f32[512,512]{1,0:T(8,128)}, f32[512,256]{1,0:T(8,128)}, bf16[512,256]{1,0:T(8,128)(2,1)}, bf16[512,512]{1,0:T(8,...) custom-call(s32[1]{0:T(128)} %bitcast.1.core_ref, ...), custom_call_target="tpu_custom_call" | custom-call | tf_op jit(solution)/shard_map/attend/pallas_call | solution.py:504
  24.2 3.7 sum_of.8.a_ref
  33.1 45.8 %collective-permute-done.6.refs_4_ = f32[128,2048]{1,0:T(8,128)} collective-permute-done((f32[128,2048]{1,0:T(8,128)S(1)}, f32[128,2048]{1,0:T(8,128)}, u32[]{:S(2)}, u32[]{:S(2)}) %collective-permute-start.6) | collective-permute-done | bytes 1048608 | tf_op jit(solution)/shard_map/ppermute | solution.py:33
  82.9 5.6 resid_of.1
  89.5 15.6 %collective-permute-done.11.refs_4_ = f32[128,2048]{1,0:T(8,128)S(1)} collective-permute-done((f32[128,2048]{1,0:T(8,128)}, f32[128,2048]{1,0:T(8,128)S(1)}, u32[]{:S(2)}, u32[]{:S(2)}) %collective-permute-start.11) | collective-permute-done | bytes 1048608 | tf_op jit(solution)/shard_map/ppermute | solution.py:33
  113.5 27.4 %own_feed.1 = (bf16[512,2048]{1,0:T(8,128)(2,1)}, bf16[512,1536]{1,0:T(8,128)(2,1)}, bf16[512,1536]{1,0:T(8,128)(2,1)}, bf16[512,1536]{1,0:T(8,128)(2,1)}, f32[2...) custom-call(f32[256,2048]{1,0:T(8,128)} %get-tuple-element.306.ra_re, ...), custom_call_target="tpu_custom_call" | custom-call | tf_op jit(solution)/shard_map/own_feed/pallas_call | solution.py:130
  140.9 15.1 %own_rest.1 = (f32[256,2048]{1,0:T(8,128)}, f32[256,2048]{1,0:T(8,128)}, f32[1536,256]{1,0:T(8,128)}, f32[1536,256]{1,0:T(8,128)}, f32[512,1536]{1,0:T(8,128)}, /*index=5*/f32[512,1536]{1,0:T(8,128)}) custom-call(s32[2]{0:T(128)} %get-tuple-element.542.where_ref, bf16[512,2048]{1,0:T(8,128)(2,1)} %get-tuple-element.332.nb_ref, ...), custom_call_target="tpu_custom_call" | custom-call | tf_op jit(solution)/shard_map/own_rest/pallas_call | solution.py:223
  157.4 4.8 collective-permute-done.19.refs_6_
  167.4 3.7 sum_of.9.refs_0_
  171.1 24.2 %group_feed.3 = (f32[1536,256]{1,0:T(8,128)}, f32[1536,256]{1,0:T(8,128)}, f32[512,1536]{1,0:T(8,128)}, f32[512,1536]{1,0:T(8,128)}) custom-call(s32[2]{0:T(128)} %get-tuple-element.542.where_ref, f32[256,2048]{1,0:T(8,128)} %collective-permute-done.7.refs_0_, f32[256,2048]{1,0:T(8,128)} %collective-permute-done.23.refs_1_, ...), custom_call_target="tpu_custom_call" | custom-call | tf_op jit(solution)/shard_map/group_feed/pallas_call | solution.py:278
  201.4 24.5 %group_feed.4 = (f32[1536,256]{1,0:T(8,128)}, f32[1536,256]{1,0:T(8,128)}, f32[512,1536]{1,0:T(8,128)}, f32[512,1536]{1,0:T(8,128)}) custom-call(s32[2]{0:T(128)} %get-tuple-element.542.where_ref, f32[128,2048]{1,0:T(8,128)} %collective-permute-done.8.refs_0_, f32[128,2048]{1,0:T(8,128)} %collective-permute-done.18.refs_1_, f32[128,2048]{1,0:T(8,128)} %copy-done.25, ...), custom_call_target="tpu_custom_call" | custom-call | tf_op jit(solution)/shard_map/group_feed/pallas_call | solution.py:278
  226.1 4.0 sum_of.10.refs_0_
  230.1 24.0 %group_feed.5 = (f32[1536,256]{1,0:T(8,128)}, f32[1536,256]{1,0:T(8,128)}, f32[512,1536]{1,0:T(8,128)}, f32[512,1536]{1,0:T(8,128)}) custom-call(s32[2]{0:T(128)} %get-tuple-element.542.where_ref, f32[128,2048]{1,0:T(8,128)} %collective-permute-done.17.refs_0_, f32[128,2048]{1,0:T(8,128)} %copy-done.24, f32[128,2048]{1,0:T(8,128)} %collective-permute-done.29.refs_2_, ...), custom_call_target="tpu_custom_call" | custom-call | tf_op jit(solution)/shard_map/group_feed/pallas_call | solution.py:278
  254.0 12.6 %collective-permute-done.36.refs_1_ = f32[256,2048]{1,0:T(8,128)} collective-permute-done((f32[256,2048]{1,0:T(8,128)S(1)}, f32[256,2048]{1,0:T(8,128)}, u32[]{:S(2)}, u32[]{:S(2)}) %collective-permute-start.36) | collective-permute-done | bytes 2097184 | tf_op jit(solution)/shard_map/ppermute | solution.py:33
  266.6 4.3 sum_of.11
  276.3 23.7 %attend_back.1 = (bf16[512,2048]{1,0:T(8,128)(2,1)}, f32[256,2048]{1,0:T(8,128)}, bf16[512,1024]{1,0:T(8,128)(2,1)}, f32[256,2048]{1,0:T(8,128)}, f32[1,2048]{1,...) custom-call(s32[1]{0:T(128)} %bitcast.1.core_ref, ...), custom_call_target="tpu_custom_call" | custom-call | tf_op jit(solution)/shard_map/attend_back/pallas_call | solution.py:639
  306.4 4.0 input_grads.7
  310.4 5.1 output_grads.3
  323.7 3.9 input_grads.6
  327.6 3.9 input_grads.5
  331.6 3.9 input_grads.4.refs_0_
  335.5 5.3 output_grads.2.refs_0_
  340.8 4.4 sum_of.13
  351.9 12.5 %collective-permute-done.46.refs_1_ = f32[512,1024]{1,0:T(8,128)} collective-permute-done((f32[512,1024]{1,0:T(8,128)}, f32[512,1024]{1,0:T(8,128)}, u32[]{:S(2)}, u32[]{:S(2)}) %collective-permute-start.46) | collective-permute-done | bytes 2097184 | tf_op jit(solution)/shard_map/ppermute | solution.py:33
  364.4 5.7 %collective-permute-done.51 = f32[256,2048]{1,0:T(8,128)} collective-permute-done((f32[256,2048]{1,0:T(8,128)}, f32[256,2048]{1,0:T(8,128)}, u32[]{:S(2)}, u32[]{:S(2)}) %collective-permute-start.51) | collective-permute-done | bytes 2097184 | tf_op jit(solution)/shard_map/ppermute | solution.py:33
  377.9 3.8 sum_of.14
  384.3 35.7 %collective-permute-done.54 = f32[512,1536]{1,0:T(8,128)} collective-permute-done((f32[512,1536]{1,0:T(8,128)}, f32[512,1536]{1,0:T(8,128)}, u32[]{:S(2)}, u32[]{:S(2)}) %collective-permute-start.54) | collective-permute-done | bytes 3145760 | tf_op jit(solution)/shard_map/ppermute | solution.py:33
  430.4 4.5 sum_of.15
  436.3 29.0 %collective-permute-done.57 = f32[4352]{0:T(1024)S(1)} collective-permute-done((f32[4352]{0:T(1024)S(1)}, f32[4352]{0:T(1024)S(1)}, u32[]{:S(2)}, u32[]{:S(2)}) %collective-permute-start.57) | collective-permute-done | bytes 17440 | tf_op jit(solution)/shard_map/ppermute | solution.py:33
  471.8 15.1 %collective-permute-done.58 = f32[4352]{0:T(1024)S(1)} collective-permute-done((f32[4352]{0:T(1024)S(1)}, f32[4352]{0:T(1024)S(1)}, u32[]{:S(2)}, u32[]{:S(2)}) %collective-permute-start.58) | collective-permute-done | bytes 17440 | tf_op jit(solution)/shard_map/ppermute | solution.py:33
  497.3 52.7 %collective-permute-done.61 = f32[256,1024]{1,0:T(8,128)S(1)} collective-permute-done((f32[256,1024]{1,0:T(8,128)S(1)}, f32[256,1024]{1,0:T(8,128)S(1)}, u32[]{:S(2)}, u32[]{:S(2)}) %collective-permute-start.61) | collective-permute-done | bytes 1048608 | tf_op jit(solution)/shard_map/ppermute | solution.py:33
  550.1 10.7 %collective-permute-done.63 = f32[512,256]{1,0:T(8,128)S(1)} collective-permute-done((f32[512,256]{1,0:T(8,128)S(1)}, f32[512,256]{1,0:T(8,128)S(1)}, u32[]{:S(2)}, u32[]{:S(2)}) %collective-permute-start.63) | collective-permute-done | bytes 524320 | tf_op jit(solution)/shard_map/ppermute | solution.py:33
  (267 shorter events, 110.2 us)
Async XLA Ops:
  20.4 58.5 %collective-permute-start.5 = (f32[256,2048]{1,0:T(8,128)S(1)}, f32[256,2048]{1,0:T(8,128)}, u32[]{:S(2)}, u32[]{:S(2)}) collective-permute-start(f32[256,2048]{1,0:T(8,128)S(1)} %get-tuple-element.281), channel_id=1, source_target_pairs={{0,4},{4,0},{8,12},{12,8},{16,20},{20,16},{24,28},{28,24},{1,5},{5... | collective-permute-start | bytes 6291464 | tf_op jit(solution)/shard_map/ppermute | solution.py:33
  27.9 55.0 %collective-permute-start.4 = (f32[256,2048]{1,0:T(8,128)}, f32[256,2048]{1,0:T(8,128)}, u32[]{:S(2)}, u32[]{:S(2)}) collective-permute-start(f32[256,2048]{1,0:T(8,128)} %sum_of.8.a_ref), channel_id=1, source_target_pairs={{0,2},{1,3},{2,0},{3,1},{4,6},{5,7},{6,4},{7,5},{8,10},{9,11},{10,... | collective-permute-start | bytes 6291464 | tf_op jit(solution)/shard_map/ppermute | solution.py:33
  30.5 48.4 %collective-permute-start.6 = (f32[128,2048]{1,0:T(8,128)S(1)}, f32[128,2048]{1,0:T(8,128)}, u32[]{:S(2)}, u32[]{:S(2)}) collective-permute-start(f32[128,2048]{1,0:T(8,128)S(1)} %constant_dynamic-slice_fusion.1), channel_id=1, source_target_pairs={{0,16},{4,20},{8,24},{12,28},{16,0},{20,4},{24,8},{28,12},{1,17},{... | collective-permute-start | bytes 3145736 | tf_op jit(solution)/shard_map/ppermute | solution.py:33
  78.9 26.2 %collective-permute-start.11 = (f32[128,2048]{1,0:T(8,128)}, f32[128,2048]{1,0:T(8,128)S(1)}, u32[]{:S(2)}, u32[]{:S(2)}) collective-permute-start(f32[128,2048]{1,0:T(8,128)} %collective-permute-done.6.refs_4_), channel_id=1, source_target_pairs={{0,4},{4,0},{8,12},{12,8},{16,20},{20,16},{24,28},{28,24},{1,5},{5... | collective-permute-start | bytes 3145736 | tf_op jit(solution)/shard_map/ppermute | solution.py:33
  88.5 17.6 %collective-permute-start.12 = (f32[64,2048]{1,0:T(8,128)}, f32[64,2048]{1,0:T(8,128)S(1)}, u32[]{:S(2)}, u32[]{:S(2)}) collective-permute-start(f32[64,2048]{1,0:T(8,128)} %get-tuple-element.311), channel_id=1, source_target_pairs={{0,1},{1,0},{2,3},{3,2},{4,5},{5,4},{6,7},{7,6},{8,9},{9,8},{10,11... | collective-permute-start | bytes 1572872 | tf_op jit(solution)/shard_map/ppermute | solution.py:33
  88.5 67.7 %collective-permute-start.9 = (f32[256,2048]{1,0:T(8,128)}, f32[256,2048]{1,0:T(8,128)}, u32[]{:S(2)}, u32[]{:S(2)}) collective-permute-start(f32[256,2048]{1,0:T(8,128)} %collective-permute-done.5.refs_2_), channel_id=1, source_target_pairs={{0,1},{1,0},{2,3},{3,2},{4,5},{5,4},{6,7},{7,6},{8,9},{9,8},{10,11... | collective-permute-start | bytes 6291464 | tf_op jit(solution)/shard_map/ppermute | solution.py:33
  89.0 67.2 %collective-permute-start.7 = (f32[256,2048]{1,0:T(8,128)}, f32[256,2048]{1,0:T(8,128)}, u32[]{:S(2)}, u32[]{:S(2)}) collective-permute-start(f32[256,2048]{1,0:T(8,128)} %get-tuple-element.307), channel_id=1, source_target_pairs={{0,4},{4,0},{8,12},{12,8},{16,20},{20,16},{24,28},{28,24},{1,5},{5... | collective-permute-start | bytes 6291464 | tf_op jit(solution)/shard_map/ppermute | solution.py:33
  106.2 49.8 %collective-permute-start.10 = (f32[128,2048]{1,0:T(8,128)}, f32[128,2048]{1,0:T(8,128)}, u32[]{:S(2)}, u32[]{:S(2)}) collective-permute-start(f32[128,2048]{1,0:T(8,128)} %collective-permute-done.6.refs_4_), channel_id=1, source_target_pairs={{0,2},{1,3},{2,0},{3,1},{4,6},{5,7},{6,4},{7,5},{8,10},{9,11},{10,... | collective-permute-start | bytes 3145736 | tf_op jit(solution)/shard_map/ppermute | solution.py:33
  107.3 48.9 %collective-permute-start.8 = (f32[128,2048]{1,0:T(8,128)}, f32[128,2048]{1,0:T(8,128)}, u32[]{:S(2)}, u32[]{:S(2)}) collective-permute-start(f32[128,2048]{1,0:T(8,128)} %get-tuple-element.308), channel_id=1, source_target_pairs={{0,16},{4,20},{8,24},{12,28},{16,0},{20,4},{24,8},{28,12},{1,17},{... | collective-permute-start | bytes 3145736 | tf_op jit(solution)/shard_map/ppermute | solution.py:33
  108.3 47.9 %collective-permute-start.16 = (f32[128,2048]{1,0:T(8,128)}, f32[128,2048]{1,0:T(8,128)}, u32[]{:S(2)}, u32[]{:S(2)}) collective-permute-start(f32[128,2048]{1,0:T(8,128)} %copy-done.21), channel_id=1, source_target_pairs={{0,2},{1,3},{2,0},{3,1},{4,6},{5,7},{6,4},{7,5},{8,10},{9,11},{10,... | collective-permute-start | bytes 3145736 | tf_op jit(solution)/shard_map/ppermute | solution.py:33
  163.6 31.6 %collective-permute-start.17 = (f32[128,2048]{1,0:T(8,128)}, f32[128,2048]{1,0:T(8,128)}, u32[]{:S(2)}, u32[]{:S(2)}) collective-permute-start(f32[128,2048]{1,0:T(8,128)} %collective-permute-done.8.refs_0_), channel_id=1, source_target_pairs={{0,4},{4,0},{8,12},{12,8},{16,20},{20,16},{24,28},{28,24},{1,5},{5... | collective-permute-start | bytes 3145736 | tf_op jit(solution)/shard_map/ppermute | solution.py:33
  165.2 30.5 %collective-permute-start.18 = (f32[128,2048]{1,0:T(8,128)}, f32[128,2048]{1,0:T(8,128)}, u32[]{:S(2)}, u32[]{:S(2)}) collective-permute-start(f32[128,2048]{1,0:T(8,128)} %collective-permute-done.8.refs_0_), channel_id=1, source_target_pairs={{0,2},{1,3},{2,0},{3,1},{4,6},{5,7},{6,4},{7,5},{8,10},{9,11},{10,... | collective-permute-start | bytes 3145736 | tf_op jit(solution)/shard_map/ppermute | solution.py:33
  166.6 29.2 %collective-permute-start.20 = (f32[128,2048]{1,0:T(8,128)}, f32[128,2048]{1,0:T(8,128)}, u32[]{:S(2)}, u32[]{:S(2)}) collective-permute-start(f32[128,2048]{1,0:T(8,128)} %collective-permute-done.10.refs_5_), channel_id=1, source_target_pairs={{0,1},{1,0},{2,3},{3,2},{4,5},{5,4},{6,7},{7,6},{8,9},{9,8},{10,11... | collective-permute-start | bytes 3145736 | tf_op jit(solution)/shard_map/ppermute | solution.py:33
  166.6 29.1 %collective-permute-start.22 = (f32[128,2048]{1,0:T(8,128)}, f32[128,2048]{1,0:T(8,128)}, u32[]{:S(2)}, u32[]{:S(2)}) collective-permute-start(f32[128,2048]{1,0:T(8,128)} %collective-permute-done.16.refs_5_), channel_id=1, source_target_pairs={{0,1},{1,0},{2,3},{3,2},{4,5},{5,4},{6,7},{7,6},{8,9},{9,8},{10,11... | collective-permute-start | bytes 3145736 | tf_op jit(solution)/shard_map/ppermute | solution.py:33
  171.1 54.9 %collective-permute-start.30 = (f32[256,2048]{1,0:T(8,128)}, f32[256,2048]{1,0:T(8,128)}, u32[]{:S(2)}, u32[]{:S(2)}) collective-permute-start(f32[256,2048]{1,0:T(8,128)} %get-tuple-element.372), channel_id=1, source_target_pairs={{0,1},{1,0},{2,3},{3,2},{4,5},{5,4},{6,7},{7,6},{8,9},{9,8},{10,11... | collective-permute-start | bytes 6291464 | tf_op jit(solution)/shard_map/ppermute | solution.py:33
  195.9 30.0 %collective-permute-start.28 = (f32[128,2048]{1,0:T(8,128)}, f32[128,2048]{1,0:T(8,128)S(1)}, u32[]{:S(2)}, u32[]{:S(2)}) collective-permute-start(f32[128,2048]{1,0:T(8,128)} %collective-permute-done.17.refs_0_), channel_id=1, source_target_pairs={{0,2},{1,3},{2,0},{3,1},{4,6},{5,7},{6,4},{7,5},{8,10},{9,11},{10,... | collective-permute-start | bytes 3145736 | tf_op jit(solution)/shard_map/ppermute | solution.py:33
  196.6 29.3 %collective-permute-start.29 = (f32[128,2048]{1,0:T(8,128)}, f32[128,2048]{1,0:T(8,128)}, u32[]{:S(2)}, u32[]{:S(2)}) collective-permute-start(f32[128,2048]{1,0:T(8,128)} %collective-permute-done.17.refs_0_), channel_id=1, source_target_pairs={{0,1},{1,0},{2,3},{3,2},{4,5},{5,4},{6,7},{7,6},{8,9},{9,8},{10,11... | collective-permute-start | bytes 3145736 | tf_op jit(solution)/shard_map/ppermute | solution.py:33
  200.7 65.9 %collective-permute-start.36 = (f32[256,2048]{1,0:T(8,128)S(1)}, f32[256,2048]{1,0:T(8,128)}, u32[]{:S(2)}, u32[]{:S(2)}) collective-permute-start(f32[256,2048]{1,0:T(8,128)S(1)} %copy-done.4), channel_id=1, source_target_pairs={{0,2},{1,3},{2,0},{3,1},{4,6},{5,7},{6,4},{7,5},{8,10},{9,11},{10,... | collective-permute-start | bytes 6291464 | tf_op jit(solution)/shard_map/ppermute | solution.py:33
  272.1 68.8 %collective-permute-start.34 = (f32[256,2048]{1,0:T(8,128)}, f32[256,2048]{1,0:T(8,128)}, u32[]{:S(2)}, u32[]{:S(2)}) collective-permute-start(f32[256,2048]{1,0:T(8,128)} %sum_of.10.refs_0_), channel_id=1, source_target_pairs={{0,2},{1,3},{2,0},{3,1},{4,6},{5,7},{6,4},{7,5},{8,10},{9,11},{10,... | collective-permute-start | bytes 6291464 | tf_op jit(solution)/shard_map/ppermute | solution.py:33
  301.6 39.2 %collective-permute-start.35 = (f32[1536,256]{1,0:T(8,128)}, f32[1536,256]{1,0:T(8,128)}, u32[]{:S(2)}, u32[]{:S(2)}) collective-permute-start(f32[1536,256]{1,0:T(8,128)} %get-tuple-element.409), channel_id=1, source_target_pairs={{0,8},{4,12},{8,0},{12,4},{16,24},{20,28},{24,16},{28,20},{1,9},{5... | collective-permute-start | bytes 4718600 | tf_op jit(solution)/shard_map/ppermute | solution.py:33
  315.5 48.9 %collective-permute-start.46 = (f32[512,1024]{1,0:T(8,128)}, f32[512,1024]{1,0:T(8,128)}, u32[]{:S(2)}, u32[]{:S(2)}) collective-permute-start(f32[512,1024]{1,0:T(8,128)} %input_grads.7), channel_id=1, source_target_pairs={{0,4},{4,0},{8,12},{12,8},{16,20},{20,16},{24,28},{28,24},{1,5},{5... | collective-permute-start | bytes 6291464 | tf_op jit(solution)/shard_map/ppermute | solution.py:33
  322.2 47.9 %collective-permute-start.51 = (f32[256,2048]{1,0:T(8,128)}, f32[256,2048]{1,0:T(8,128)}, u32[]{:S(2)}, u32[]{:S(2)}) collective-permute-start(f32[256,2048]{1,0:T(8,128)} %sum_of.12), channel_id=1, source_target_pairs={{0,2},{1,3},{2,0},{3,1},{4,6},{5,7},{6,4},{7,5},{8,10},{9,11},{10,... | collective-permute-start | bytes 6291464 | tf_op jit(solution)/shard_map/ppermute | solution.py:33
  348.3 71.7 %collective-permute-start.54 = (f32[512,1536]{1,0:T(8,128)}, f32[512,1536]{1,0:T(8,128)}, u32[]{:S(2)}, u32[]{:S(2)}) collective-permute-start(f32[512,1536]{1,0:T(8,128)} %get-tuple-element.494), channel_id=1, source_target_pairs={{0,8},{4,12},{8,0},{12,4},{16,24},{20,28},{24,16},{28,20},{1,9},{5... | collective-permute-start | bytes 9437192 | tf_op jit(solution)/shard_map/ppermute | solution.py:33
  350.7 69.3 %collective-permute-start.52 = (f32[2048,256]{1,0:T(8,128)}, f32[2048,256]{1,0:T(8,128)}, u32[]{:S(2)}, u32[]{:S(2)}) collective-permute-start(f32[2048,256]{1,0:T(8,128)} %output_grads.3), channel_id=1, source_target_pairs={{0,4},{4,0},{8,12},{12,8},{16,20},{20,16},{24,28},{28,24},{1,5},{5... | collective-permute-start | bytes 6291464 | tf_op jit(solution)/shard_map/ppermute | solution.py:33
  375.9 44.1 %collective-permute-start.53 = (f32[256,2048]{1,0:T(8,128)}, f32[256,2048]{1,0:T(8,128)S(1)}, u32[]{:S(2)}, u32[]{:S(2)}) collective-permute-start(f32[256,2048]{1,0:T(8,128)} %fusion.5), channel_id=1, source_target_pairs={{0,1},{1,0},{2,3},{3,2},{4,5},{5,4},{6,7},{7,6},{8,9},{9,8},{10,11... | collective-permute-start | bytes 6291464 | tf_op jit(solution)/shard_map/ppermute | solution.py:33
  377.0 109.9 %collective-permute-start.59 = (f32[512,1024]{1,0:T(8,128)}, f32[512,1024]{1,0:T(8,128)}, u32[]{:S(2)}, u32[]{:S(2)}) collective-permute-start(f32[512,1024]{1,0:T(8,128)} %input_grads.6), channel_id=1, source_target_pairs={{0,4},{4,0},{8,12},{12,8},{16,20},{20,16},{24,28},{28,24},{1,5},{5... | collective-permute-start | bytes 6291464 | tf_op jit(solution)/shard_map/ppermute | solution.py:33
  381.7 105.2 %collective-permute-start.60 = (f32[512,1024]{1,0:T(8,128)}, f32[512,1024]{1,0:T(8,128)}, u32[]{:S(2)}, u32[]{:S(2)}) collective-permute-start(f32[512,1024]{1,0:T(8,128)} %sum_of.14), channel_id=1, source_target_pairs={{0,8},{4,12},{8,0},{12,4},{16,24},{20,28},{24,16},{28,20},{1,9},{5... | collective-permute-start | bytes 6291464 | tf_op jit(solution)/shard_map/ppermute | solution.py:33
  426.6 38.7 %collective-permute-start.57 = (f32[4352]{0:T(1024)S(1)}, f32[4352]{0:T(1024)S(1)}, u32[]{:S(2)}, u32[]{:S(2)}) collective-permute-start(f32[4352]{0:T(1024)S(1)} %add.100), channel_id=1, source_target_pairs={{0,8},{4,12},{8,0},{12,4},{16,24},{20,28},{24,16},{28,20},{1,9},{5... | collective-permute-start | bytes 52232 | tf_op jit(solution)/shard_map/ppermute | solution.py:33
  436.2 59.3 %collective-permute-start.62 = (f32[1024,256]{1,0:T(8,128)S(1)}, f32[1024,256]{1,0:T(8,128)S(1)}, u32[]{:S(2)}, u32[]{:S(2)}) collective-permute-start(f32[1024,256]{1,0:T(8,128)S(1)} %slice.54), channel_id=1, source_target_pairs={{0,8},{4,12},{8,0},{12,4},{16,24},{20,28},{24,16},{28,20},{1,9},{5... | collective-permute-start | bytes 3145736 | tf_op jit(solution)/shard_map/ppermute | solution.py:33
  465.3 21.6 %collective-permute-start.58 = (f32[4352]{0:T(1024)S(1)}, f32[4352]{0:T(1024)S(1)}, u32[]{:S(2)}, u32[]{:S(2)}) collective-permute-start(f32[4352]{0:T(1024)S(1)} %add.101), channel_id=1, source_target_pairs={{0,16},{4,20},{8,24},{12,28},{16,0},{20,4},{24,8},{28,12},{1,17},{... | collective-permute-start | bytes 52232 | tf_op jit(solution)/shard_map/ppermute | solution.py:33
  490.1 59.9 %collective-permute-start.61 = (f32[256,1024]{1,0:T(8,128)S(1)}, f32[256,1024]{1,0:T(8,128)S(1)}, u32[]{:S(2)}, u32[]{:S(2)}) collective-permute-start(f32[256,1024]{1,0:T(8,128)S(1)} %unstack.21), channel_id=1, source_target_pairs={{0,16},{4,20},{8,24},{12,28},{16,0},{20,4},{24,8},{28,12},{1,17},{... | collective-permute-start | bytes 3145736 | tf_op jit(solution)/shard_map/ppermute | solution.py:33
  495.6 65.2 %collective-permute-start.63 = (f32[512,256]{1,0:T(8,128)S(1)}, f32[512,256]{1,0:T(8,128)S(1)}, u32[]{:S(2)}, u32[]{:S(2)}) collective-permute-start(f32[512,256]{1,0:T(8,128)S(1)} %unstack.23), channel_id=1, source_target_pairs={{0,16},{4,20},{8,24},{12,28},{16,0},{20,4},{24,8},{28,12},{1,17},{... | collective-permute-start | bytes 1572872 | tf_op jit(solution)/shard_map/ppermute | solution.py:33
  (83 other events, 741.2 us)

commit v3 on v2

--- a/solution.py
+++ b/solution.py
@@ -174,20 +174,16 @@
     down = dot_tn(hidden, cc_ref[...])
     gate = dot(at_ref[...], d_gate)
     up = dot(at_ref[...], d_up)
-    count = len(sums) // 2
+    count = len(sums) // 3
     for j in range(count):
         part = slice(j * block, (j + 1) * block)
-        for k, rows, fresh in (
-            (j, slice(None), down[:, part]),
-            (count + j, slice(0, block), gate[part]),
-            (count + j, slice(block, 2 * block), up[part]),
-        ):
-            old = 0.0 if before is None else before[k][rows, :]
-            sums[k][rows, :] = fresh + old
+        for k, fresh in ((j, down[:, part]), (count + j, gate[part]), (2 * count + j, up[part])):
+            old = 0.0 if before is None else before[k][...]
+            sums[k][...] = fresh + old
 
 
 def rest_kernel(where_ref, nb_ref, cb_ref, hid_ref, dg_ref, du_ref, wd_ref, *rest):
-    count = (len(rest) - 4) // 2
+    count = (len(rest) - 4) // 3
     ya_ref, yb_ref, *sums = rest[:-2]
     at_ref, cc_ref = rest[-2:]
     half = ya_ref.shape[0]
@@ -207,9 +203,9 @@
 
 def sum_specs(count, block, hidden):
     specs = [pl.BlockSpec((TILE, block), lambda i, *_: (i, 0))] * count
-    specs += [pl.BlockSpec((2 * block, TILE), lambda i, *_: (0, i))] * count
+    specs += [pl.BlockSpec((block, TILE), lambda i, *_: (0, i))] * (2 * count)
     shapes = [jax.ShapeDtypeStruct((hidden, block), f32)] * count
-    shapes += [jax.ShapeDtypeStruct((2 * block, hidden), f32)] * count
+    shapes += [jax.ShapeDtypeStruct((block, hidden), f32)] * (2 * count)
     return specs, shapes
 
 
@@ -246,21 +242,25 @@
     return out[0], out[1], list(out[2:])
 
 
-def group_kernel(pieces, count, where_ref, *refs):
-    n_refs, refs = refs[:pieces], refs[pieces:]
-    c_refs, refs = refs[:pieces], refs[pieces:]
+def group_kernel(n_pieces, c_pieces, count, where_ref, *refs):
+    n_refs, refs = refs[:n_pieces], refs[n_pieces:]
+    c_refs, refs = refs[:c_pieces], refs[c_pieces:]
     g_ref, wg_ref, wu_ref, wd_ref = refs[:4]
-    before = refs[4 : 4 + 2 * count]
-    sums = refs[4 + 2 * count : 4 + 4 * count]
-    nb_ref, cb_ref, at_ref, cc_ref = refs[4 + 4 * count :]
+    before = refs[4 : 4 + 3 * count]
+    sums = refs[4 + 3 * count : 4 + 6 * count]
+    nb_ref, cb_ref, at_ref, cc_ref = refs[4 + 6 * count :]
     block = cc_ref.shape[1] // count
 
     @pl.when(pl.program_id(0) == 0)
     def _():
         at = 0
-        for n_ref, c_ref in zip(n_refs, c_refs):
+        for n_ref in n_refs:
             size = n_ref.shape[0]
             nb_ref[at : at + size, :] = (n_ref[...] * g_ref[...]).astype(b16)
+            at += size
+        at = 0
+        for c_ref in c_refs:
+            size = c_ref.shape[0]
             cb_ref[at : at + size, :] = (c_ref[...] * 0.5).astype(b16)
             at += size
         put_columns(at_ref, cc_ref, nb_ref, cb_ref, where_ref, count, block)
@@ -276,7 +276,7 @@
     specs, shapes = sum_specs(count, block, ff)
     return list(
         pl.pallas_call(
-            functools.partial(group_kernel, len(ns), count),
+            functools.partial(group_kernel, len(ns), len(cs), count),
             grid_spec=pltpu.PrefetchScalarGridSpec(
                 num_scalar_prefetch=1,
                 grid=(ff // TILE,),
@@ -310,18 +310,14 @@
         at = slice(i * size, (i + 1) * size)
         total = a_ref[at, :] + b_ref[...]
         outs[0][at, :] = total
-        if len(outs) == 1 + count:
-            outs[1 + i][...] = total
-        elif len(outs) > 1:
-            small = outs[1].shape[0]
-            for j in range(size // small):
-                outs[1 + i * (size // small) + j][...] = total[j * small : (j + 1) * small]
-
-
-def sum_of(a, bs, split=False):
+    pieces = outs[1:]
+    for i, piece in enumerate(pieces):
+        piece[...] = outs[0][i * piece.shape[0] : (i + 1) * piece.shape[0], :]
+
+
+def sum_of(a, bs, split=0):
     shapes = [jax.ShapeDtypeStruct(a.shape, f32)]
-    if split:
-        shapes += [jax.ShapeDtypeStruct((a.shape[0] // PIECES, a.shape[1]), f32)] * PIECES
+    shapes += [jax.ShapeDtypeStruct((a.shape[0] // max(split, 1), a.shape[1]), f32)] * split
     return pl.pallas_call(
         functools.partial(sum_kernel, len(bs)),
         in_specs=[whole(x.shape) for x in (a, *bs)],
@@ -333,11 +329,13 @@
     )(a, *bs)
 
 
-def resid_kernel(x_at_ref, tok_ref, a_ref, b_ref, r_ref, n_ref, quarter_ref, *pieces):
+def resid_kernel(x_at_ref, tok_ref, a_ref, b_ref, c_ref, r_ref, n_ref, quarter_ref, *pieces):
     size = pieces[0].shape[0]
     for i, piece in enumerate(pieces):
         at = slice(i * size, (i + 1) * size)
-        resid = tok_ref[at, :].astype(f32) + (a_ref[at, :] + b_ref[at, :])
+        part, first = (b_ref, 0) if i < len(pieces) // 2 else (c_ref, len(pieces) // 2)
+        far = part[(i - first) * size : (i - first + 1) * size, :]
+        resid = tok_ref[at, :].astype(f32) + (a_ref[at, :] + far)
         r_ref[at, :] = resid
         piece[...] = resid
         n_ref[at, :] = resid * lax.rsqrt(jnp.mean(resid * resid, axis=-1, keepdims=True) + EPS)
@@ -345,7 +343,7 @@
     quarter_ref[...] = n_ref[pl.ds(pl.multiple_of(x_at_ref[0] * small, small), small), :]
 
 
-def resid_of(x_at, tok, a, b):
+def resid_of(x_at, tok, a, b, c):
     rows, width = a.shape
     shapes = [(rows, width), (rows, width), (rows // 2, width)] + [(rows // PIECES, width)] * PIECES
     return pl.pallas_call(
@@ -353,13 +351,13 @@
         grid_spec=pltpu.PrefetchScalarGridSpec(
             num_scalar_prefetch=1,
             grid=(1,),
-            in_specs=[whole(a.shape)] * 3,
+            in_specs=[whole(a.shape)] * 2 + [whole(b.shape)] * 2,
             out_specs=[whole(s) for s in shapes],
         ),
         out_shape=[jax.ShapeDtypeStruct(s, f32) for s in shapes],
         compiler_params=vmem(),
         name="resid_of",
-    )(x_at, tok, a, b)
+    )(x_at, tok, a, b, c)
 
 
 def feed(normed, cot, w_gate, w_up, w_down):
@@ -380,9 +378,7 @@
     pair = jnp.concatenate([d_gate, d_up], axis=1)
     both = [dot_tn(take(normed), pair) for take in takes]
     ff = hidden.shape[1]
-    return [dot_tn(hidden, take(cot)) for take in takes] + [
-        jnp.concatenate([b[:, :ff], b[:, ff:]]) for b in both
-    ]
+    return [dot_tn(hidden, take(cot)) for take in takes] + [b[:, :ff] for b in both] + [b[:, ff:] for b in both]
 
 
 def plain_own_feed(r_a, r_b, cot, g, w_gate, w_up, w_down):
@@ -446,7 +442,7 @@
 
 
 def attend_kernel(half, core_ref, tok_ref, g_ref, wq_ref, wk_ref, wv_ref, qg_ref, kg_ref, wo_ref, cos_ref, sin_ref, *outs):
-    n_ref, q_ref, k_ref, v_ref, att_ref, mine_ref = outs[:6]
+    n_ref, q_ref, k_ref, v_ref, att_ref, wide_ref, mine_ref = outs[:7]
     width = qg_ref.shape[1]
     cosine, sine = cos_ref[...], sin_ref[...]
     unit, _ = norm_of(tok_ref[...].astype(f32))
@@ -470,11 +466,12 @@
             q_rot = turn(q_unit * qg_ref[...], cosine, sine).astype(b16)
             probs = softmax_of(q_rot, k_rot).astype(b16)
             att_ref[:, to] = dot(probs, values[:, at]).astype(b16)
+    wide_ref[...] = att_ref[...].astype(f32) * 2.0
     mixed = dot(att_ref[...], wo_ref[...])
 
     @pl.when(pl.program_id(0) < half)
     def _():
-        for i, ref in enumerate(outs[6:]):
+        for i, ref in enumerate(outs[7:]):
             ref[...] = mixed[i * ref.shape[0] : (i + 1) * ref.shape[0]]
 
     @pl.when(pl.program_id(0) >= half)
@@ -498,7 +495,7 @@
         return pl.BlockSpec((SEQ_LEN, columns), place), jax.ShapeDtypeStruct((rows, columns), dtype)
 
     nq, nk = wq.shape[1], wk.shape[1]
-    outs = [out(width, b16), out(nq, f32), out(nk, f32), out(nk, b16), out(nq, b16)]
+    outs = [out(width, b16), out(nq, f32), out(nk, f32), out(nk, b16), out(nq, b16), out(nq, f32)]
     part = jax.ShapeDtypeStruct((rows // 2, width), f32)
     piece = SEQ_LEN // PIECES
     return pl.pallas_call(
@@ -527,8 +524,8 @@
     ins, outs = refs[:18], refs[18:]
     dna_ref, ra_ref, cot_ref, tok_ref, q_ref, k_ref, v_ref, att_ref = ins[:8]
     gm_ref, ga_ref, qg_ref, kg_ref, wq_ref, wk_ref, wv_ref, wo_ref, cos_ref, sin_ref = ins[8:]
-    dr_ref, drm_ref, dqkv_ref, d1a_ref, ga_out, gq_out, gk_out = outs[:7]
-    d1b_refs, (r_ref, dn_ref) = outs[7:-2], outs[-2:]
+    dr_ref, drm_ref, dqkv_ref, wide_ref, d1a_ref, ga_out, gq_out, gk_out = outs[:8]
+    d1b_refs, (r_ref, dn_ref) = outs[8:-2], outs[-2:]
     step = pl.program_id(0)
     width = qg_ref.shape[1]
     cosine, sine = cos_ref[...], sin_ref[...]
@@ -592,6 +589,7 @@
         dqkv_ref[:, here] = norm_back(d_kn * kg_ref[...], k_unit, k_inv).astype(b16)
         here = slice(nq + nk + kv * width, nq + nk + (kv + 1) * width)
         dqkv_ref[:, here] = d_values.astype(b16)
+    wide_ref[...] = dqkv_ref[...].astype(f32) * 2.0
     d_norm1 = (
         dot_nt(dqkv_ref[:, :nq], wq_ref[...])
         + dot_nt(dqkv_ref[:, nq : nq + nk], wk_ref[...])
@@ -660,6 +658,7 @@
                 block(width, same),
                 block(width, low),
                 block(nq + 2 * nk, same),
+                block(nq + 2 * nk, same),
                 block(width, low),
             ]
             + [whole(s) for s in small]
@@ -670,6 +669,7 @@
             jax.ShapeDtypeStruct((rows, width), b16),
             part,
             jax.ShapeDtypeStruct((rows, nq + 2 * nk), b16),
+            jax.ShapeDtypeStruct((rows, nq + 2 * nk), f32),
             part,
         ]
         + [jax.ShapeDtypeStruct(s, f32) for s in small]
@@ -679,48 +679,114 @@
     )(core, *dn_b, *r_b, dn_a, r_a, cot, tokens, q, k, v, att, *consts)
 
 
-def rows_kernel(where_ref, a_ref, b_ref, out_ref):
-    out_ref[...] = dot_tn(a_ref[...], b_ref[...])
-
-
-def input_grads(where, a, b, block):
+def back_kernel(dr_ref, a_ref, b_ref, tok_ref, g_ref, out_ref, *pieces):
+    size = pieces[0].shape[0]
+    for i, piece in enumerate(pieces):
+        at = slice(i * size, (i + 1) * size)
+        unit, inv = norm_of(tok_ref[at, :].astype(f32))
+        grads = dr_ref[at, :] + norm_back((a_ref[at, :] + b_ref[at, :]) * g_ref[...], unit, inv)
+        out_ref[at, :] = grads
+        piece[...] = grads
+
+
+def back_of(dr, a, b, tok, g):
+    rows, width = a.shape
+    shapes = [(rows, width)] + [(rows // PIECES, width)] * PIECES
+    return pl.pallas_call(
+        back_kernel,
+        grid=(1,),
+        in_specs=[whole(x.shape) for x in (dr, a, b, tok, g)],
+        out_specs=[whole(x) for x in shapes],
+        out_shape=[jax.ShapeDtypeStruct(x, f32) for x in shapes],
+        compiler_params=vmem(),
+        name="back_of",
+    )(dr, a, b, tok, g)
+
+
+def few_kernel(normed, where_ref, a_ref, g_ref, out_ref, row_ref):
+    block = out_ref.shape[1] // where_ref.shape[0]
+    here = a_ref[...].astype(f32)
+    if normed:
+        here = (norm_of(here)[0] * g_ref[...]).astype(b16).astype(f32)
+    row_ref[...] = here
+    for j in range(where_ref.shape[0]):
+        at = pl.ds(pl.multiple_of(where_ref[j] * block, 128), block)
+        out_ref[:, j * block : (j + 1) * block] = row_ref[:, at]
+
+
+def few_of(where, a, g, block, normed):
+    half, width = a.shape[0] if normed else a.shape[0] // 2, a.shape[1]
+    out = (half, where.shape[0] * block)
+    return pl.pallas_call(
+        functools.partial(few_kernel, normed),
+        grid_spec=pltpu.PrefetchScalarGridSpec(
+            num_scalar_prefetch=1,
+            grid=(1,),
+            in_specs=[whole((half, width)), whole(g.shape)],
+            out_specs=whole(out),
+            scratch_shapes=[pltpu.VMEM((half, width), f32)],
+        ),
+        out_shape=jax.ShapeDtypeStruct(out, f32),
+        compiler_params=vmem(),
+        name="few_of",
+    )(where, a, g)
+
+
+def plain_few_of(where, a, g, block, normed):
+    half = a.shape[0] if normed else a.shape[0] // 2
+    here = a[:half].astype(f32)
+    if normed:
+        here = rms_norm(here, g)[0].astype(b16).astype(f32)
+    return jnp.concatenate([lax.dynamic_slice_in_dim(here, w * block, block, 1) for w in where], axis=1) * 2.0
+
+
+def pair_kernel(inward, where_ref, a_ref, b_ref, few_a_ref, few_b_ref, wide_ref, out_ref, far_a_ref, far_b_ref):
+    half = few_a_ref.shape[0]
+
+    @pl.when(pl.program_id(0) == 0)
+    def _():
+        far_b_ref[...] = (wide_ref[...] * 0.5).astype(b16)
+
+    far_a_ref[:half, :] = few_a_ref[...].astype(b16)
+    far_a_ref[half:, :] = few_b_ref[...].astype(b16)
+    if inward:
+        out_ref[...] = dot_tn(a_ref[...], b_ref[...]) + dot_tn(far_a_ref[...], far_b_ref[...])
+    else:
+        out_ref[...] = dot_tn(b_ref[...], a_ref[...]) + dot_tn(far_b_ref[...], far_a_ref[...])
+
+
+def pair_grads(where, first, a, b, few, wide, block, inward):
     rows, columns, count = a.shape[0], b.shape[1], where.shape[0]
+    out = (block, columns) if inward else (columns, block)
     return pl.pallas_call(
-        rows_kernel,
+        functools.partial(pair_kernel, inward),
         grid_spec=pltpu.PrefetchScalarGridSpec(
             num_scalar_prefetch=1,
             grid=(count,),
-            in_specs=[pl.BlockSpec((rows, block), lambda j, at: (0, at[j])), whole((rows, columns))],
-            out_specs=pl.BlockSpec((block, columns), lambda j, _: (j, 0)),
+            in_specs=[pl.BlockSpec((rows, block), lambda j, at: (0, at[j])), whole((rows, columns))]
+            + [pl.BlockSpec((rows // 2, block), lambda j, _: (0, first + j))] * 2
+            + [whole((rows, columns))],
+            out_specs=pl.BlockSpec(out, lambda j, _: (j, 0)),
+            scratch_shapes=[pltpu.VMEM((rows, block), b16), pltpu.VMEM((rows, columns), b16)],
         ),
-        out_shape=jax.ShapeDtypeStruct((count * block, columns), f32),
+        out_shape=jax.ShapeDtypeStruct((count * out[0], out[1]), f32),
         compiler_params=vmem(),
-        name="input_grads",
-    )(where, a, b)
-
-
-def output_grads(where, a, b, block):
-    rows, columns, count = a.shape[0], a.shape[1], where.shape[0]
-    return pl.pallas_call(
-        rows_kernel,
-        grid_spec=pltpu.PrefetchScalarGridSpec(
-            num_scalar_prefetch=1,
-            grid=(count,),
-            in_specs=[whole((rows, columns)), pl.BlockSpec((rows, block), lambda j, at: (0, at[j]))],
-            out_specs=pl.BlockSpec((columns, block), lambda j, _: (j, 0)),
-        ),
-        out_shape=jax.ShapeDtypeStruct((count * columns, block), f32),
-        compiler_params=vmem(),
-        name="output_grads",
-    )(where, a, b)
-
-
-def plain_input_grads(where, a, b, block):
-    return jnp.concatenate([dot_tn(lax.dynamic_slice_in_dim(a, w * block, block, 1), b) for w in where])
-
-
-def plain_output_grads(where, a, b, block):
-    return jnp.concatenate([dot_tn(a, lax.dynamic_slice_in_dim(b, w * block, block, 1)) for w in where])
+        name="pair_grads",
+    )(where, a, b, *few, wide)
+
+
+def plain_pair_grads(where, first, a, b, few, wide, block, inward):
+    far_a = (jnp.concatenate(few) * 0.5).astype(b16)
+    far_b = (wide * 0.5).astype(b16)
+    out = []
+    for j, w in enumerate(where):
+        near_a = lax.dynamic_slice_in_dim(a, w * block, block, 1)
+        other = far_a[:, (first + j) * block : (first + j + 1) * block]
+        if inward:
+            out.append(dot_tn(near_a, b) + dot_tn(other, far_b))
+        else:
+            out.append(dot_tn(b, near_a) + dot_tn(far_b, other))
+    return jnp.concatenate(out)
 
 
 def tensor_masks():
@@ -807,6 +873,13 @@
     def x_swap(a):
         return swap(a, "tensor", 2)
 
+    few = pick(few_of, plain_few_of)
+    pair = pick(pair_grads, plain_pair_grads)
+    rest = middle + [far]
+    blocks = relative(rest)
+    q = len(blocks) // 2
+    theirs_at = at([near ^ o for o in blocks])
+
     cot_mine, cot_theirs = mine_of(cotangent), theirs_of(cotangent)
     cot_own = jnp.concatenate([cot_mine, cot_theirs])
     c0 = cot_mine.astype(f32) * 2.0
@@ -814,149 +887,139 @@
     c1 = swap(c0, "dp", near)
     c2 = swap(c0_quarter, "dp", far)
     tok_mine = mine_of(tokens)
-    normed1, query, keys, values, attended, mixed_a, *mixed_b = seq(
+    normed1, query, keys, values, attended, att_wide, mixed_a, *mixed_b = seq(
         *attend(core_at, tokens_then, ga, w_query, w_key, w_value, gq, gk, w_out, cosine, sine)
     )
     mixed_got = seq(*core_swaps(mixed_b))
-    (mixed_chip,) = sum_of(mixed_a, mixed_got)
-    mixed_chip = seq(mixed_chip)
-    mixed_x = x_swap(mixed_chip)
-    c1, c2 = seq(c1, c2)
-    c3 = swap(c2, "dp", near)
-    c2x = x_swap(c2)
-    c1t = core_swap(c1)
-
-    mixed_x = seq(mixed_x)
-    r_a, n0, n0_quarter, *r_split = seq(*resid_of(x_at, tok_mine, mixed_chip, mixed_x))
+    mixed_chip, *mixed_split = seq(*sum_of(mixed_a, mixed_got, split=2))
+    mixed_x = [x_swap(p) for p in mixed_split]
+    near_n = swap(seq(few(theirs_at, tok_mine, ga, block, True)), "dp", near)
+    c1, c2, near_n, *mixed_x = seq(c1, c2, near_n, *mixed_x)
+
+    r_a, n0, n0_quarter, *r_split = seq(*resid_of(x_at, tok_mine, mixed_chip, *mixed_x))
     n1 = swap(n0, "dp", near)
     n2 = swap(n0_quarter, "dp", far)
-    r_b = core_swaps(r_split)
-    c3, *r_b = seq(c3, *r_b)
-    c3x = x_swap(c3)
+    c2x = x_swap(c2)
+    r_b = seq(*core_swaps(r_split))
 
     normed2, hidden, d_gate, d_up, dn_a, *dn_b, mlp_gain = seq(
         *pick(own_feed, plain_own_feed)(r_a, r_b, cot_own, gm, w_gate, w_up, w_down)
     )
-    dn_got = core_swaps(dn_b)
     offsets = relative(middle)
     down_a, down_b, sums = pick(own_rest, plain_own_rest)(
         at(offsets), normed2, cot_own, hidden, d_gate, d_up, w_down, block
     )
-    down_a, down_b, *sums = seq(down_a, down_b, *sums)
-    n1, n2, c1t, c2x, c3x = seq(n1, n2, c1t, c2x, c3x)
+    down_a, down_b, *both = seq(down_a, down_b, *sums, *dn_b)
+    sums, dn_b = both[:-PIECES], both[-PIECES:]
+    n2, c2x = seq(n2, c2x)
+    n2x = x_swap(n2)
     n3 = swap(n2, "dp", near)
-    n2x = x_swap(n2)
-    n1t = core_swap(n1)
-    moved_c = core_swaps((c2, c2x, c3, c3x))
-    down_got = core_swap(down_b)
-    dn_got = seq(*dn_got)
+    n1, *dn_got = seq(n1, *core_swaps(dn_b))
     (dn_chip,) = sum_of(dn_a, dn_got)
-    n1t, dn_chip = seq(n1t, dn_chip)
+    c2 = jnp.concatenate([c2, c2x])
+    dn_chip, c2 = seq(dn_chip, c2)
+    n1t, c1t = core_swaps((n1, c1))
+    n1t, c1t, n2x, n3, dn_chip, c2 = seq(n1t, c1t, n2x, n3, dn_chip, c2)
+    dn_x = x_swap(dn_chip)
+    c3 = swap(c2, "dp", near)
 
     def add_group(ns, cs, sums):
         group = pick(group_feed, plain_group_feed)
         return list(seq(*group(at(offsets), ns, cs, gm, w_gate, w_up, w_down, sums, block)))
 
+    n2t, c2t = core_swaps((n2, c2))
     sums = add_group([n1, n1t], [c1, c1t], sums)
-    n3, n2x, *moved_c = seq(n3, n2x, *moved_c)
+    n2t, c2t = seq(n2t, c2t)
+    n2xt = seq(core_swap(n2x))
+    sums = add_group([n2, n2x, n2t, n2xt], [c2, c2t], sums)
+    dn_x, c3, n3 = seq(dn_x, c3, n3)
+
     n3x = x_swap(n3)
-    n2t, n2xt, n3t = core_swaps((n2, n2x, n3))
-    n2t, n2xt = seq(n2t, n2xt)
-    dn_chip = seq(dn_chip)
-    dn_x = x_swap(dn_chip)
-    sums = add_group([n2, n2x, n2t, n2xt], [c2, c2x, moved_c[0], moved_c[1]], sums)
-    n3x, n3t, down_got = seq(n3x, n3t, down_got)
-    (down_chip,) = sum_of(down_a, [down_got])
-    n3xt, down_chip = seq(core_swap(n3x), down_chip)
-    sums = add_group([n3, n3x, n3t, n3xt], [c3, c3x, moved_c[2], moved_c[3]], sums)
-    k = len(offsets)
-    h = k // 2
-
-    def first_step(parts):
-        return [swap(p, "dp", middle[0]) for p in parts[h:]]
-
-    got_down, got_gu = first_step(sums[:k]), first_step(sums[k:])
-    keep_down, keep_gu = sums[:h], sums[k : k + h]
-
-    dn_x = seq(dn_x)
-    dn_mine, *dn_split = seq(*sum_of(dn_chip, [dn_x], split=True))
-    down_x = x_swap(down_chip)
+    dn_mine, *dn_split = seq(*sum_of(dn_chip, [dn_x], split=PIECES))
     dn_theirs = seq(*core_swaps(dn_split))
-    dr_b, dr_mine, d_qkv, d1_a, gain_a, gain_q, gain_k, *d1_b = seq(
+    near_att = swap(att_wide, "dp", near)
+    c3t, n3t, down_got = core_swaps((c3, n3, down_b))
+    dr_b, dr_mine, d_qkv, d_wide, d1_a, gain_a, gain_q, gain_k, *d1_b = seq(
         *attend_back(
             core_at, dn_mine, dn_theirs, r_a, r_b, cot_own, tokens, query, keys, values, attended,
             gm, ga, gq, gk, w_query, w_key, w_value, w_out, cosine, sine,
         )
     )
+    near_r = few(theirs_at, dr_b, gm, block, False)
+    near_r, n3x, c3t, n3t, near_att, down_got = seq(near_r, n3x, c3t, n3t, near_att, down_got)
+    near_d = swap(d_wide, "dp", near)
+    near_r = swap(near_r, "dp", near)
     gains = jnp.concatenate([gain_a[0], gain_q[0], gain_k[0], mlp_gain[0]])
-    gains_got = swap(gains, "dp", near)
-    d1_got = core_swaps(d1_b)
-
-    every = [near] + middle + [far]
-    rest = every[1:]
-    blocks = relative(every)
-    q = len(blocks) // 4
-    of_in, of_out = pick(input_grads, plain_input_grads), pick(output_grads, plain_output_grads)
-
-    def ins(i, count=1):
-        return of_in(at(blocks[i * q : (i + count) * q]), normed1, d_qkv, block)
-
-    def outs(i, count=1):
-        return of_out(at(blocks[i * q : (i + count) * q]), attended, dr_b, block)
-
-    in_3 = seq(ins(3))
-    in_got3 = swap(in_3, "dp", near)
-    out_23 = seq(outs(2, 2))
-    out_got = swap(out_23, "dp", near)
-    *d1_got, gains_got = seq(*d1_got, gains_got)
-    (d1_chip,) = sum_of(d1_a, d1_got)
-    d1_chip = seq(d1_chip)
-    d1_x = x_swap(d1_chip)
-    gains = gains + gains_got
-    in_2 = seq(ins(2))
-    in_got2 = swap(in_2, "dp", near)
-    out_01, in_1, in_0 = seq(outs(0, 2), ins(1), ins(0))
-    got_down = one(seq(*got_down), h)
+    gains_got = x_swap(gains)
+    n3xt = seq(core_swap(n3x))
+    sums = add_group([n3, n3x, n3t, n3xt], [c3, c3t], sums)
+    k = len(offsets)
+    h = k // 2
+    lists = [sums[i * k : (i + 1) * k] for i in range(3)]
+    keep = [p[:h] for p in lists]
+    send = [p[h:] for p in lists]
+
+    def first_step(parts):
+        return [swap(p, "dp", middle[0]) for p in parts]
 
     def finish(keep, got):
         return scatter_sum([a + b for a, b in zip(keep, got)], middle[1:])
 
-    summed_down = finish(keep_down, got_down)
-    down_x = seq(down_x)
-    down_mine, *down_split = seq(*sum_of(down_chip, [down_x], split=True))
-    down_theirs = core_swaps(down_split)
-    in_got3, *down_theirs = seq(in_got3, *down_theirs)
-    (in_1,) = sum_of(in_1, [in_got3])
+    got = first_step(send[0]) + first_step(send[1])
+    gains = gains + seq(gains_got)
+    near_nt, gains_got, *d1_got = seq(*core_swaps((near_n, gains, *d1_b)))
+    gains = gains + gains_got
+    gains_got = swap(gains, "dp", near)
+    (d1_chip,), (down_chip,) = sum_of(d1_a, d1_got), sum_of(down_a, [down_got])
+    d1_chip, down_chip = seq(d1_chip, down_chip)
+    d1_x = x_swap(d1_chip)
+    near_d, near_r, gains_got, down_chip, *got = seq(near_d, near_r, gains_got, down_chip, *got)
+    gains = gains + gains_got
+    near_ns = [near_n, near_nt]
+    down_x = x_swap(down_chip)
+
+    def ins(i):
+        return pair(at(blocks[i * q : (i + 1) * q]), i * q, normed1, d_qkv, near_ns, near_d, block, True)
+
+    def outs(i):
+        return pair(at(blocks[i * q : (i + 1) * q]), i * q, dr_b, attended, near_rs, near_att, block, False)
+
+    near_rt = core_swap(near_r)
+    in_1 = seq(ins(1))
     in_mid = swap(in_1, "dp", rest[0])
-    down_theirs = jnp.concatenate(down_theirs)
-    r_theirs = jnp.concatenate(r_b)
-    output = in_order((r_a + down_mine).astype(b16), (r_theirs + down_theirs).astype(b16))
-    d1_x = seq(d1_x)
-    d1_mine = d1_chip + d1_x
-    _, unit1, rms1 = rms_norm(tok_mine.astype(f32), ga)
-    gt_mine = seq(dr_mine + rms_back(d1_mine, ga, unit1, rms1))
-    gt_theirs = core_swap(gt_mine)
-    got_gu = one(seq(*got_gu), h)
-    summed_gu = finish(keep_gu, got_gu)
-    out_got, gt_theirs = seq(out_got, gt_theirs)
-    (out_01,) = sum_of(out_01, [out_got])
-    at_half = out_01.shape[0] // 2
-    out_mid = swap(out_01[at_half:], "dp", rest[0])
-    grad_tokens = in_order(gt_mine, gt_theirs)
-    gains = seq(gains + x_swap(gains))
-    gains = seq(gains + core_swap(gains))
-    for mask in bits[1:]:
-        gains = seq(gains + swap(gains, "dp", mask))
-    in_got2 = seq(in_got2)
+    near_rs = [near_r, seq(near_rt)]
+    out_1 = seq(outs(1))
+    out_mid = swap(out_1, "dp", rest[0])
+    gains_got = swap(gains, "dp", rest[0])
+    in_0, out_0 = seq(ins(0), outs(0))
+    summed_down = finish(keep[0], got[:h])
+    summed_gate = finish(keep[1], got[h:])
+    if len(rest) == 2:
+        summed_down, summed_gate = seq(summed_down, summed_gate)
 
     def split(a):
         return list(a.reshape(q, a.shape[0] // q, a.shape[1]))
 
-    in_mid = seq(in_mid)
-    summed_qkv = scatter_sum(split(in_0 + in_got2 + in_mid), rest[1:])
-    out_mid = seq(out_mid)
-    summed_out = scatter_sum(split(out_01[:at_half] + out_mid), rest[1:])
-    summed_qkv, summed_out = seq(summed_qkv, summed_out)
+    d1_x = seq(d1_x)
+    gt_mine, *gt_split = seq(*back_of(dr_mine, d1_chip, d1_x, tok_mine, ga))
+    gt_theirs = jnp.concatenate(seq(*core_swaps(gt_split)))
+    grad_tokens = seq(in_order(gt_mine, gt_theirs))
+    in_mid, out_mid, gains_got, down_x, *send_up = seq(in_mid, out_mid, gains_got, down_x, *send[2])
+    got_up = first_step(send_up)
+    gains = gains + gains_got
+    gains_got = swap(gains, "dp", far)
+    both = seq(*split(in_0 + in_mid), *split(out_0 + out_mid))
+    summed_qkv, summed_out = scatter_sum(both[:q], rest[1:]), scatter_sum(both[q:], rest[1:])
+    down_mine, *down_split = seq(*sum_of(down_chip, [down_x], split=PIECES))
+    down_theirs = seq(*core_swaps(down_split))
+    down_theirs, r_theirs = jnp.concatenate(down_theirs), jnp.concatenate(r_b)
+    output = seq(in_order((r_a + down_mine).astype(b16), (r_theirs + down_theirs).astype(b16)))
+    gains = gains + gains_got
+    for mask in rest[1:-1]:
+        gains = gains + swap(gains, "dp", mask)
+    if len(rest) == 2:
+        summed_qkv, summed_out, *got_up = seq(summed_qkv, summed_out, *got_up)
+    summed_up = finish(keep[2], got_up)
     nq, nk = w_query.shape[1], w_key.shape[1]
     gains = gains + 0.0 * seq.token.astype(f32)
     return (
@@ -970,8 +1033,8 @@
         gains[width + hd : width + 2 * hd],
         summed_out,
         gains[width + 2 * hd :],
-        summed_gu[:block],
-        summed_gu[block:],
+        summed_gate,
+        summed_up,
         summed_down,
     )
 

time: 576 us -> 539 us (0.936)
  waiting for transfers between devices: 251 us -> 234 us
  other arithmetic: 31.2 us -> 20.5 us
  local copies, waits for them, and re-layouts: 20.3 us -> 14.4 us
    ppermute x64 -> x69, waiting for transfers between devices: 251 us -> 234 us  [swap(): return lax.ppermute(value, axis, [(i, i ^ mask) for i in range(size)])]
    pallas_call x9 -> x10, Pallas kernels: 98.8 us -> 107 us  [the longest x3 73.9 us: group_feed(): pl.pallas_call(functools.partial(group_kernel, len(ns), len(cs), count),...]
    pallas_call x8 -> x6, Pallas kernels: 32.2 us -> 24.9 us  [sum_of(): pl.pallas_call(functools.partial(sum_kernel, len(bs)), in_specs=[whole(x....]
    add x7 -> x3, other arithmetic: 6.81 us -> 0.54 us  [the longest x2 0.53 us: body(): both = seq(*split(in_0 + in_mid), *split(out_0 + out_mid))]
    ppermute x64 -> x69, starting transfers between devices: 44.4 us -> 42.8 us  [swap(): return lax.ppermute(value, axis, [(i, i ^ mask) for i in range(size)])]
  transfers between devices with their start and end apart: 64 -> 69, of which waited for: 25 -> 19; matrix products, arithmetic and copies ran while one was open for 6% -> 4% of each run, Pallas kernels for 35% -> 39%
where the time goes in v3:
time: 539 us; the launch traced here: 532 us
  waiting for transfers between devices  234 us (43%)
  Pallas kernels  218 us (40%)
  starting transfers between devices  42.8 us (8%)
  other arithmetic  20.5 us (4%)
  local copies, waits for them, and re-layouts  14.4 us (3%)
    ppermute x69, waiting for transfers between devices, swap(): return lax.ppermute(value, axis, [(i, i ^ mask) for i in range(size)])  234 us
    pallas_call x3, Pallas kernels, group_feed(): pl.pallas_call(functools.partial(group_kernel, len(ns), len(cs), count),...  73.9 us
    ppermute x69, starting transfers between devices, swap(): return lax.ppermute(value, axis, [(i, i ^ mask) for i in range(size)])  42.8 us
    pallas_call x1, Pallas kernels, own_feed(): pl.pallas_call(own_kernel, grid=(hidden // TILE,), in_specs=[whole((half,...  27.6 us
    pallas_call x6, Pallas kernels, sum_of(): pl.pallas_call(functools.partial(sum_kernel, len(bs)), in_specs=[whole(x....  24.9 us
    pallas_call x1, Pallas kernels, attend_back(): pl.pallas_call(functools.partial(attend_back_kernel, half), grid_spec=plt...  24.5 us
    pallas_call x4, Pallas kernels, pair_grads(): pl.pallas_call(functools.partial(pair_kernel, inward), grid_spec=pltpu.Pr...  19.9 us
    pallas_call x1, Pallas kernels, own_rest(): pl.pallas_call(rest_kernel, grid_spec=pltpu.PrefetchScalarGridSpec(num_sc...  14.7 us
  transfers between devices with their start and end apart: 69, of which 19 were waited for; matrix products, arithmetic and copies ran while one was open for 4% of the time, Pallas kernels for 39%

profile of v3, /device:TPU:0, one launch (start us, length us, event | category | flops | bytes accessed | tf_op | source)
XLA Modules:
  0.0 532.1 jit_solution(11596441634730817880)
XLA Ops:
  3.3 3.1 collective-permute-start.4
  8.6 13.9 %attend.1 = (bf16[512,2048]{1,0:T(8,128)(2,1)}, f32[512,512]{1,0:T(8,128)}, f32[512,256]{1,0:T(8,128)}, bf16[512,256]{1,0:T(8,128)(2,1)}, bf16[512,512]{1,0:T(8,...) custom-call(s32[1]{0:T(128)} %bitcast.1.core_ref, ...), custom_call_target="tpu_custom_call" | custom-call | tf_op jit(solution)/shard_map/attend/pallas_call | solution.py:501
  26.5 3.7 few_of.2
  32.8 4.3 sum_of.6
  39.6 39.2 %collective-permute-done.5 = f32[128,2048]{1,0:T(8,128)} collective-permute-done((f32[128,2048]{1,0:T(8,128)S(1)}, f32[128,2048]{1,0:T(8,128)}, u32[]{:S(2)}, u32[]{:S(2)}) %collective-permute-start.5) | collective-permute-done | bytes 1048608 | tf_op jit(solution)/shard_map/ppermute | solution.py:33
  78.8 6.0 %collective-permute-done.8.c_ref = f32[128,2048]{1,0:T(8,128)S(1)} collective-permute-done((f32[128,2048]{1,0:T(8,128)}, f32[128,2048]{1,0:T(8,128)S(1)}, u32[]{:S(2)}, u32[]{:S(2)}) %collective-permute-start.8) | collective-permute-done | bytes 1048608 | tf_op jit(solution)/shard_map/ppermute | solution.py:33
  85.8 5.6 %resid_of.1 = (f32[256,2048]{1,0:T(8,128)}, f32[256,2048]{1,0:T(8,128)}, f32[128,2048]{1,0:T(8,128)}, f32[64,2048]{1,0:T(8,128)}, f32[64,2048]{1,0:T(8,128)}, /*index=5*/f32[64,2048]{1,0:T(8,128)}, f32[64,2048]{1,0:T(8,128)}) custom-call(s32[1]{0:T(128)} %bitcast.x_at_ref, bf16[256,2048]{1,0:T(8,128)(2,1)} %constant_dynamic-slice_fusion.3.a_ref.tok_ref, ...), custom_call_target="tpu_custom_call" | custom-call | tf_op jit(solution)/shard_map/resid_of/pallas_call | solution.py:349
  100.3 27.6 %own_feed.1 = (bf16[512,2048]{1,0:T(8,128)(2,1)}, bf16[512,1536]{1,0:T(8,128)(2,1)}, bf16[512,1536]{1,0:T(8,128)(2,1)}, bf16[512,1536]{1,0:T(8,128)(2,1)}, f32[2...) custom-call(f32[256,2048]{1,0:T(8,128)} %get-tuple-element.366.ra_re, ...), custom_call_target="tpu_custom_call" | custom-call | tf_op jit(solution)/shard_map/own_feed/pallas_call | solution.py:130
  127.9 14.7 %own_rest.1 = (f32[256,2048]{1,0:T(8,128)}, f32[256,2048]{1,0:T(8,128)}, f32[1536,256]{1,0:T(8,128)}, f32[1536,256]{1,0:T(8,128)}, f32[256,1536]{1,0:T(8,128)}, ...) custom-call(s32[2]{0:T(128)} %get-tuple-element.646.where_ref, ...), custom_call_target="tpu_custom_call" | custom-call | tf_op jit(solution)/shard_map/own_rest/pallas_call | solution.py:219
  150.7 4.4 sum_of.7.refs_0_
  155.1 17.7 %collective-permute-done.22.refs_1_ = f32[128,2048]{1,0:T(8,128)} collective-permute-done((f32[128,2048]{1,0:T(8,128)}, f32[128,2048]{1,0:T(8,128)}, u32[]{:S(2)}, u32[]{:S(2)}) %collective-permute-start.22) | collective-permute-done | bytes 1048608 | tf_op jit(solution)/shard_map/ppermute | solution.py:33
  175.6 24.7 %group_feed.3 = (f32[1536,256]{1,0:T(8,128)}, f32[1536,256]{1,0:T(8,128)}, f32[256,1536]{1,0:T(8,128)}, f32[256,1536]{1,0:T(8,128)}, f32[256,1536]{1,0:T(8,128)}, /*index=5*/f32[256,1536]{1,0:T(8,128)}) custom-call(s32[2]{0:T(128)} %get-tuple-element.646.where_ref, f32[256,2048]{1,0:T(8,128)} %collective-permute-done.9.refs_0_, ...), custom_call_target="tpu_custom_call" | custom-call | tf_op jit(solution)/shard_map/group_feed/pallas_call | solution.py:278
  200.4 24.5 %group_feed.4 = (f32[1536,256]{1,0:T(8,128)}, f32[1536,256]{1,0:T(8,128)}, f32[256,1536]{1,0:T(8,128)}, f32[256,1536]{1,0:T(8,128)}, f32[256,1536]{1,0:T(8,128)}, /*index=5*/f32[256,1536]{1,0:T(8,128)}) custom-call(s32[2]{0:T(128)} %get-tuple-element.646.where_ref, f32[128,2048]{1,0:T(8,128)} %collective-permute-done.18.refs_0_, ...), custom_call_target="tpu_custom_call" | custom-call | tf_op jit(solution)/shard_map/group_feed/pallas_call | solution.py:278
  225.0 4.3 sum_of.8
  231.6 6.6 %collective-permute-done.30.refs_1_ = f32[64,2048]{1,0:T(8,128)S(1)} collective-permute-done((f32[64,2048]{1,0:T(8,128)}, f32[64,2048]{1,0:T(8,128)S(1)}, u32[]{:S(2)}, u32[]{:S(2)}) %collective-permute-start.30) | collective-permute-done | bytes 524320 | tf_op jit(solution)/shard_map/ppermute | solution.py:33
  241.0 24.5 %attend_back.1 = (bf16[512,2048]{1,0:T(8,128)(2,1)}, f32[256,2048]{1,0:T(8,128)}, bf16[512,1024]{1,0:T(8,128)(2,1)}, f32[512,1024]{1,0:T(8,128)}, f32[256,2048]{...) custom-call(s32[1]{0:T(128)} %bitcast.1.core_ref, ...), custom_call_target="tpu_custom_call" | custom-call | tf_op jit(solution)/shard_map/attend_back/pallas_call | solution.py:637
  266.0 3.2 few_of.3
  273.3 24.7 %group_feed.5 = (f32[1536,256]{1,0:T(8,128)}, f32[1536,256]{1,0:T(8,128)}, f32[256,1536]{1,0:T(8,128)}, f32[256,1536]{1,0:T(8,128)}, f32[256,1536]{1,0:T(8,128)}, /*index=5*/f32[256,1536]{1,0:T(8,128)}) custom-call(s32[2]{0:T(128)} %get-tuple-element.646.where_ref, f32[128,2048]{1,0:T(8,128)} %copy-done.23, f32[128,2048]{1,0:T(8,128)} %collective-permute-done.34.refs_1_, ...), custom_call_target="tpu_custom_call" | custom-call | tf_op jit(solution)/shard_map/group_feed/pallas_call | solution.py:278
  302.0 3.8 sum_of.10.refs_0_
  305.8 3.7 sum_of.9.a_ref
  310.5 8.4 %collective-permute-done.33.wide_ref = f32[512,1024]{1,0:T(8,128)S(1)} collective-permute-done((f32[512,1024]{1,0:T(8,128)}, f32[512,1024]{1,0:T(8,128)S(1)}, u32[]{:S(2)}, u32[]{:S(2)}) %collective-permute-start.33) | collective-permute-done | bytes 2097184 | tf_op jit(solution)/shard_map/ppermute | solution.py:33
  319.7 21.4 %collective-permute-done.39.few_a_ref = f32[256,1024]{1,0:T(8,128)S(1)} collective-permute-done((f32[256,1024]{1,0:T(8,128)}, f32[256,1024]{1,0:T(8,128)S(1)}, u32[]{:S(2)}, u32[]{:S(2)}) %collective-permute-start.39) | collective-permute-done | bytes 1048608 | tf_op jit(solution)/shard_map/ppermute | solution.py:33
  341.3 27.5 %collective-permute-done.50 = f32[256,1536]{1,0:T(8,128)} collective-permute-done((f32[256,1536]{1,0:T(8,128)}, f32[256,1536]{1,0:T(8,128)}, u32[]{:S(2)}, u32[]{:S(2)}) %collective-permute-start.50) | collective-permute-done | bytes 1572896 | tf_op jit(solution)/shard_map/ppermute | solution.py:33
  369.4 5.5 %pair_grads.4 = f32[512,1024]{1,0:T(8,128)} custom-call(s32[2]{0:T(128)} %broadcast_xor_fusion.where_ref, bf16[512,2048]{1,0:T(8,128)(2,1)} %get-tuple-element.550.a_ref, bf16[512,1024]{1,0:T(8,128)(2,1)} %get-tuple-element.551.b_ref, f32[256,1024]{1,0:T(8,128)} %copy-done.12, f32[256,1024]{1,0:T(8,128)} %collective-permute-done.42.few_b_ref, ...), custom_call_target="tpu_custom_call" | custom-call | tf_op jit(solution)/shard_map/pair_grads/pallas_call | solution.py:761
  377.3 5.6 %pair_grads.6 = f32[512,1024]{1,0:T(8,128)} custom-call(s32[2]{0:T(128)} %get-tuple-element.645.where_ref, bf16[512,2048]{1,0:T(8,128)(2,1)} %get-tuple-element.550.a_ref, bf16[512,1024]{1,0:T(8,128)(2,1)} %get-tuple-element.551.b_ref, f32[256,1024]{1,0:T(8,128)} %copy-done.12, f32[256,1024]{1,0:T(8,128)} %collective-permute-done.42.few_b_ref, ...), custom_call_target="tpu_custom_call" | custom-call | tf_op jit(solution)/shard_map/pair_grads/pallas_call | solution.py:761
  382.9 3.3 add.79
  389.0 4.3 pair_grads.7
  393.3 4.5 pair_grads.5
  397.8 6.1 %back_of.1 = (f32[256,2048]{1,0:T(8,128)}, f32[64,2048]{1,0:T(8,128)}, f32[64,2048]{1,0:T(8,128)}, f32[64,2048]{1,0:T(8,128)}, f32[64,2048]{1,0:T(8,128)}) custom-call(f32[256,2048]{1,0:T(8,128)} %get-tuple-element.564.dr_ref, f32[256,2048]{1,0:T(8,128)} %sum_of.9.a_ref, f32[256,2048]{1,0:T(8,128)} %collective-permute-done.56.b_ref, ...), custom_call_target="tpu_custom_call" | custom-call | tf_op jit(solution)/shard_map/back_of/pallas_call | solution.py:695
  409.6 36.5 %collective-permute-done.54 = f32[4352]{0:T(1024)S(1)} collective-permute-done((f32[4352]{0:T(1024)S(1)}, f32[4352]{0:T(1024)S(1)}, u32[]{:S(2)}, u32[]{:S(2)}) %collective-permute-start.54) | collective-permute-done | bytes 17440 | tf_op jit(solution)/shard_map/ppermute | solution.py:33
  449.4 4.3 sum_of.11
  462.7 63.4 %collective-permute-done.67 = f32[512,256]{1,0:T(8,128)S(1)} collective-permute-done((f32[512,256]{1,0:T(8,128)S(1)}, f32[512,256]{1,0:T(8,128)S(1)}, u32[]{:S(2)}, u32[]{:S(2)}) %collective-permute-start.67) | collective-permute-done | bytes 524320 | tf_op jit(solution)/shard_map/ppermute | solution.py:33
  (262 shorter events, 78.8 us)
Async XLA Ops:
  3.3 81.5 %collective-permute-start.4 = (f32[256,2048]{1,0:T(8,128)S(1)}, f32[256,2048]{1,0:T(8,128)}, u32[]{:S(2)}, u32[]{:S(2)}) collective-permute-start(f32[256,2048]{1,0:T(8,128)S(1)} %get-tuple-element.334), channel_id=1, source_target_pairs={{0,4},{4,0},{8,12},{12,8},{16,20},{20,16},{24,28},{28,24},{1,5},{5... | collective-permute-start | bytes 6291464 | tf_op jit(solution)/shard_map/ppermute | solution.py:33
  30.2 48.6 %collective-permute-start.5 = (f32[128,2048]{1,0:T(8,128)S(1)}, f32[128,2048]{1,0:T(8,128)}, u32[]{:S(2)}, u32[]{:S(2)}) collective-permute-start(f32[128,2048]{1,0:T(8,128)S(1)} %constant_dynamic-slice_fusion.1), channel_id=1, source_target_pairs={{0,16},{4,20},{8,24},{12,28},{16,0},{20,4},{24,8},{28,12},{1,17},{... | collective-permute-start | bytes 3145736 | tf_op jit(solution)/shard_map/ppermute | solution.py:33
  37.1 41.7 %collective-permute-start.6 = (f32[256,1024]{1,0:T(8,128)}, f32[256,1024]{1,0:T(8,128)S(1)}, u32[]{:S(2)}, u32[]{:S(2)}) collective-permute-start(f32[256,1024]{1,0:T(8,128)} %few_of.2), channel_id=1, source_target_pairs={{0,4},{4,0},{8,12},{12,8},{16,20},{20,16},{24,28},{28,24},{1,5},{5... | collective-permute-start | bytes 3145736 | tf_op jit(solution)/shard_map/ppermute | solution.py:33
  37.6 41.2 %collective-permute-start.7 = (f32[128,2048]{1,0:T(8,128)}, f32[128,2048]{1,0:T(8,128)S(1)}, u32[]{:S(2)}, u32[]{:S(2)}) collective-permute-start(f32[128,2048]{1,0:T(8,128)} %get-tuple-element.353), channel_id=1, source_target_pairs={{0,2},{1,3},{2,0},{3,1},{4,6},{5,7},{6,4},{7,5},{8,10},{9,11},{10,... | collective-permute-start | bytes 3145736 | tf_op jit(solution)/shard_map/ppermute | solution.py:33
  39.1 45.8 %collective-permute-start.8 = (f32[128,2048]{1,0:T(8,128)}, f32[128,2048]{1,0:T(8,128)S(1)}, u32[]{:S(2)}, u32[]{:S(2)}) collective-permute-start(f32[128,2048]{1,0:T(8,128)} %get-tuple-element.354), channel_id=1, source_target_pairs={{0,2},{1,3},{2,0},{3,1},{4,6},{5,7},{6,4},{7,5},{8,10},{9,11},{10,... | collective-permute-start | bytes 3145736 | tf_op jit(solution)/shard_map/ppermute | solution.py:33
  91.5 55.4 %collective-permute-start.9 = (f32[256,2048]{1,0:T(8,128)}, f32[256,2048]{1,0:T(8,128)}, u32[]{:S(2)}, u32[]{:S(2)}) collective-permute-start(f32[256,2048]{1,0:T(8,128)} %get-tuple-element.367), channel_id=1, source_target_pairs={{0,4},{4,0},{8,12},{12,8},{16,20},{20,16},{24,28},{28,24},{1,5},{5... | collective-permute-start | bytes 6291464 | tf_op jit(solution)/shard_map/ppermute | solution.py:33
  93.5 49.7 %collective-permute-start.18 = (f32[128,2048]{1,0:T(8,128)}, f32[128,2048]{1,0:T(8,128)}, u32[]{:S(2)}, u32[]{:S(2)}) collective-permute-start(f32[128,2048]{1,0:T(8,128)} %get-tuple-element.409), channel_id=1, source_target_pairs={{0,16},{4,20},{8,24},{12,28},{16,0},{20,4},{24,8},{28,12},{1,17},{... | collective-permute-start | bytes 3145736 | tf_op jit(solution)/shard_map/ppermute | solution.py:33
  93.9 49.6 %collective-permute-start.19 = (f32[128,2048]{1,0:T(8,128)}, f32[128,2048]{1,0:T(8,128)}, u32[]{:S(2)}, u32[]{:S(2)}) collective-permute-start(f32[128,2048]{1,0:T(8,128)} %collective-permute-done.5), channel_id=1, source_target_pairs={{0,2},{1,3},{2,0},{3,1},{4,6},{5,7},{6,4},{7,5},{8,10},{9,11},{10,... | collective-permute-start | bytes 3145736 | tf_op jit(solution)/shard_map/ppermute | solution.py:33
  144.6 29.0 %collective-permute-start.21 = (f32[256,2048]{1,0:T(8,128)}, f32[256,2048]{1,0:T(8,128)}, u32[]{:S(2)}, u32[]{:S(2)}) collective-permute-start(f32[256,2048]{1,0:T(8,128)} %collective-permute-done.4.refs_2_), channel_id=1, source_target_pairs={{0,1},{1,0},{2,3},{3,2},{4,5},{5,4},{6,7},{7,6},{8,9},{9,8},{10,11... | collective-permute-start | bytes 6291464 | tf_op jit(solution)/shard_map/ppermute | solution.py:33
  173.7 51.3 %collective-permute-start.24 = (f32[256,2048]{1,0:T(8,128)}, f32[256,2048]{1,0:T(8,128)}, u32[]{:S(2)}, u32[]{:S(2)}) collective-permute-start(f32[256,2048]{1,0:T(8,128)} %sum_of.7.refs_0_), channel_id=1, source_target_pairs={{0,2},{1,3},{2,0},{3,1},{4,6},{5,7},{6,4},{7,5},{8,10},{9,11},{10,... | collective-permute-start | bytes 6291464 | tf_op jit(solution)/shard_map/ppermute | solution.py:33
  174.6 50.3 %collective-permute-start.25 = (f32[256,2048]{1,0:T(8,128)S(1)}, f32[256,2048]{1,0:T(8,128)}, u32[]{:S(2)}, u32[]{:S(2)}) collective-permute-start(f32[256,2048]{1,0:T(8,128)S(1)} %pad_maximum_fusion.1.refs_4_), channel_id=1, source_target_pairs={{0,4},{4,0},{8,12},{12,8},{16,20},{20,16},{24,28},{28,24},{1,5},{5... | collective-permute-start | bytes 6291464 | tf_op jit(solution)/shard_map/ppermute | solution.py:33
  229.3 39.8 %collective-permute-start.38 = (f32[256,2048]{1,0:T(8,128)}, f32[256,2048]{1,0:T(8,128)}, u32[]{:S(2)}, u32[]{:S(2)}) collective-permute-start(f32[256,2048]{1,0:T(8,128)} %get-tuple-element.503), channel_id=1, source_target_pairs={{0,1},{1,0},{2,3},{3,2},{4,5},{5,4},{6,7},{7,6},{8,9},{9,8},{10,11... | collective-permute-start | bytes 6291464 | tf_op jit(solution)/shard_map/ppermute | solution.py:33
  229.8 39.3 %collective-permute-start.35 = (f32[256,2048]{1,0:T(8,128)}, f32[256,2048]{1,0:T(8,128)}, u32[]{:S(2)}, u32[]{:S(2)}) collective-permute-start(f32[256,2048]{1,0:T(8,128)} %collective-permute-done.25.refs_4_), channel_id=1, source_target_pairs={{0,1},{1,0},{2,3},{3,2},{4,5},{5,4},{6,7},{7,6},{8,9},{9,8},{10,11... | collective-permute-start | bytes 6291464 | tf_op jit(solution)/shard_map/ppermute | solution.py:33
  238.2 27.3 %collective-permute-start.37 = (f32[512,512]{1,0:T(8,128)}, f32[512,512]{1,0:T(8,128)S(1)}, u32[]{:S(2)}, u32[]{:S(2)}) collective-permute-start(f32[512,512]{1,0:T(8,128)} %get-tuple-element.502), channel_id=1, source_target_pairs={{0,4},{4,0},{8,12},{12,8},{16,20},{20,16},{24,28},{28,24},{1,5},{5... | collective-permute-start | bytes 3145736 | tf_op jit(solution)/shard_map/ppermute | solution.py:33
  239.8 29.4 %collective-permute-start.34 = (f32[128,2048]{1,0:T(8,128)}, f32[128,2048]{1,0:T(8,128)}, u32[]{:S(2)}, u32[]{:S(2)}) collective-permute-start(f32[128,2048]{1,0:T(8,128)} %copy-done.23), channel_id=1, source_target_pairs={{0,2},{1,3},{2,0},{3,1},{4,6},{5,7},{6,4},{7,5},{8,10},{9,11},{10,... | collective-permute-start | bytes 3145736 | tf_op jit(solution)/shard_map/ppermute | solution.py:33
  240.9 28.3 %collective-permute-start.36 = (f32[128,2048]{1,0:T(8,128)}, f32[128,2048]{1,0:T(8,128)S(1)}, u32[]{:S(2)}, u32[]{:S(2)}) collective-permute-start(f32[128,2048]{1,0:T(8,128)} %copy-done.23), channel_id=1, source_target_pairs={{0,1},{1,0},{2,3},{3,2},{4,5},{5,4},{6,7},{7,6},{8,9},{9,8},{10,11... | collective-permute-start | bytes 3145736 | tf_op jit(solution)/shard_map/ppermute | solution.py:33
  270.3 48.7 %collective-permute-start.33 = (f32[512,1024]{1,0:T(8,128)}, f32[512,1024]{1,0:T(8,128)S(1)}, u32[]{:S(2)}, u32[]{:S(2)}) collective-permute-start(f32[512,1024]{1,0:T(8,128)} %get-tuple-element.498), channel_id=1, source_target_pairs={{0,4},{4,0},{8,12},{12,8},{16,20},{20,16},{24,28},{28,24},{1,5},{5... | collective-permute-start | bytes 6291464 | tf_op jit(solution)/shard_map/ppermute | solution.py:33
  271.0 27.4 %collective-permute-start.44 = (f32[64,2048]{1,0:T(8,128)}, f32[64,2048]{1,0:T(8,128)S(1)}, u32[]{:S(2)}, u32[]{:S(2)}) collective-permute-start(f32[64,2048]{1,0:T(8,128)} %get-tuple-element.531), channel_id=1, source_target_pairs={{0,1},{1,0},{2,3},{3,2},{4,5},{5,4},{6,7},{7,6},{8,9},{9,8},{10,11... | collective-permute-start | bytes 1572872 | tf_op jit(solution)/shard_map/ppermute | solution.py:33
  271.1 28.8 %collective-permute-start.45 = (f32[64,2048]{1,0:T(8,128)}, f32[64,2048]{1,0:T(8,128)}, u32[]{:S(2)}, u32[]{:S(2)}) collective-permute-start(f32[64,2048]{1,0:T(8,128)} %get-tuple-element.532), channel_id=1, source_target_pairs={{0,1},{1,0},{2,3},{3,2},{4,5},{5,4},{6,7},{7,6},{8,9},{9,8},{10,11... | collective-permute-start | bytes 1572872 | tf_op jit(solution)/shard_map/ppermute | solution.py:33
  273.1 27.3 %collective-permute-start.46 = (f32[64,2048]{1,0:T(8,128)}, f32[64,2048]{1,0:T(8,128)S(1)}, u32[]{:S(2)}, u32[]{:S(2)}) collective-permute-start(f32[64,2048]{1,0:T(8,128)} %get-tuple-element.533), channel_id=1, source_target_pairs={{0,1},{1,0},{2,3},{3,2},{4,5},{5,4},{6,7},{7,6},{8,9},{9,8},{10,11... | collective-permute-start | bytes 1572872 | tf_op jit(solution)/shard_map/ppermute | solution.py:33
  298.4 42.9 %collective-permute-start.49 = (f32[1536,256]{1,0:T(8,128)}, f32[1536,256]{1,0:T(8,128)}, u32[]{:S(2)}, u32[]{:S(2)}) collective-permute-start(f32[1536,256]{1,0:T(8,128)} %get-tuple-element.546), channel_id=1, source_target_pairs={{0,8},{4,12},{8,0},{12,4},{16,24},{20,28},{24,16},{28,20},{1,9},{5... | collective-permute-start | bytes 4718600 | tf_op jit(solution)/shard_map/ppermute | solution.py:33
  299.9 68.9 %collective-permute-start.50 = (f32[256,1536]{1,0:T(8,128)}, f32[256,1536]{1,0:T(8,128)}, u32[]{:S(2)}, u32[]{:S(2)}) collective-permute-start(f32[256,1536]{1,0:T(8,128)} %get-tuple-element.547), channel_id=1, source_target_pairs={{0,8},{4,12},{8,0},{12,4},{16,24},{20,28},{24,16},{28,20},{1,9},{5... | collective-permute-start | bytes 4718600 | tf_op jit(solution)/shard_map/ppermute | solution.py:33
  301.2 39.8 %collective-permute-start.39 = (f32[256,1024]{1,0:T(8,128)}, f32[256,1024]{1,0:T(8,128)S(1)}, u32[]{:S(2)}, u32[]{:S(2)}) collective-permute-start(f32[256,1024]{1,0:T(8,128)} %few_of.3), channel_id=1, source_target_pairs={{0,4},{4,0},{8,12},{12,8},{16,20},{20,16},{24,28},{28,24},{1,5},{5... | collective-permute-start | bytes 3145736 | tf_op jit(solution)/shard_map/ppermute | solution.py:33
  309.5 88.3 %collective-permute-start.56 = (f32[256,2048]{1,0:T(8,128)}, f32[256,2048]{1,0:T(8,128)}, u32[]{:S(2)}, u32[]{:S(2)}) collective-permute-start(f32[256,2048]{1,0:T(8,128)} %sum_of.9.a_ref), channel_id=1, source_target_pairs={{0,2},{1,3},{2,0},{3,1},{4,6},{5,7},{6,4},{7,5},{8,10},{9,11},{10,... | collective-permute-start | bytes 6291464 | tf_op jit(solution)/shard_map/ppermute | solution.py:33
  374.9 71.2 %collective-permute-start.51 = (f32[512,1024]{1,0:T(8,128)}, f32[512,1024]{1,0:T(8,128)S(1)}, u32[]{:S(2)}, u32[]{:S(2)}) collective-permute-start(f32[512,1024]{1,0:T(8,128)} %pair_grads.4), channel_id=1, source_target_pairs={{0,8},{4,12},{8,0},{12,4},{16,24},{20,28},{24,16},{28,20},{1,9},{5... | collective-permute-start | bytes 6291464 | tf_op jit(solution)/shard_map/ppermute | solution.py:33
  376.4 69.6 %collective-permute-start.55 = (f32[256,2048]{1,0:T(8,128)}, f32[256,2048]{1,0:T(8,128)}, u32[]{:S(2)}, u32[]{:S(2)}) collective-permute-start(f32[256,2048]{1,0:T(8,128)} %sum_of.10.refs_0_), channel_id=1, source_target_pairs={{0,2},{1,3},{2,0},{3,1},{4,6},{5,7},{6,4},{7,5},{8,10},{9,11},{10,... | collective-permute-start | bytes 6291464 | tf_op jit(solution)/shard_map/ppermute | solution.py:33
  404.4 41.7 %collective-permute-start.53 = (f32[1024,256]{1,0:T(8,128)S(1)}, f32[1024,256]{1,0:T(8,128)S(1)}, u32[]{:S(2)}, u32[]{:S(2)}) collective-permute-start(f32[1024,256]{1,0:T(8,128)S(1)} %copy-done.25), channel_id=1, source_target_pairs={{0,8},{4,12},{8,0},{12,4},{16,24},{20,28},{24,16},{28,20},{1,9},{5... | collective-permute-start | bytes 3145736 | tf_op jit(solution)/shard_map/ppermute | solution.py:33
  408.7 37.4 %collective-permute-start.54 = (f32[4352]{0:T(1024)S(1)}, f32[4352]{0:T(1024)S(1)}, u32[]{:S(2)}, u32[]{:S(2)}) collective-permute-start(f32[4352]{0:T(1024)S(1)} %add.77), channel_id=1, source_target_pairs={{0,8},{4,12},{8,0},{12,4},{16,24},{20,28},{24,16},{28,20},{1,9},{5... | collective-permute-start | bytes 52232 | tf_op jit(solution)/shard_map/ppermute | solution.py:33
  447.6 79.4 %collective-permute-start.68 = (f32[256,1536]{1,0:T(8,128)}, f32[256,1536]{1,0:T(8,128)S(1)}, u32[]{:S(2)}, u32[]{:S(2)}) collective-permute-start(f32[256,1536]{1,0:T(8,128)} %get-tuple-element.622), channel_id=1, source_target_pairs={{0,8},{4,12},{8,0},{12,4},{16,24},{20,28},{24,16},{28,20},{1,9},{5... | collective-permute-start | bytes 4718600 | tf_op jit(solution)/shard_map/ppermute | solution.py:33
  454.2 72.7 %collective-permute-start.66 = (f32[256,1024]{1,0:T(8,128)}, f32[256,1024]{1,0:T(8,128)S(1)}, u32[]{:S(2)}, u32[]{:S(2)}) collective-permute-start(f32[256,1024]{1,0:T(8,128)} %get-tuple-element.619), channel_id=1, source_target_pairs={{0,16},{4,20},{8,24},{12,28},{16,0},{20,4},{24,8},{28,12},{1,17},{... | collective-permute-start | bytes 3145736 | tf_op jit(solution)/shard_map/ppermute | solution.py:33
  456.4 69.7 %collective-permute-start.67 = (f32[512,256]{1,0:T(8,128)S(1)}, f32[512,256]{1,0:T(8,128)S(1)}, u32[]{:S(2)}, u32[]{:S(2)}) collective-permute-start(f32[512,256]{1,0:T(8,128)S(1)} %get-tuple-element.621), channel_id=1, source_target_pairs={{0,16},{4,20},{8,24},{12,28},{16,0},{20,4},{24,8},{28,12},{1,17},{... | collective-permute-start | bytes 1572872 | tf_op jit(solution)/shard_map/ppermute | solution.py:33
  460.0 69.3 %collective-permute-start.65 = (f32[4352]{0:T(1024)S(1)}, f32[4352]{0:T(1024)S(1)}, u32[]{:S(2)}, u32[]{:S(2)}) collective-permute-start(f32[4352]{0:T(1024)S(1)} %add.84), channel_id=1, source_target_pairs={{0,16},{4,20},{8,24},{12,28},{16,0},{20,4},{24,8},{28,12},{1,17},{... | collective-permute-start | bytes 52232 | tf_op jit(solution)/shard_map/ppermute | solution.py:33
  (84 other events, 935.6 us)

commit v4 on v3

--- a/solution.py
+++ b/solution.py
@@ -878,7 +878,9 @@
     rest = middle + [far]
     blocks = relative(rest)
     q = len(blocks) // 2
-    theirs_at = at([near ^ o for o in blocks])
+    rest_out = [near] + middle[1:] + [far]
+    blocks_out = relative(rest_out)
+    theirs_at, theirs_out = at([near ^ o for o in blocks]), at([middle[0] ^ o for o in blocks_out])
 
     cot_mine, cot_theirs = mine_of(cotangent), theirs_of(cotangent)
     cot_own = jnp.concatenate([cot_mine, cot_theirs])
@@ -937,7 +939,7 @@
     n3x = x_swap(n3)
     dn_mine, *dn_split = seq(*sum_of(dn_chip, [dn_x], split=PIECES))
     dn_theirs = seq(*core_swaps(dn_split))
-    near_att = swap(att_wide, "dp", near)
+    near_att = swap(att_wide, "dp", middle[0])
     c3t, n3t, down_got = core_swaps((c3, n3, down_b))
     dr_b, dr_mine, d_qkv, d_wide, d1_a, gain_a, gain_q, gain_k, *d1_b = seq(
         *attend_back(
@@ -945,10 +947,10 @@
             gm, ga, gq, gk, w_query, w_key, w_value, w_out, cosine, sine,
         )
     )
-    near_r = few(theirs_at, dr_b, gm, block, False)
+    near_r = few(theirs_out, dr_b, gm, block, False)
     near_r, n3x, c3t, n3t, near_att, down_got = seq(near_r, n3x, c3t, n3t, near_att, down_got)
     near_d = swap(d_wide, "dp", near)
-    near_r = swap(near_r, "dp", near)
+    near_r = swap(near_r, "dp", middle[0])
     gains = jnp.concatenate([gain_a[0], gain_q[0], gain_k[0], mlp_gain[0]])
     gains_got = x_swap(gains)
     n3xt = seq(core_swap(n3x))
@@ -966,30 +968,29 @@
         return scatter_sum([a + b for a, b in zip(keep, got)], middle[1:])
 
     got = first_step(send[0]) + first_step(send[1])
-    gains = gains + seq(gains_got)
+    near_r, gains_got, *d1_b = seq(near_r, gains_got, *d1_b)
+    gains = gains + gains_got
     near_nt, gains_got, *d1_got = seq(*core_swaps((near_n, gains, *d1_b)))
     gains = gains + gains_got
     gains_got = swap(gains, "dp", near)
     (d1_chip,), (down_chip,) = sum_of(d1_a, d1_got), sum_of(down_a, [down_got])
     d1_chip, down_chip = seq(d1_chip, down_chip)
     d1_x = x_swap(d1_chip)
-    near_d, near_r, gains_got, down_chip, *got = seq(near_d, near_r, gains_got, down_chip, *got)
+    def ins(i):
+        return pair(at(blocks[i * q : (i + 1) * q]), i * q, normed1, d_qkv, near_ns, near_d, block, True)
+
+    def outs(i):
+        return pair(at(blocks_out[i * q : (i + 1) * q]), i * q, dr_b, attended, near_rs, near_att, block, False)
+
+    near_rs = [near_r, seq(core_swap(near_r))]
+    out_1 = seq(outs(1))
+    out_mid = swap(out_1, "dp", rest_out[0])
+    near_d, gains_got, near_nt = seq(near_d, gains_got, near_nt)
     gains = gains + gains_got
     near_ns = [near_n, near_nt]
+    in_1, out_mid, down_chip, *got = seq(seq(ins(1)), out_mid, down_chip, *got)
     down_x = x_swap(down_chip)
-
-    def ins(i):
-        return pair(at(blocks[i * q : (i + 1) * q]), i * q, normed1, d_qkv, near_ns, near_d, block, True)
-
-    def outs(i):
-        return pair(at(blocks[i * q : (i + 1) * q]), i * q, dr_b, attended, near_rs, near_att, block, False)
-
-    near_rt = core_swap(near_r)
-    in_1 = seq(ins(1))
     in_mid = swap(in_1, "dp", rest[0])
-    near_rs = [near_r, seq(near_rt)]
-    out_1 = seq(outs(1))
-    out_mid = swap(out_1, "dp", rest[0])
     gains_got = swap(gains, "dp", rest[0])
     in_0, out_0 = seq(ins(0), outs(0))
     summed_down = finish(keep[0], got[:h])
@@ -1004,12 +1005,16 @@
     gt_mine, *gt_split = seq(*back_of(dr_mine, d1_chip, d1_x, tok_mine, ga))
     gt_theirs = jnp.concatenate(seq(*core_swaps(gt_split)))
     grad_tokens = seq(in_order(gt_mine, gt_theirs))
-    in_mid, out_mid, gains_got, down_x, *send_up = seq(in_mid, out_mid, gains_got, down_x, *send[2])
+    in_mid, gains_got, down_x, *send_up = seq(in_mid, gains_got, down_x, *send[2])
     got_up = first_step(send_up)
     gains = gains + gains_got
     gains_got = swap(gains, "dp", far)
     both = seq(*split(in_0 + in_mid), *split(out_0 + out_mid))
-    summed_qkv, summed_out = scatter_sum(both[:q], rest[1:]), scatter_sum(both[q:], rest[1:])
+    if len(rest) == 2:
+        cut = both[3].shape[0] // 2
+        last = swap(jnp.concatenate([both[1], both[3][:cut], both[3][cut:]], axis=1), "dp", far)
+    else:
+        summed_qkv, summed_out = scatter_sum(both[:q], rest[1:]), scatter_sum(both[q:], rest_out[1:])
     down_mine, *down_split = seq(*sum_of(down_chip, [down_x], split=PIECES))
     down_theirs = seq(*core_swaps(down_split))
     down_theirs, r_theirs = jnp.concatenate(down_theirs), jnp.concatenate(r_b)
@@ -1018,7 +1023,11 @@
     for mask in rest[1:-1]:
         gains = gains + swap(gains, "dp", mask)
     if len(rest) == 2:
-        summed_qkv, summed_out, *got_up = seq(summed_qkv, summed_out, *got_up)
+        last, *got_up = seq(last, *got_up)
+        columns = both[0].shape[1]
+        summed_qkv = both[0] + last[:, :columns]
+        end = jnp.concatenate([last[:, columns : columns + block], last[:, columns + block :]])
+        summed_out = both[2] + end
     summed_up = finish(keep[2], got_up)
     nq, nk = w_query.shape[1], w_key.shape[1]
     gains = gains + 0.0 * seq.token.astype(f32)

time: 539 us -> 509 us (0.944)
  waiting for transfers between devices: 234 us -> 202 us
  other arithmetic: 20.5 us -> 26 us
    ppermute x69 -> x68, waiting for transfers between devices: 234 us -> 202 us  [swap(): return lax.ppermute(value, axis, [(i, i ^ mask) for i in range(size)])]
    ppermute x69 -> x68, starting transfers between devices: 42.8 us -> 41.9 us  [swap(): return lax.ppermute(value, axis, [(i, i ^ mask) for i in range(size)])]
  transfers between devices with their start and end apart: 69 -> 68, of which waited for: 19 -> 20; matrix products, arithmetic and copies ran while one was open for 4% -> 5% of each run, Pallas kernels for 39% -> 41%
where the time goes in v4:
time: 509 us; the launch traced here: 503 us
  Pallas kernels  218 us (43%)
  waiting for transfers between devices  202 us (40%)
  starting transfers between devices  41.9 us (8%)
  other arithmetic  26 us (5%)
  local copies, waits for them, and re-layouts  12.8 us (3%)
    ppermute x68, waiting for transfers between devices, swap(): return lax.ppermute(value, axis, [(i, i ^ mask) for i in range(size)])  202 us
    pallas_call x3, Pallas kernels, group_feed(): pl.pallas_call(functools.partial(group_kernel, len(ns), len(cs), count),...  73.9 us
    ppermute x68, starting transfers between devices, swap(): return lax.ppermute(value, axis, [(i, i ^ mask) for i in range(size)])  41.9 us
    pallas_call x1, Pallas kernels, own_feed(): pl.pallas_call(own_kernel, grid=(hidden // TILE,), in_specs=[whole((half,...  27.8 us
    pallas_call x6, Pallas kernels, sum_of(): pl.pallas_call(functools.partial(sum_kernel, len(bs)), in_specs=[whole(x....  24.8 us
    pallas_call x1, Pallas kernels, attend_back(): pl.pallas_call(functools.partial(attend_back_kernel, half), grid_spec=plt...  24.3 us
    pallas_call x4, Pallas kernels, pair_grads(): pl.pallas_call(functools.partial(pair_kernel, inward), grid_spec=pltpu.Pr...  19.8 us
    pallas_call x1, Pallas kernels, own_rest(): pl.pallas_call(rest_kernel, grid_spec=pltpu.PrefetchScalarGridSpec(num_sc...  14.7 us
  transfers between devices with their start and end apart: 68, of which 20 were waited for; matrix products, arithmetic and copies ran while one was open for 5% of the time, Pallas kernels for 41%

profile of v4, /device:TPU:0, one launch (start us, length us, event | category | flops | bytes accessed | tf_op | source)
XLA Modules:
  0.0 502.8 jit_solution(400735887248345655)
XLA Ops:
  3.3 3.1 collective-permute-start.4
  8.6 13.9 %attend.1 = (bf16[512,2048]{1,0:T(8,128)(2,1)}, f32[512,512]{1,0:T(8,128)}, f32[512,256]{1,0:T(8,128)}, bf16[512,256]{1,0:T(8,128)(2,1)}, bf16[512,512]{1,0:T(8,...) custom-call(s32[1]{0:T(128)} %bitcast.1.core_ref, ...), custom_call_target="tpu_custom_call" | custom-call | tf_op jit(solution)/shard_map/attend/pallas_call | solution.py:501
  26.5 3.7 few_of.2
  32.8 4.3 sum_of.6
  39.6 39.2 %collective-permute-done.5 = f32[128,2048]{1,0:T(8,128)} collective-permute-done((f32[128,2048]{1,0:T(8,128)S(1)}, f32[128,2048]{1,0:T(8,128)}, u32[]{:S(2)}, u32[]{:S(2)}) %collective-permute-start.5) | collective-permute-done | bytes 1048608 | tf_op jit(solution)/shard_map/ppermute | solution.py:33
  78.8 6.0 %collective-permute-done.8.c_ref = f32[128,2048]{1,0:T(8,128)S(1)} collective-permute-done((f32[128,2048]{1,0:T(8,128)}, f32[128,2048]{1,0:T(8,128)S(1)}, u32[]{:S(2)}, u32[]{:S(2)}) %collective-permute-start.8) | collective-permute-done | bytes 1048608 | tf_op jit(solution)/shard_map/ppermute | solution.py:33
  85.8 5.6 %resid_of.1 = (f32[256,2048]{1,0:T(8,128)}, f32[256,2048]{1,0:T(8,128)}, f32[128,2048]{1,0:T(8,128)}, f32[64,2048]{1,0:T(8,128)}, f32[64,2048]{1,0:T(8,128)}, /*index=5*/f32[64,2048]{1,0:T(8,128)}, f32[64,2048]{1,0:T(8,128)}) custom-call(s32[1]{0:T(128)} %bitcast.x_at_ref, bf16[256,2048]{1,0:T(8,128)(2,1)} %constant_dynamic-slice_fusion.3.a_ref.tok_ref, ...), custom_call_target="tpu_custom_call" | custom-call | tf_op jit(solution)/shard_map/resid_of/pallas_call | solution.py:349
  100.2 27.8 %own_feed.1 = (bf16[512,2048]{1,0:T(8,128)(2,1)}, bf16[512,1536]{1,0:T(8,128)(2,1)}, bf16[512,1536]{1,0:T(8,128)(2,1)}, bf16[512,1536]{1,0:T(8,128)(2,1)}, f32[2...) custom-call(f32[256,2048]{1,0:T(8,128)} %get-tuple-element.372.ra_re, ...), custom_call_target="tpu_custom_call" | custom-call | tf_op jit(solution)/shard_map/own_feed/pallas_call | solution.py:130
  128.1 14.7 %own_rest.1 = (f32[256,2048]{1,0:T(8,128)}, f32[256,2048]{1,0:T(8,128)}, f32[1536,256]{1,0:T(8,128)}, f32[1536,256]{1,0:T(8,128)}, f32[256,1536]{1,0:T(8,128)}, ...) custom-call(s32[2]{0:T(128)} %multiply_xor_fusion.1.where_ref, ...), custom_call_target="tpu_custom_call" | custom-call | tf_op jit(solution)/shard_map/own_rest/pallas_call | solution.py:219
  150.9 4.4 sum_of.7.refs_0_
  155.3 17.6 %collective-permute-done.22.refs_1_ = f32[128,2048]{1,0:T(8,128)} collective-permute-done((f32[128,2048]{1,0:T(8,128)}, f32[128,2048]{1,0:T(8,128)}, u32[]{:S(2)}, u32[]{:S(2)}) %collective-permute-start.22) | collective-permute-done | bytes 1048608 | tf_op jit(solution)/shard_map/ppermute | solution.py:33
  175.8 24.7 %group_feed.3 = (f32[1536,256]{1,0:T(8,128)}, f32[1536,256]{1,0:T(8,128)}, f32[256,1536]{1,0:T(8,128)}, f32[256,1536]{1,0:T(8,128)}, f32[256,1536]{1,0:T(8,128)}, /*index=5*/f32[256,1536]{1,0:T(8,128)}) custom-call(s32[2]{0:T(128)} %multiply_xor_fusion.1.where_ref, f32[256,2048]{1,0:T(8,128)} %collective-permute-done.9.refs_0_, ...), custom_call_target="tpu_custom_call" | custom-call | tf_op jit(solution)/shard_map/group_feed/pallas_call | solution.py:278
  200.5 24.5 %group_feed.4 = (f32[1536,256]{1,0:T(8,128)}, f32[1536,256]{1,0:T(8,128)}, f32[256,1536]{1,0:T(8,128)}, f32[256,1536]{1,0:T(8,128)}, f32[256,1536]{1,0:T(8,128)}, /*index=5*/f32[256,1536]{1,0:T(8,128)}) custom-call(s32[2]{0:T(128)} %multiply_xor_fusion.1.where_ref, f32[128,2048]{1,0:T(8,128)} %collective-permute-done.18.refs_0_, ...), custom_call_target="tpu_custom_call" | custom-call | tf_op jit(solution)/shard_map/group_feed/pallas_call | solution.py:278
  225.1 4.3 sum_of.8
  231.7 6.6 %collective-permute-done.30.refs_1_ = f32[64,2048]{1,0:T(8,128)S(1)} collective-permute-done((f32[64,2048]{1,0:T(8,128)}, f32[64,2048]{1,0:T(8,128)S(1)}, u32[]{:S(2)}, u32[]{:S(2)}) %collective-permute-start.30) | collective-permute-done | bytes 524320 | tf_op jit(solution)/shard_map/ppermute | solution.py:33
  241.6 24.3 %attend_back.1 = (bf16[512,2048]{1,0:T(8,128)(2,1)}, f32[256,2048]{1,0:T(8,128)}, bf16[512,1024]{1,0:T(8,128)(2,1)}, f32[512,1024]{1,0:T(8,128)}, f32[256,2048]{...) custom-call(s32[1]{0:T(128)} %bitcast.1.core_ref, ...), custom_call_target="tpu_custom_call" | custom-call | tf_op jit(solution)/shard_map/attend_back/pallas_call | solution.py:637
  265.9 3.2 few_of.3
  272.4 24.7 %group_feed.5 = (f32[1536,256]{1,0:T(8,128)}, f32[1536,256]{1,0:T(8,128)}, f32[256,1536]{1,0:T(8,128)}, f32[256,1536]{1,0:T(8,128)}, f32[256,1536]{1,0:T(8,128)}, /*index=5*/f32[256,1536]{1,0:T(8,128)}) custom-call(s32[2]{0:T(128)} %multiply_xor_fusion.1.where_ref, f32[128,2048]{1,0:T(8,128)} %copy-done.23, f32[128,2048]{1,0:T(8,128)} %collective-permute-done.34.refs_1_, ...), custom_call_target="tpu_custom_call" | custom-call | tf_op jit(solution)/shard_map/group_feed/pallas_call | solution.py:278
  305.9 3.7 sum_of.10.refs_0_
  309.7 3.7 sum_of.9.a_ref
  314.7 4.4 pair_grads.4
  319.7 27.6 %collective-permute-done.33.wide_ref = f32[512,1024]{1,0:T(8,128)S(1)} collective-permute-done((f32[512,1024]{1,0:T(8,128)}, f32[512,1024]{1,0:T(8,128)S(1)}, u32[]{:S(2)}, u32[]{:S(2)}) %collective-permute-start.33) | collective-permute-done | bytes 2097184 | tf_op jit(solution)/shard_map/ppermute | solution.py:33
  349.3 20.1 %collective-permute-done.48 = f32[4352]{0:T(1024)S(1)} collective-permute-done((f32[4352]{0:T(1024)S(1)}, f32[4352]{0:T(1024)S(1)}, u32[]{:S(2)}, u32[]{:S(2)}) %collective-permute-start.48) | collective-permute-done | bytes 17440 | tf_op jit(solution)/shard_map/ppermute | solution.py:33
  369.3 5.5 %pair_grads.5 = f32[512,1024]{1,0:T(8,128)} custom-call(s32[2]{0:T(128)} %broadcast_xor_fusion.1.where_ref, bf16[512,2048]{1,0:T(8,128)(2,1)} %get-tuple-element.373.a_ref, bf16[512,1024]{1,0:T(8,128)(2,1)} %get-tuple-element.505.b_ref, f32[256,1024]{1,0:T(8,128)} %copy-done.12, f32[256,1024]{1,0:T(8,128)} %collective-permute-done.42.few_b_ref, ...), custom_call_target="tpu_custom_call" | custom-call | tf_op jit(solution)/shard_map/pair_grads/pallas_call | solution.py:761
  377.1 4.3 pair_grads.7
  381.3 5.6 %pair_grads.6 = f32[512,1024]{1,0:T(8,128)} custom-call(s32[2]{0:T(128)} %multiply_xor_fusion.where_ref, bf16[512,2048]{1,0:T(8,128)(2,1)} %get-tuple-element.373.a_ref, bf16[512,1024]{1,0:T(8,128)(2,1)} %get-tuple-element.505.b_ref, f32[256,1024]{1,0:T(8,128)} %copy-done.12, f32[256,1024]{1,0:T(8,128)} %collective-permute-done.42.few_b_ref, ...), custom_call_target="tpu_custom_call" | custom-call | tf_op jit(solution)/shard_map/pair_grads/pallas_call | solution.py:761
  386.9 3.3 add.79
  393.0 6.1 %back_of.1 = (f32[256,2048]{1,0:T(8,128)}, f32[64,2048]{1,0:T(8,128)}, f32[64,2048]{1,0:T(8,128)}, f32[64,2048]{1,0:T(8,128)}, f32[64,2048]{1,0:T(8,128)}) custom-call(f32[256,2048]{1,0:T(8,128)} %get-tuple-element.577.dr_ref, f32[256,2048]{1,0:T(8,128)} %sum_of.9.a_ref, f32[256,2048]{1,0:T(8,128)} %collective-permute-done.56.b_ref, ...), custom_call_target="tpu_custom_call" | custom-call | tf_op jit(solution)/shard_map/back_of/pallas_call | solution.py:695
  405.1 17.4 %collective-permute-done.54 = f32[4352]{0:T(1024)S(1)} collective-permute-done((f32[4352]{0:T(1024)S(1)}, f32[4352]{0:T(1024)S(1)}, u32[]{:S(2)}, u32[]{:S(2)}) %collective-permute-start.54) | collective-permute-done | bytes 17440 | tf_op jit(solution)/shard_map/ppermute | solution.py:33
  427.9 4.3 sum_of.11
  438.2 56.5 %collective-permute-done.66 = f32[256,1536]{1,0:T(8,128)S(1)} collective-permute-done((f32[256,1536]{1,0:T(8,128)}, f32[256,1536]{1,0:T(8,128)S(1)}, u32[]{:S(2)}, u32[]{:S(2)}) %collective-permute-start.66) | collective-permute-done | bytes 1572896 | tf_op jit(solution)/shard_map/ppermute | solution.py:33
  498.7 2.8 add.91
  (276 shorter events, 82.3 us)
Async XLA Ops:
  3.3 81.5 %collective-permute-start.4 = (f32[256,2048]{1,0:T(8,128)S(1)}, f32[256,2048]{1,0:T(8,128)}, u32[]{:S(2)}, u32[]{:S(2)}) collective-permute-start(f32[256,2048]{1,0:T(8,128)S(1)} %get-tuple-element.340), channel_id=1, source_target_pairs={{0,4},{4,0},{8,12},{12,8},{16,20},{20,16},{24,28},{28,24},{1,5},{5... | collective-permute-start | bytes 6291464 | tf_op jit(solution)/shard_map/ppermute | solution.py:33
  30.2 48.6 %collective-permute-start.5 = (f32[128,2048]{1,0:T(8,128)S(1)}, f32[128,2048]{1,0:T(8,128)}, u32[]{:S(2)}, u32[]{:S(2)}) collective-permute-start(f32[128,2048]{1,0:T(8,128)S(1)} %constant_dynamic-slice_fusion.1), channel_id=1, source_target_pairs={{0,16},{4,20},{8,24},{12,28},{16,0},{20,4},{24,8},{28,12},{1,17},{... | collective-permute-start | bytes 3145736 | tf_op jit(solution)/shard_map/ppermute | solution.py:33
  37.1 41.7 %collective-permute-start.6 = (f32[256,1024]{1,0:T(8,128)}, f32[256,1024]{1,0:T(8,128)S(1)}, u32[]{:S(2)}, u32[]{:S(2)}) collective-permute-start(f32[256,1024]{1,0:T(8,128)} %few_of.2), channel_id=1, source_target_pairs={{0,4},{4,0},{8,12},{12,8},{16,20},{20,16},{24,28},{28,24},{1,5},{5... | collective-permute-start | bytes 3145736 | tf_op jit(solution)/shard_map/ppermute | solution.py:33
  37.6 41.2 %collective-permute-start.7 = (f32[128,2048]{1,0:T(8,128)}, f32[128,2048]{1,0:T(8,128)S(1)}, u32[]{:S(2)}, u32[]{:S(2)}) collective-permute-start(f32[128,2048]{1,0:T(8,128)} %get-tuple-element.359), channel_id=1, source_target_pairs={{0,2},{1,3},{2,0},{3,1},{4,6},{5,7},{6,4},{7,5},{8,10},{9,11},{10,... | collective-permute-start | bytes 3145736 | tf_op jit(solution)/shard_map/ppermute | solution.py:33
  39.1 45.8 %collective-permute-start.8 = (f32[128,2048]{1,0:T(8,128)}, f32[128,2048]{1,0:T(8,128)S(1)}, u32[]{:S(2)}, u32[]{:S(2)}) collective-permute-start(f32[128,2048]{1,0:T(8,128)} %get-tuple-element.360), channel_id=1, source_target_pairs={{0,2},{1,3},{2,0},{3,1},{4,6},{5,7},{6,4},{7,5},{8,10},{9,11},{10,... | collective-permute-start | bytes 3145736 | tf_op jit(solution)/shard_map/ppermute | solution.py:33
  91.5 55.6 %collective-permute-start.9 = (f32[256,2048]{1,0:T(8,128)}, f32[256,2048]{1,0:T(8,128)}, u32[]{:S(2)}, u32[]{:S(2)}) collective-permute-start(f32[256,2048]{1,0:T(8,128)} %get-tuple-element.374), channel_id=1, source_target_pairs={{0,4},{4,0},{8,12},{12,8},{16,20},{20,16},{24,28},{28,24},{1,5},{5... | collective-permute-start | bytes 6291464 | tf_op jit(solution)/shard_map/ppermute | solution.py:33
  93.5 49.9 %collective-permute-start.18 = (f32[128,2048]{1,0:T(8,128)}, f32[128,2048]{1,0:T(8,128)}, u32[]{:S(2)}, u32[]{:S(2)}) collective-permute-start(f32[128,2048]{1,0:T(8,128)} %get-tuple-element.416), channel_id=1, source_target_pairs={{0,16},{4,20},{8,24},{12,28},{16,0},{20,4},{24,8},{28,12},{1,17},{... | collective-permute-start | bytes 3145736 | tf_op jit(solution)/shard_map/ppermute | solution.py:33
  93.9 49.7 %collective-permute-start.19 = (f32[128,2048]{1,0:T(8,128)}, f32[128,2048]{1,0:T(8,128)}, u32[]{:S(2)}, u32[]{:S(2)}) collective-permute-start(f32[128,2048]{1,0:T(8,128)} %collective-permute-done.5), channel_id=1, source_target_pairs={{0,2},{1,3},{2,0},{3,1},{4,6},{5,7},{6,4},{7,5},{8,10},{9,11},{10,... | collective-permute-start | bytes 3145736 | tf_op jit(solution)/shard_map/ppermute | solution.py:33
  144.8 29.0 %collective-permute-start.21 = (f32[256,2048]{1,0:T(8,128)}, f32[256,2048]{1,0:T(8,128)}, u32[]{:S(2)}, u32[]{:S(2)}) collective-permute-start(f32[256,2048]{1,0:T(8,128)} %collective-permute-done.4.refs_2_), channel_id=1, source_target_pairs={{0,1},{1,0},{2,3},{3,2},{4,5},{5,4},{6,7},{7,6},{8,9},{9,8},{10,11... | collective-permute-start | bytes 6291464 | tf_op jit(solution)/shard_map/ppermute | solution.py:33
  147.0 26.8 %collective-permute-start.20 = (f32[256,2048]{1,0:T(8,128)}, f32[256,2048]{1,0:T(8,128)}, u32[]{:S(2)}, u32[]{:S(2)}) collective-permute-start(f32[256,2048]{1,0:T(8,128)} %collective-permute-done.9.refs_0_), channel_id=1, source_target_pairs={{0,1},{1,0},{2,3},{3,2},{4,5},{5,4},{6,7},{7,6},{8,9},{9,8},{10,11... | collective-permute-start | bytes 6291464 | tf_op jit(solution)/shard_map/ppermute | solution.py:33
  147.2 25.7 %collective-permute-start.22 = (f32[128,2048]{1,0:T(8,128)}, f32[128,2048]{1,0:T(8,128)}, u32[]{:S(2)}, u32[]{:S(2)}) collective-permute-start(f32[128,2048]{1,0:T(8,128)} %collective-permute-done.18.refs_0_), channel_id=1, source_target_pairs={{0,2},{1,3},{2,0},{3,1},{4,6},{5,7},{6,4},{7,5},{8,10},{9,11},{10,... | collective-permute-start | bytes 3145736 | tf_op jit(solution)/shard_map/ppermute | solution.py:33
  173.8 26.7 %collective-permute-start.27 = (f32[256,2048]{1,0:T(8,128)S(1)}, f32[256,2048]{1,0:T(8,128)}, u32[]{:S(2)}, u32[]{:S(2)}) collective-permute-start(f32[256,2048]{1,0:T(8,128)S(1)} %pad_maximum_fusion.1.refs_4_), channel_id=1, source_target_pairs={{0,1},{1,0},{2,3},{3,2},{4,5},{5,4},{6,7},{7,6},{8,9},{9,8},{10,11... | collective-permute-start | bytes 6291464 | tf_op jit(solution)/shard_map/ppermute | solution.py:33
  173.9 51.1 %collective-permute-start.24 = (f32[256,2048]{1,0:T(8,128)}, f32[256,2048]{1,0:T(8,128)}, u32[]{:S(2)}, u32[]{:S(2)}) collective-permute-start(f32[256,2048]{1,0:T(8,128)} %sum_of.7.refs_0_), channel_id=1, source_target_pairs={{0,2},{1,3},{2,0},{3,1},{4,6},{5,7},{6,4},{7,5},{8,10},{9,11},{10,... | collective-permute-start | bytes 6291464 | tf_op jit(solution)/shard_map/ppermute | solution.py:33
  174.8 50.2 %collective-permute-start.25 = (f32[256,2048]{1,0:T(8,128)S(1)}, f32[256,2048]{1,0:T(8,128)}, u32[]{:S(2)}, u32[]{:S(2)}) collective-permute-start(f32[256,2048]{1,0:T(8,128)S(1)} %pad_maximum_fusion.1.refs_4_), channel_id=1, source_target_pairs={{0,4},{4,0},{8,12},{12,8},{16,20},{20,16},{24,28},{28,24},{1,5},{5... | collective-permute-start | bytes 6291464 | tf_op jit(solution)/shard_map/ppermute | solution.py:33
  229.4 39.8 %collective-permute-start.38 = (f32[256,2048]{1,0:T(8,128)}, f32[256,2048]{1,0:T(8,128)}, u32[]{:S(2)}, u32[]{:S(2)}) collective-permute-start(f32[256,2048]{1,0:T(8,128)} %get-tuple-element.516), channel_id=1, source_target_pairs={{0,1},{1,0},{2,3},{3,2},{4,5},{5,4},{6,7},{7,6},{8,9},{9,8},{10,11... | collective-permute-start | bytes 6291464 | tf_op jit(solution)/shard_map/ppermute | solution.py:33
  229.9 39.3 %collective-permute-start.35 = (f32[256,2048]{1,0:T(8,128)}, f32[256,2048]{1,0:T(8,128)}, u32[]{:S(2)}, u32[]{:S(2)}) collective-permute-start(f32[256,2048]{1,0:T(8,128)} %collective-permute-done.25.refs_4_), channel_id=1, source_target_pairs={{0,1},{1,0},{2,3},{3,2},{4,5},{5,4},{6,7},{7,6},{8,9},{9,8},{10,11... | collective-permute-start | bytes 6291464 | tf_op jit(solution)/shard_map/ppermute | solution.py:33
  238.3 30.9 %collective-permute-start.37 = (f32[512,512]{1,0:T(8,128)}, f32[512,512]{1,0:T(8,128)S(1)}, u32[]{:S(2)}, u32[]{:S(2)}) collective-permute-start(f32[512,512]{1,0:T(8,128)} %get-tuple-element.515), channel_id=1, source_target_pairs={{0,8},{4,12},{8,0},{12,4},{16,24},{20,28},{24,16},{28,20},{1,9},{5... | collective-permute-start | bytes 3145736 | tf_op jit(solution)/shard_map/ppermute | solution.py:33
  239.9 29.3 %collective-permute-start.34 = (f32[128,2048]{1,0:T(8,128)S(1)}, f32[128,2048]{1,0:T(8,128)}, u32[]{:S(2)}, u32[]{:S(2)}) collective-permute-start(f32[128,2048]{1,0:T(8,128)S(1)} %collective-permute-done.23.refs_0_), channel_id=1, source_target_pairs={{0,2},{1,3},{2,0},{3,1},{4,6},{5,7},{6,4},{7,5},{8,10},{9,11},{10,... | collective-permute-start | bytes 3145736 | tf_op jit(solution)/shard_map/ppermute | solution.py:33
  241.1 28.1 %collective-permute-start.36 = (f32[128,2048]{1,0:T(8,128)S(1)}, f32[128,2048]{1,0:T(8,128)}, u32[]{:S(2)}, u32[]{:S(2)}) collective-permute-start(f32[128,2048]{1,0:T(8,128)S(1)} %collective-permute-done.23.refs_0_), channel_id=1, source_target_pairs={{0,1},{1,0},{2,3},{3,2},{4,5},{5,4},{6,7},{7,6},{8,9},{9,8},{10,11... | collective-permute-start | bytes 3145736 | tf_op jit(solution)/shard_map/ppermute | solution.py:33
  269.8 27.4 %collective-permute-start.39 = (f32[256,1024]{1,0:T(8,128)}, f32[256,1024]{1,0:T(8,128)S(1)}, u32[]{:S(2)}, u32[]{:S(2)}) collective-permute-start(f32[256,1024]{1,0:T(8,128)} %few_of.3), channel_id=1, source_target_pairs={{0,8},{4,12},{8,0},{12,4},{16,24},{20,28},{24,16},{28,20},{1,9},{5... | collective-permute-start | bytes 3145736 | tf_op jit(solution)/shard_map/ppermute | solution.py:33
  270.5 30.1 %collective-permute-start.42 = (f32[256,1024]{1,0:T(8,128)S(1)}, f32[256,1024]{1,0:T(8,128)}, u32[]{:S(2)}, u32[]{:S(2)}) collective-permute-start(f32[256,1024]{1,0:T(8,128)S(1)} %copy-done.13), channel_id=1, source_target_pairs={{0,1},{1,0},{2,3},{3,2},{4,5},{5,4},{6,7},{7,6},{8,9},{9,8},{10,11... | collective-permute-start | bytes 3145736 | tf_op jit(solution)/shard_map/ppermute | solution.py:33
  270.5 26.6 %collective-permute-start.40 = (f32[4352]{0:T(1024)S(1)}, f32[4352]{0:T(1024)S(1)}, u32[]{:S(2)}, u32[]{:S(2)}) collective-permute-start(f32[4352]{0:T(1024)S(1)} %pad_maximum_fusion.4), channel_id=1, source_target_pairs={{0,2},{1,3},{2,0},{3,1},{4,6},{5,7},{6,4},{7,5},{8,10},{9,11},{10,... | collective-permute-start | bytes 52232 | tf_op jit(solution)/shard_map/ppermute | solution.py:33
  298.6 48.7 %collective-permute-start.33 = (f32[512,1024]{1,0:T(8,128)}, f32[512,1024]{1,0:T(8,128)S(1)}, u32[]{:S(2)}, u32[]{:S(2)}) collective-permute-start(f32[512,1024]{1,0:T(8,128)} %get-tuple-element.507), channel_id=1, source_target_pairs={{0,4},{4,0},{8,12},{12,8},{16,20},{20,16},{24,28},{28,24},{1,5},{5... | collective-permute-start | bytes 6291464 | tf_op jit(solution)/shard_map/ppermute | solution.py:33
  303.9 71.0 %collective-permute-start.51 = (f32[1536,256]{1,0:T(8,128)}, f32[1536,256]{1,0:T(8,128)}, u32[]{:S(2)}, u32[]{:S(2)}) collective-permute-start(f32[1536,256]{1,0:T(8,128)} %get-tuple-element.570), channel_id=1, source_target_pairs={{0,8},{4,12},{8,0},{12,4},{16,24},{20,28},{24,16},{28,20},{1,9},{5... | collective-permute-start | bytes 4718600 | tf_op jit(solution)/shard_map/ppermute | solution.py:33
  304.6 70.2 %collective-permute-start.52 = (f32[256,1536]{1,0:T(8,128)}, f32[256,1536]{1,0:T(8,128)}, u32[]{:S(2)}, u32[]{:S(2)}) collective-permute-start(f32[256,1536]{1,0:T(8,128)} %get-tuple-element.571), channel_id=1, source_target_pairs={{0,8},{4,12},{8,0},{12,4},{16,24},{20,28},{24,16},{28,20},{1,9},{5... | collective-permute-start | bytes 4718600 | tf_op jit(solution)/shard_map/ppermute | solution.py:33
  313.3 79.7 %collective-permute-start.56 = (f32[256,2048]{1,0:T(8,128)}, f32[256,2048]{1,0:T(8,128)}, u32[]{:S(2)}, u32[]{:S(2)}) collective-permute-start(f32[256,2048]{1,0:T(8,128)} %sum_of.9.a_ref), channel_id=1, source_target_pairs={{0,2},{1,3},{2,0},{3,1},{4,6},{5,7},{6,4},{7,5},{8,10},{9,11},{10,... | collective-permute-start | bytes 6291464 | tf_op jit(solution)/shard_map/ppermute | solution.py:33
  319.1 55.8 %collective-permute-start.50 = (f32[1024,256]{1,0:T(8,128)}, f32[1024,256]{1,0:T(8,128)S(1)}, u32[]{:S(2)}, u32[]{:S(2)}) collective-permute-start(f32[1024,256]{1,0:T(8,128)} %pair_grads.4), channel_id=1, source_target_pairs={{0,4},{4,0},{8,12},{12,8},{16,20},{20,16},{24,28},{28,24},{1,5},{5... | collective-permute-start | bytes 3145736 | tf_op jit(solution)/shard_map/ppermute | solution.py:33
  374.9 47.6 %collective-permute-start.53 = (f32[512,1024]{1,0:T(8,128)}, f32[512,1024]{1,0:T(8,128)S(1)}, u32[]{:S(2)}, u32[]{:S(2)}) collective-permute-start(f32[512,1024]{1,0:T(8,128)} %pair_grads.5), channel_id=1, source_target_pairs={{0,8},{4,12},{8,0},{12,4},{16,24},{20,28},{24,16},{28,20},{1,9},{5... | collective-permute-start | bytes 6291464 | tf_op jit(solution)/shard_map/ppermute | solution.py:33
  375.7 47.0 %collective-permute-start.55 = (f32[256,2048]{1,0:T(8,128)}, f32[256,2048]{1,0:T(8,128)}, u32[]{:S(2)}, u32[]{:S(2)}) collective-permute-start(f32[256,2048]{1,0:T(8,128)} %sum_of.10.refs_0_), channel_id=1, source_target_pairs={{0,2},{1,3},{2,0},{3,1},{4,6},{5,7},{6,4},{7,5},{8,10},{9,11},{10,... | collective-permute-start | bytes 6291464 | tf_op jit(solution)/shard_map/ppermute | solution.py:33
  424.5 70.1 %collective-permute-start.66 = (f32[256,1536]{1,0:T(8,128)}, f32[256,1536]{1,0:T(8,128)S(1)}, u32[]{:S(2)}, u32[]{:S(2)}) collective-permute-start(f32[256,1536]{1,0:T(8,128)} %pad_maximum_fusion.2), channel_id=1, source_target_pairs={{0,16},{4,20},{8,24},{12,28},{16,0},{20,4},{24,8},{28,12},{1,17},{... | collective-permute-start | bytes 4718600 | tf_op jit(solution)/shard_map/ppermute | solution.py:33
  426.8 68.3 %collective-permute-start.67 = (f32[256,1536]{1,0:T(8,128)}, f32[256,1536]{1,0:T(8,128)}, u32[]{:S(2)}, u32[]{:S(2)}) collective-permute-start(f32[256,1536]{1,0:T(8,128)} %get-tuple-element.633), channel_id=1, source_target_pairs={{0,8},{4,12},{8,0},{12,4},{16,24},{20,28},{24,16},{28,20},{1,9},{5... | collective-permute-start | bytes 4718600 | tf_op jit(solution)/shard_map/ppermute | solution.py:33
  436.9 60.6 %collective-permute-start.65 = (f32[4352]{0:T(1024)S(1)}, f32[4352]{0:T(1024)S(1)}, u32[]{:S(2)}, u32[]{:S(2)}) collective-permute-start(f32[4352]{0:T(1024)S(1)} %add.84), channel_id=1, source_target_pairs={{0,16},{4,20},{8,24},{12,28},{16,0},{20,4},{24,8},{28,12},{1,17},{... | collective-permute-start | bytes 52232 | tf_op jit(solution)/shard_map/ppermute | solution.py:33
  (88 other events, 777.0 us)

commit v5 on v4

--- a/solution.py
+++ b/solution.py
@@ -895,8 +895,7 @@
     mixed_got = seq(*core_swaps(mixed_b))
     mixed_chip, *mixed_split = seq(*sum_of(mixed_a, mixed_got, split=2))
     mixed_x = [x_swap(p) for p in mixed_split]
-    near_n = swap(seq(few(theirs_at, tok_mine, ga, block, True)), "dp", near)
-    c1, c2, near_n, *mixed_x = seq(c1, c2, near_n, *mixed_x)
+    c1, c2, *mixed_x = seq(c1, c2, *mixed_x)
 
     r_a, n0, n0_quarter, *r_split = seq(*resid_of(x_at, tok_mine, mixed_chip, *mixed_x))
     n1 = swap(n0, "dp", near)
@@ -920,8 +919,9 @@
     (dn_chip,) = sum_of(dn_a, dn_got)
     c2 = jnp.concatenate([c2, c2x])
     dn_chip, c2 = seq(dn_chip, c2)
-    n1t, c1t = core_swaps((n1, c1))
-    n1t, c1t, n2x, n3, dn_chip, c2 = seq(n1t, c1t, n2x, n3, dn_chip, c2)
+    near_n = few(theirs_at, seq(tok_mine), ga, block, True)
+    n1t, c1t, down_got = core_swaps((n1, c1, down_b))
+    n1t, c1t, down_got, n2x, n3, dn_chip, c2, near_n = seq(n1t, c1t, down_got, n2x, n3, dn_chip, c2, near_n)
     dn_x = x_swap(dn_chip)
     c3 = swap(c2, "dp", near)
 
@@ -938,9 +938,10 @@
 
     n3x = x_swap(n3)
     dn_mine, *dn_split = seq(*sum_of(dn_chip, [dn_x], split=PIECES))
-    dn_theirs = seq(*core_swaps(dn_split))
+    *dn_theirs, c3, n3, near_n, att_wide = seq(*core_swaps(dn_split), c3, n3, near_n, att_wide)
+    near_n = swap(near_n, "dp", near)
     near_att = swap(att_wide, "dp", middle[0])
-    c3t, n3t, down_got = core_swaps((c3, n3, down_b))
+    c3t, n3t = core_swaps((c3, n3))
     dr_b, dr_mine, d_qkv, d_wide, d1_a, gain_a, gain_q, gain_k, *d1_b = seq(
         *attend_back(
             core_at, dn_mine, dn_theirs, r_a, r_b, cot_own, tokens, query, keys, values, attended,
@@ -948,7 +949,7 @@
         )
     )
     near_r = few(theirs_out, dr_b, gm, block, False)
-    near_r, n3x, c3t, n3t, near_att, down_got = seq(near_r, n3x, c3t, n3t, near_att, down_got)
+    near_r, n3x, c3t, n3t, near_att, near_n = seq(near_r, n3x, c3t, n3t, near_att, near_n)
     near_d = swap(d_wide, "dp", near)
     near_r = swap(near_r, "dp", middle[0])
     gains = jnp.concatenate([gain_a[0], gain_q[0], gain_k[0], mlp_gain[0]])

time: 509 us -> 511 us (level)
  waiting for transfers between devices: 202 us -> 190 us
  Pallas kernels: 218 us -> 227 us
    ppermute x68, waiting for transfers between devices: 202 us -> 190 us  [swap(): return lax.ppermute(value, axis, [(i, i ^ mask) for i in range(size)])]
    pallas_call x1, Pallas kernels: 14.7 us -> 25.2 us  [own_rest(): pl.pallas_call(rest_kernel, grid_spec=pltpu.PrefetchScalarGridSpec(num_sc...]
  transfers between devices with their start and end apart: 68 -> 68, of which waited for: 20 -> 23; matrix products, arithmetic and copies ran while one was open for 5% -> 5% of each run, Pallas kernels for 41% -> 43%
where the time goes in v5:
time: 511 us; the launch traced here: 507 us
  Pallas kernels  227 us (44%)
  waiting for transfers between devices  190 us (37%)
  starting transfers between devices  45.5 us (9%)
  other arithmetic  26 us (5%)
  local copies, waits for them, and re-layouts  15.8 us (3%)
    ppermute x68, waiting for transfers between devices, swap(): return lax.ppermute(value, axis, [(i, i ^ mask) for i in range(size)])  190 us
    pallas_call x3, Pallas kernels, group_feed(): pl.pallas_call(functools.partial(group_kernel, len(ns), len(cs), count),...  73.6 us
    ppermute x68, starting transfers between devices, swap(): return lax.ppermute(value, axis, [(i, i ^ mask) for i in range(size)])  45.5 us
    pallas_call x1, Pallas kernels, own_feed(): pl.pallas_call(own_kernel, grid=(hidden // TILE,), in_specs=[whole((half,...  27.3 us
    pallas_call x1, Pallas kernels, own_rest(): pl.pallas_call(rest_kernel, grid_spec=pltpu.PrefetchScalarGridSpec(num_sc...  25.2 us
    pallas_call x1, Pallas kernels, attend_back(): pl.pallas_call(functools.partial(attend_back_kernel, half), grid_spec=plt...  24.5 us
    pallas_call x6, Pallas kernels, sum_of(): pl.pallas_call(functools.partial(sum_kernel, len(bs)), in_specs=[whole(x....  24.1 us
    pallas_call x4, Pallas kernels, pair_grads(): pl.pallas_call(functools.partial(pair_kernel, inward), grid_spec=pltpu.Pr...  19.8 us
  transfers between devices with their start and end apart: 68, of which 23 were waited for; matrix products, arithmetic and copies ran while one was open for 5% of the time, Pallas kernels for 43%

profile of v5, /device:TPU:0, one launch (start us, length us, event | category | flops | bytes accessed | tf_op | source)
XLA Modules:
  0.0 506.8 jit_solution(6485726652511376762)
XLA Ops:
  3.3 3.1 collective-permute-start.4
  8.6 13.9 %attend.1 = (bf16[512,2048]{1,0:T(8,128)(2,1)}, f32[512,512]{1,0:T(8,128)}, f32[512,256]{1,0:T(8,128)}, bf16[512,256]{1,0:T(8,128)(2,1)}, bf16[512,512]{1,0:T(8,...) custom-call(s32[1]{0:T(128)} %bitcast.1.core_ref, ...), custom_call_target="tpu_custom_call" | custom-call | tf_op jit(solution)/shard_map/attend/pallas_call | solution.py:501
  27.3 4.3 sum_of.6
  36.0 37.4 %collective-permute-done.5 = f32[128,2048]{1,0:T(8,128)} collective-permute-done((f32[128,2048]{1,0:T(8,128)S(1)}, f32[128,2048]{1,0:T(8,128)}, u32[]{:S(2)}, u32[]{:S(2)}) %collective-permute-start.5) | collective-permute-done | bytes 1048608 | tf_op jit(solution)/shard_map/ppermute | solution.py:33
  73.4 5.9 %collective-permute-done.7.c_ref = f32[128,2048]{1,0:T(8,128)S(1)} collective-permute-done((f32[128,2048]{1,0:T(8,128)}, f32[128,2048]{1,0:T(8,128)S(1)}, u32[]{:S(2)}, u32[]{:S(2)}) %collective-permute-start.7) | collective-permute-done | bytes 1048608 | tf_op jit(solution)/shard_map/ppermute | solution.py:33
  80.3 5.6 %resid_of.1 = (f32[256,2048]{1,0:T(8,128)}, f32[256,2048]{1,0:T(8,128)}, f32[128,2048]{1,0:T(8,128)}, f32[64,2048]{1,0:T(8,128)}, f32[64,2048]{1,0:T(8,128)}, /*index=5*/f32[64,2048]{1,0:T(8,128)}, f32[64,2048]{1,0:T(8,128)}) custom-call(s32[1]{0:T(128)} %bitcast.x_at_ref, bf16[256,2048]{1,0:T(8,128)(2,1)} %constant_dynamic-slice_fusion.3.tok_ref.a_ref, ...), custom_call_target="tpu_custom_call" | custom-call | tf_op jit(solution)/shard_map/resid_of/pallas_call | solution.py:349
  95.9 27.3 %own_feed.1 = (bf16[512,2048]{1,0:T(8,128)(2,1)}, bf16[512,1536]{1,0:T(8,128)(2,1)}, bf16[512,1536]{1,0:T(8,128)(2,1)}, bf16[512,1536]{1,0:T(8,128)(2,1)}, f32[2...) custom-call(f32[256,2048]{1,0:T(8,128)} %get-tuple-element.375.ra_re, ...), custom_call_target="tpu_custom_call" | custom-call | tf_op jit(solution)/shard_map/own_feed/pallas_call | solution.py:130
  123.3 25.2 %own_rest.1 = (f32[256,2048]{1,0:T(8,128)}, f32[256,2048]{1,0:T(8,128)}, f32[1536,256]{1,0:T(8,128)}, f32[1536,256]{1,0:T(8,128)}, f32[256,1536]{1,0:T(8,128)}, ...) custom-call(s32[2]{0:T(128)} %multiply_xor_fusion.1.where_ref, ...), custom_call_target="tpu_custom_call" | custom-call | tf_op jit(solution)/shard_map/own_rest/pallas_call | solution.py:219
  155.7 3.1 pad_maximum_fusion.1.refs_4_
  158.8 3.7 sum_of.7.refs_0_
  162.4 3.8 few_of.2
  166.3 12.4 %collective-permute-done.22.refs_1_ = f32[128,2048]{1,0:T(8,128)S(1)} collective-permute-done((f32[128,2048]{1,0:T(8,128)}, f32[128,2048]{1,0:T(8,128)S(1)}, u32[]{:S(2)}, u32[]{:S(2)}) %collective-permute-start.22) | collective-permute-done | bytes 1048608 | tf_op jit(solution)/shard_map/ppermute | solution.py:33
  182.7 24.5 %group_feed.3 = (f32[1536,256]{1,0:T(8,128)}, f32[1536,256]{1,0:T(8,128)}, f32[256,1536]{1,0:T(8,128)}, f32[256,1536]{1,0:T(8,128)}, f32[256,1536]{1,0:T(8,128)}, /*index=5*/f32[256,1536]{1,0:T(8,128)}) custom-call(s32[2]{0:T(128)} %multiply_xor_fusion.1.where_ref, f32[256,2048]{1,0:T(8,128)} %collective-permute-done.8.refs_0_, ...), custom_call_target="tpu_custom_call" | custom-call | tf_op jit(solution)/shard_map/group_feed/pallas_call | solution.py:278
  207.3 24.5 %group_feed.4 = (f32[1536,256]{1,0:T(8,128)}, f32[1536,256]{1,0:T(8,128)}, f32[256,1536]{1,0:T(8,128)}, f32[256,1536]{1,0:T(8,128)}, f32[256,1536]{1,0:T(8,128)}, /*index=5*/f32[256,1536]{1,0:T(8,128)}) custom-call(s32[2]{0:T(128)} %multiply_xor_fusion.1.where_ref, f32[128,2048]{1,0:T(8,128)} %collective-permute-done.17.refs_0_, f32[128,2048]{1,0:T(8,128)} %copy-done.25, ...), custom_call_target="tpu_custom_call" | custom-call | tf_op jit(solution)/shard_map/group_feed/pallas_call | solution.py:278
  231.8 4.3 sum_of.8
  243.9 24.5 %attend_back.1 = (bf16[512,2048]{1,0:T(8,128)(2,1)}, f32[256,2048]{1,0:T(8,128)}, bf16[512,1024]{1,0:T(8,128)(2,1)}, f32[512,1024]{1,0:T(8,128)}, f32[256,2048]{...) custom-call(s32[1]{0:T(128)} %bitcast.1.core_ref, ...), custom_call_target="tpu_custom_call" | custom-call | tf_op jit(solution)/shard_map/attend_back/pallas_call | solution.py:637
  268.4 3.2 few_of.3
  275.6 24.6 %group_feed.5 = (f32[1536,256]{1,0:T(8,128)}, f32[1536,256]{1,0:T(8,128)}, f32[256,1536]{1,0:T(8,128)}, f32[256,1536]{1,0:T(8,128)}, f32[256,1536]{1,0:T(8,128)}, /*index=5*/f32[256,1536]{1,0:T(8,128)}) custom-call(s32[2]{0:T(128)} %multiply_xor_fusion.1.where_ref, f32[128,2048]{1,0:T(8,128)} %collective-permute-done.23.refs_0_, ...), custom_call_target="tpu_custom_call" | custom-call | tf_op jit(solution)/shard_map/group_feed/pallas_call | solution.py:278
  309.5 3.8 sum_of.10.refs_0_
  313.3 3.7 sum_of.9.a_ref
  319.0 4.4 pair_grads.4
  324.0 26.1 %collective-permute-done.38.wide_ref = f32[512,1024]{1,0:T(8,128)S(1)} collective-permute-done((f32[512,1024]{1,0:T(8,128)}, f32[512,1024]{1,0:T(8,128)S(1)}, u32[]{:S(2)}, u32[]{:S(2)}) %collective-permute-start.38) | collective-permute-done | bytes 2097184 | tf_op jit(solution)/shard_map/ppermute | solution.py:33
  352.1 20.3 %collective-permute-done.48 = f32[4352]{0:T(1024)S(1)} collective-permute-done((f32[4352]{0:T(1024)S(1)}, f32[4352]{0:T(1024)S(1)}, u32[]{:S(2)}, u32[]{:S(2)}) %collective-permute-start.48) | collective-permute-done | bytes 17440 | tf_op jit(solution)/shard_map/ppermute | solution.py:33
  372.4 5.5 %pair_grads.5 = f32[512,1024]{1,0:T(8,128)} custom-call(s32[2]{0:T(128)} %broadcast_xor_fusion.3.where_ref, bf16[512,2048]{1,0:T(8,128)(2,1)} %get-tuple-element.376.a_ref, bf16[512,1024]{1,0:T(8,128)(2,1)} %get-tuple-element.515.b_ref, f32[256,1024]{1,0:T(8,128)} %copy-done.12, f32[256,1024]{1,0:T(8,128)} %collective-permute-done.42.few_b_ref, ...), custom_call_target="tpu_custom_call" | custom-call | tf_op jit(solution)/shard_map/pair_grads/pallas_call | solution.py:761
  381.5 4.3 pair_grads.7
  385.8 5.6 %pair_grads.6 = f32[512,1024]{1,0:T(8,128)} custom-call(s32[2]{0:T(128)} %multiply_xor_fusion.where_ref, bf16[512,2048]{1,0:T(8,128)(2,1)} %get-tuple-element.376.a_ref, bf16[512,1024]{1,0:T(8,128)(2,1)} %get-tuple-element.515.b_ref, f32[256,1024]{1,0:T(8,128)} %copy-done.12, f32[256,1024]{1,0:T(8,128)} %collective-permute-done.42.few_b_ref, ...), custom_call_target="tpu_custom_call" | custom-call | tf_op jit(solution)/shard_map/pair_grads/pallas_call | solution.py:761
  391.4 3.4 add.79
  396.1 6.1 %back_of.1 = (f32[256,2048]{1,0:T(8,128)}, f32[64,2048]{1,0:T(8,128)}, f32[64,2048]{1,0:T(8,128)}, f32[64,2048]{1,0:T(8,128)}, f32[64,2048]{1,0:T(8,128)}) custom-call(f32[256,2048]{1,0:T(8,128)} %get-tuple-element.587.dr_ref, f32[256,2048]{1,0:T(8,128)} %sum_of.9.a_ref, f32[256,2048]{1,0:T(8,128)} %collective-permute-done.56.b_ref, ...), custom_call_target="tpu_custom_call" | custom-call | tf_op jit(solution)/shard_map/back_of/pallas_call | solution.py:695
  408.5 18.3 %collective-permute-done.54 = f32[4352]{0:T(1024)S(1)} collective-permute-done((f32[4352]{0:T(1024)S(1)}, f32[4352]{0:T(1024)S(1)}, u32[]{:S(2)}, u32[]{:S(2)}) %collective-permute-start.54) | collective-permute-done | bytes 17440 | tf_op jit(solution)/shard_map/ppermute | solution.py:33
  431.2 4.3 sum_of.11
  442.5 56.8 %collective-permute-done.66 = f32[256,1536]{1,0:T(8,128)S(1)} collective-permute-done((f32[256,1536]{1,0:T(8,128)}, f32[256,1536]{1,0:T(8,128)S(1)}, u32[]{:S(2)}, u32[]{:S(2)}) %collective-permute-start.66) | collective-permute-done | bytes 1572896 | tf_op jit(solution)/shard_map/ppermute | solution.py:33
  503.0 2.8 add.91
  (278 shorter events, 88.0 us)
Async XLA Ops:
  3.3 76.0 %collective-permute-start.4 = (f32[256,2048]{1,0:T(8,128)S(1)}, f32[256,2048]{1,0:T(8,128)}, u32[]{:S(2)}, u32[]{:S(2)}) collective-permute-start(f32[256,2048]{1,0:T(8,128)S(1)} %get-tuple-element.345), channel_id=1, source_target_pairs={{0,4},{4,0},{8,12},{12,8},{16,20},{20,16},{24,28},{28,24},{1,5},{5... | collective-permute-start | bytes 6291464 | tf_op jit(solution)/shard_map/ppermute | solution.py:33
  24.7 48.7 %collective-permute-start.5 = (f32[128,2048]{1,0:T(8,128)S(1)}, f32[128,2048]{1,0:T(8,128)}, u32[]{:S(2)}, u32[]{:S(2)}) collective-permute-start(f32[128,2048]{1,0:T(8,128)S(1)} %constant_dynamic-slice_fusion.1), channel_id=1, source_target_pairs={{0,16},{4,20},{8,24},{12,28},{16,0},{20,4},{24,8},{28,12},{1,17},{... | collective-permute-start | bytes 3145736 | tf_op jit(solution)/shard_map/ppermute | solution.py:33
  31.6 41.8 %collective-permute-start.6 = (f32[128,2048]{1,0:T(8,128)}, f32[128,2048]{1,0:T(8,128)S(1)}, u32[]{:S(2)}, u32[]{:S(2)}) collective-permute-start(f32[128,2048]{1,0:T(8,128)} %get-tuple-element.362), channel_id=1, source_target_pairs={{0,2},{1,3},{2,0},{3,1},{4,6},{5,7},{6,4},{7,5},{8,10},{9,11},{10,... | collective-permute-start | bytes 3145736 | tf_op jit(solution)/shard_map/ppermute | solution.py:33
  33.1 46.2 %collective-permute-start.7 = (f32[128,2048]{1,0:T(8,128)}, f32[128,2048]{1,0:T(8,128)S(1)}, u32[]{:S(2)}, u32[]{:S(2)}) collective-permute-start(f32[128,2048]{1,0:T(8,128)} %get-tuple-element.363), channel_id=1, source_target_pairs={{0,2},{1,3},{2,0},{3,1},{4,6},{5,7},{6,4},{7,5},{8,10},{9,11},{10,... | collective-permute-start | bytes 3145736 | tf_op jit(solution)/shard_map/ppermute | solution.py:33
  85.8 67.0 %collective-permute-start.8 = (f32[256,2048]{1,0:T(8,128)}, f32[256,2048]{1,0:T(8,128)}, u32[]{:S(2)}, u32[]{:S(2)}) collective-permute-start(f32[256,2048]{1,0:T(8,128)} %get-tuple-element.377), channel_id=1, source_target_pairs={{0,4},{4,0},{8,12},{12,8},{16,20},{20,16},{24,28},{28,24},{1,5},{5... | collective-permute-start | bytes 6291464 | tf_op jit(solution)/shard_map/ppermute | solution.py:33
  86.8 62.2 %collective-permute-start.17 = (f32[128,2048]{1,0:T(8,128)}, f32[128,2048]{1,0:T(8,128)}, u32[]{:S(2)}, u32[]{:S(2)}) collective-permute-start(f32[128,2048]{1,0:T(8,128)} %get-tuple-element.419), channel_id=1, source_target_pairs={{0,16},{4,20},{8,24},{12,28},{16,0},{20,4},{24,8},{28,12},{1,17},{... | collective-permute-start | bytes 3145736 | tf_op jit(solution)/shard_map/ppermute | solution.py:33
  89.5 59.8 %collective-permute-start.18 = (f32[128,2048]{1,0:T(8,128)}, f32[128,2048]{1,0:T(8,128)}, u32[]{:S(2)}, u32[]{:S(2)}) collective-permute-start(f32[128,2048]{1,0:T(8,128)} %collective-permute-done.5), channel_id=1, source_target_pairs={{0,2},{1,3},{2,0},{3,1},{4,6},{5,7},{6,4},{7,5},{8,10},{9,11},{10,... | collective-permute-start | bytes 3145736 | tf_op jit(solution)/shard_map/ppermute | solution.py:33
  150.6 28.4 %collective-permute-start.20 = (f32[256,2048]{1,0:T(8,128)}, f32[256,2048]{1,0:T(8,128)}, u32[]{:S(2)}, u32[]{:S(2)}) collective-permute-start(f32[256,2048]{1,0:T(8,128)} %collective-permute-done.4.refs_2_), channel_id=1, source_target_pairs={{0,1},{1,0},{2,3},{3,2},{4,5},{5,4},{6,7},{7,6},{8,9},{9,8},{10,11... | collective-permute-start | bytes 6291464 | tf_op jit(solution)/shard_map/ppermute | solution.py:33
  151.4 27.7 %collective-permute-start.21 = (f32[256,2048]{1,0:T(8,128)}, f32[256,2048]{1,0:T(8,128)}, u32[]{:S(2)}, u32[]{:S(2)}) collective-permute-start(f32[256,2048]{1,0:T(8,128)} %get-tuple-element.425), channel_id=1, source_target_pairs={{0,1},{1,0},{2,3},{3,2},{4,5},{5,4},{6,7},{7,6},{8,9},{9,8},{10,11... | collective-permute-start | bytes 6291464 | tf_op jit(solution)/shard_map/ppermute | solution.py:33
  152.9 26.2 %collective-permute-start.19 = (f32[256,2048]{1,0:T(8,128)}, f32[256,2048]{1,0:T(8,128)}, u32[]{:S(2)}, u32[]{:S(2)}) collective-permute-start(f32[256,2048]{1,0:T(8,128)} %collective-permute-done.8.refs_0_), channel_id=1, source_target_pairs={{0,1},{1,0},{2,3},{3,2},{4,5},{5,4},{6,7},{7,6},{8,9},{9,8},{10,11... | collective-permute-start | bytes 6291464 | tf_op jit(solution)/shard_map/ppermute | solution.py:33
  153.1 25.6 %collective-permute-start.22 = (f32[128,2048]{1,0:T(8,128)}, f32[128,2048]{1,0:T(8,128)S(1)}, u32[]{:S(2)}, u32[]{:S(2)}) collective-permute-start(f32[128,2048]{1,0:T(8,128)} %collective-permute-done.17.refs_0_), channel_id=1, source_target_pairs={{0,2},{1,3},{2,0},{3,1},{4,6},{5,7},{6,4},{7,5},{8,10},{9,11},{10,... | collective-permute-start | bytes 3145736 | tf_op jit(solution)/shard_map/ppermute | solution.py:33
  179.1 28.2 %collective-permute-start.27 = (f32[256,2048]{1,0:T(8,128)}, f32[256,2048]{1,0:T(8,128)}, u32[]{:S(2)}, u32[]{:S(2)}) collective-permute-start(f32[256,2048]{1,0:T(8,128)} %pad_maximum_fusion.1.refs_4_), channel_id=1, source_target_pairs={{0,1},{1,0},{2,3},{3,2},{4,5},{5,4},{6,7},{7,6},{8,9},{9,8},{10,11... | collective-permute-start | bytes 6291464 | tf_op jit(solution)/shard_map/ppermute | solution.py:33
  179.1 52.6 %collective-permute-start.24 = (f32[256,2048]{1,0:T(8,128)S(1)}, f32[256,2048]{1,0:T(8,128)}, u32[]{:S(2)}, u32[]{:S(2)}) collective-permute-start(f32[256,2048]{1,0:T(8,128)S(1)} %copy-done.3), channel_id=1, source_target_pairs={{0,2},{1,3},{2,0},{3,1},{4,6},{5,7},{6,4},{7,5},{8,10},{9,11},{10,... | collective-permute-start | bytes 6291464 | tf_op jit(solution)/shard_map/ppermute | solution.py:33
  180.7 51.1 %collective-permute-start.25 = (f32[256,2048]{1,0:T(8,128)}, f32[256,2048]{1,0:T(8,128)}, u32[]{:S(2)}, u32[]{:S(2)}) collective-permute-start(f32[256,2048]{1,0:T(8,128)} %pad_maximum_fusion.1.refs_4_), channel_id=1, source_target_pairs={{0,4},{4,0},{8,12},{12,8},{16,20},{20,16},{24,28},{28,24},{1,5},{5... | collective-permute-start | bytes 6291464 | tf_op jit(solution)/shard_map/ppermute | solution.py:33
  240.5 31.2 %collective-permute-start.34 = (f32[256,2048]{1,0:T(8,128)}, f32[256,2048]{1,0:T(8,128)}, u32[]{:S(2)}, u32[]{:S(2)}) collective-permute-start(f32[256,2048]{1,0:T(8,128)} %collective-permute-done.25.refs_4_), channel_id=1, source_target_pairs={{0,1},{1,0},{2,3},{3,2},{4,5},{5,4},{6,7},{7,6},{8,9},{9,8},{10,11... | collective-permute-start | bytes 6291464 | tf_op jit(solution)/shard_map/ppermute | solution.py:33
  240.6 31.0 %collective-permute-start.33 = (f32[128,2048]{1,0:T(8,128)}, f32[128,2048]{1,0:T(8,128)}, u32[]{:S(2)}, u32[]{:S(2)}) collective-permute-start(f32[128,2048]{1,0:T(8,128)} %collective-permute-done.23.refs_0_), channel_id=1, source_target_pairs={{0,2},{1,3},{2,0},{3,1},{4,6},{5,7},{6,4},{7,5},{8,10},{9,11},{10,... | collective-permute-start | bytes 3145736 | tf_op jit(solution)/shard_map/ppermute | solution.py:33
  241.1 30.5 %collective-permute-start.35 = (f32[128,2048]{1,0:T(8,128)}, f32[128,2048]{1,0:T(8,128)S(1)}, u32[]{:S(2)}, u32[]{:S(2)}) collective-permute-start(f32[128,2048]{1,0:T(8,128)} %collective-permute-done.23.refs_0_), channel_id=1, source_target_pairs={{0,1},{1,0},{2,3},{3,2},{4,5},{5,4},{6,7},{7,6},{8,9},{9,8},{10,11... | collective-permute-start | bytes 3145736 | tf_op jit(solution)/shard_map/ppermute | solution.py:33
  241.2 30.4 %collective-permute-start.36 = (f32[512,512]{1,0:T(8,128)}, f32[512,512]{1,0:T(8,128)S(1)}, u32[]{:S(2)}, u32[]{:S(2)}) collective-permute-start(f32[512,512]{1,0:T(8,128)} %get-tuple-element.519), channel_id=1, source_target_pairs={{0,8},{4,12},{8,0},{12,4},{16,24},{20,28},{24,16},{28,20},{1,9},{5... | collective-permute-start | bytes 3145736 | tf_op jit(solution)/shard_map/ppermute | solution.py:33
  242.8 28.8 %collective-permute-start.37 = (f32[256,1024]{1,0:T(8,128)}, f32[256,1024]{1,0:T(8,128)S(1)}, u32[]{:S(2)}, u32[]{:S(2)}) collective-permute-start(f32[256,1024]{1,0:T(8,128)} %few_of.2), channel_id=1, source_target_pairs={{0,4},{4,0},{8,12},{12,8},{16,20},{20,16},{24,28},{28,24},{1,5},{5... | collective-permute-start | bytes 3145736 | tf_op jit(solution)/shard_map/ppermute | solution.py:33
  272.6 27.6 %collective-permute-start.39 = (f32[256,1024]{1,0:T(8,128)}, f32[256,1024]{1,0:T(8,128)S(1)}, u32[]{:S(2)}, u32[]{:S(2)}) collective-permute-start(f32[256,1024]{1,0:T(8,128)} %few_of.3), channel_id=1, source_target_pairs={{0,8},{4,12},{8,0},{12,4},{16,24},{20,28},{24,16},{28,20},{1,9},{5... | collective-permute-start | bytes 3145736 | tf_op jit(solution)/shard_map/ppermute | solution.py:33
  273.0 30.5 %collective-permute-start.42 = (f32[256,1024]{1,0:T(8,128)S(1)}, f32[256,1024]{1,0:T(8,128)}, u32[]{:S(2)}, u32[]{:S(2)}) collective-permute-start(f32[256,1024]{1,0:T(8,128)S(1)} %collective-permute-done.37.few_a_ref), channel_id=1, source_target_pairs={{0,1},{1,0},{2,3},{3,2},{4,5},{5,4},{6,7},{7,6},{8,9},{9,8},{10,11... | collective-permute-start | bytes 3145736 | tf_op jit(solution)/shard_map/ppermute | solution.py:33
  273.2 26.9 %collective-permute-start.40 = (f32[4352]{0:T(1024)S(1)}, f32[4352]{0:T(1024)S(1)}, u32[]{:S(2)}, u32[]{:S(2)}) collective-permute-start(f32[4352]{0:T(1024)S(1)} %pad_maximum_fusion.4), channel_id=1, source_target_pairs={{0,2},{1,3},{2,0},{3,1},{4,6},{5,7},{6,4},{7,5},{8,10},{9,11},{10,... | collective-permute-start | bytes 52232 | tf_op jit(solution)/shard_map/ppermute | solution.py:33
  301.3 48.7 %collective-permute-start.38 = (f32[512,1024]{1,0:T(8,128)}, f32[512,1024]{1,0:T(8,128)S(1)}, u32[]{:S(2)}, u32[]{:S(2)}) collective-permute-start(f32[512,1024]{1,0:T(8,128)} %get-tuple-element.523), channel_id=1, source_target_pairs={{0,4},{4,0},{8,12},{12,8},{16,20},{20,16},{24,28},{28,24},{1,5},{5... | collective-permute-start | bytes 6291464 | tf_op jit(solution)/shard_map/ppermute | solution.py:33
  307.5 70.4 %collective-permute-start.51 = (f32[1536,256]{1,0:T(8,128)}, f32[1536,256]{1,0:T(8,128)S(1)}, u32[]{:S(2)}, u32[]{:S(2)}) collective-permute-start(f32[1536,256]{1,0:T(8,128)} %get-tuple-element.580), channel_id=1, source_target_pairs={{0,8},{4,12},{8,0},{12,4},{16,24},{20,28},{24,16},{28,20},{1,9},{5... | collective-permute-start | bytes 4718600 | tf_op jit(solution)/shard_map/ppermute | solution.py:33
  308.3 69.9 %collective-permute-start.52 = (f32[256,1536]{1,0:T(8,128)}, f32[256,1536]{1,0:T(8,128)}, u32[]{:S(2)}, u32[]{:S(2)}) collective-permute-start(f32[256,1536]{1,0:T(8,128)} %get-tuple-element.581), channel_id=1, source_target_pairs={{0,8},{4,12},{8,0},{12,4},{16,24},{20,28},{24,16},{28,20},{1,9},{5... | collective-permute-start | bytes 4718600 | tf_op jit(solution)/shard_map/ppermute | solution.py:33
  317.0 79.1 %collective-permute-start.56 = (f32[256,2048]{1,0:T(8,128)}, f32[256,2048]{1,0:T(8,128)}, u32[]{:S(2)}, u32[]{:S(2)}) collective-permute-start(f32[256,2048]{1,0:T(8,128)} %sum_of.9.a_ref), channel_id=1, source_target_pairs={{0,2},{1,3},{2,0},{3,1},{4,6},{5,7},{6,4},{7,5},{8,10},{9,11},{10,... | collective-permute-start | bytes 6291464 | tf_op jit(solution)/shard_map/ppermute | solution.py:33
  323.4 55.6 %collective-permute-start.50 = (f32[1024,256]{1,0:T(8,128)}, f32[1024,256]{1,0:T(8,128)}, u32[]{:S(2)}, u32[]{:S(2)}) collective-permute-start(f32[1024,256]{1,0:T(8,128)} %pair_grads.4), channel_id=1, source_target_pairs={{0,4},{4,0},{8,12},{12,8},{16,20},{20,16},{24,28},{28,24},{1,5},{5... | collective-permute-start | bytes 3145736 | tf_op jit(solution)/shard_map/ppermute | solution.py:33
  379.0 47.8 %collective-permute-start.53 = (f32[512,1024]{1,0:T(8,128)}, f32[512,1024]{1,0:T(8,128)S(1)}, u32[]{:S(2)}, u32[]{:S(2)}) collective-permute-start(f32[512,1024]{1,0:T(8,128)} %pair_grads.5), channel_id=1, source_target_pairs={{0,8},{4,12},{8,0},{12,4},{16,24},{20,28},{24,16},{28,20},{1,9},{5... | collective-permute-start | bytes 6291464 | tf_op jit(solution)/shard_map/ppermute | solution.py:33
  379.9 47.3 %collective-permute-start.55 = (f32[256,2048]{1,0:T(8,128)}, f32[256,2048]{1,0:T(8,128)}, u32[]{:S(2)}, u32[]{:S(2)}) collective-permute-start(f32[256,2048]{1,0:T(8,128)} %sum_of.10.refs_0_), channel_id=1, source_target_pairs={{0,2},{1,3},{2,0},{3,1},{4,6},{5,7},{6,4},{7,5},{8,10},{9,11},{10,... | collective-permute-start | bytes 6291464 | tf_op jit(solution)/shard_map/ppermute | solution.py:33
  429.1 70.2 %collective-permute-start.66 = (f32[256,1536]{1,0:T(8,128)}, f32[256,1536]{1,0:T(8,128)S(1)}, u32[]{:S(2)}, u32[]{:S(2)}) collective-permute-start(f32[256,1536]{1,0:T(8,128)} %pad_maximum_fusion.2), channel_id=1, source_target_pairs={{0,16},{4,20},{8,24},{12,28},{16,0},{20,4},{24,8},{28,12},{1,17},{... | collective-permute-start | bytes 4718600 | tf_op jit(solution)/shard_map/ppermute | solution.py:33
  429.8 69.5 %collective-permute-start.67 = (f32[256,1536]{1,0:T(8,128)}, f32[256,1536]{1,0:T(8,128)}, u32[]{:S(2)}, u32[]{:S(2)}) collective-permute-start(f32[256,1536]{1,0:T(8,128)} %get-tuple-element.643), channel_id=1, source_target_pairs={{0,8},{4,12},{8,0},{12,4},{16,24},{20,28},{24,16},{28,20},{1,9},{5... | collective-permute-start | bytes 4718600 | tf_op jit(solution)/shard_map/ppermute | solution.py:33
  440.1 61.7 %collective-permute-start.65 = (f32[4352]{0:T(1024)S(1)}, f32[4352]{0:T(1024)S(1)}, u32[]{:S(2)}, u32[]{:S(2)}) collective-permute-start(f32[4352]{0:T(1024)S(1)} %add.84), channel_id=1, source_target_pairs={{0,16},{4,20},{8,24},{12,28},{16,0},{20,4},{24,8},{28,12},{1,17},{... | collective-permute-start | bytes 52232 | tf_op jit(solution)/shard_map/ppermute | solution.py:33
  (89 other events, 757.8 us)

commit v6 on v5

--- a/solution.py
+++ b/solution.py
@@ -174,16 +174,20 @@
     down = dot_tn(hidden, cc_ref[...])
     gate = dot(at_ref[...], d_gate)
     up = dot(at_ref[...], d_up)
-    count = len(sums) // 3
+    count = len(sums) // 2
     for j in range(count):
         part = slice(j * block, (j + 1) * block)
-        for k, fresh in ((j, down[:, part]), (count + j, gate[part]), (2 * count + j, up[part])):
-            old = 0.0 if before is None else before[k][...]
-            sums[k][...] = fresh + old
+        for k, rows, fresh in (
+            (j, slice(None), down[:, part]),
+            (count + j, slice(0, block), gate[part]),
+            (count + j, slice(block, 2 * block), up[part]),
+        ):
+            old = 0.0 if before is None else before[k][rows, :]
+            sums[k][rows, :] = fresh + old
 
 
 def rest_kernel(where_ref, nb_ref, cb_ref, hid_ref, dg_ref, du_ref, wd_ref, *rest):
-    count = (len(rest) - 4) // 3
+    count = (len(rest) - 4) // 2
     ya_ref, yb_ref, *sums = rest[:-2]
     at_ref, cc_ref = rest[-2:]
     half = ya_ref.shape[0]
@@ -203,9 +207,9 @@
 
 def sum_specs(count, block, hidden):
     specs = [pl.BlockSpec((TILE, block), lambda i, *_: (i, 0))] * count
-    specs += [pl.BlockSpec((block, TILE), lambda i, *_: (0, i))] * (2 * count)
+    specs += [pl.BlockSpec((2 * block, TILE), lambda i, *_: (0, i))] * count
     shapes = [jax.ShapeDtypeStruct((hidden, block), f32)] * count
-    shapes += [jax.ShapeDtypeStruct((block, hidden), f32)] * (2 * count)
+    shapes += [jax.ShapeDtypeStruct((2 * block, hidden), f32)] * count
     return specs, shapes
 
 
@@ -246,9 +250,9 @@
     n_refs, refs = refs[:n_pieces], refs[n_pieces:]
     c_refs, refs = refs[:c_pieces], refs[c_pieces:]
     g_ref, wg_ref, wu_ref, wd_ref = refs[:4]
-    before = refs[4 : 4 + 3 * count]
-    sums = refs[4 + 3 * count : 4 + 6 * count]
-    nb_ref, cb_ref, at_ref, cc_ref = refs[4 + 6 * count :]
+    before = refs[4 : 4 + 2 * count]
+    sums = refs[4 + 2 * count : 4 + 4 * count]
+    nb_ref, cb_ref, at_ref, cc_ref = refs[4 + 4 * count :]
     block = cc_ref.shape[1] // count
 
     @pl.when(pl.program_id(0) == 0)
@@ -378,7 +382,7 @@
     pair = jnp.concatenate([d_gate, d_up], axis=1)
     both = [dot_tn(take(normed), pair) for take in takes]
     ff = hidden.shape[1]
-    return [dot_tn(hidden, take(cot)) for take in takes] + [b[:, :ff] for b in both] + [b[:, ff:] for b in both]
+    return [dot_tn(hidden, take(cot)) for take in takes] + [jnp.concatenate([b[:, :ff], b[:, ff:]]) for b in both]
 
 
 def plain_own_feed(r_a, r_b, cot, g, w_gate, w_up, w_down):
@@ -958,7 +962,7 @@
     sums = add_group([n3, n3x, n3t, n3xt], [c3, c3t], sums)
     k = len(offsets)
     h = k // 2
-    lists = [sums[i * k : (i + 1) * k] for i in range(3)]
+    lists = [sums[i * k : (i + 1) * k] for i in range(2)]
     keep = [p[:h] for p in lists]
     send = [p[h:] for p in lists]
 
@@ -968,7 +972,7 @@
     def finish(keep, got):
         return scatter_sum([a + b for a, b in zip(keep, got)], middle[1:])
 
-    got = first_step(send[0]) + first_step(send[1])
+    got = first_step(send[1])
     near_r, gains_got, *d1_b = seq(near_r, gains_got, *d1_b)
     gains = gains + gains_got
     near_nt, gains_got, *d1_got = seq(*core_swaps((near_n, gains, *d1_b)))
@@ -986,18 +990,18 @@
     near_rs = [near_r, seq(core_swap(near_r))]
     out_1 = seq(outs(1))
     out_mid = swap(out_1, "dp", rest_out[0])
-    near_d, gains_got, near_nt = seq(near_d, gains_got, near_nt)
-    gains = gains + gains_got
+    near_d, near_nt = seq(near_d, near_nt)
     near_ns = [near_n, near_nt]
-    in_1, out_mid, down_chip, *got = seq(seq(ins(1)), out_mid, down_chip, *got)
+    in_1, down_chip, *got = seq(seq(ins(1)), down_chip, *got)
     down_x = x_swap(down_chip)
     in_mid = swap(in_1, "dp", rest[0])
+    in_0, out_0 = seq(ins(0), outs(0))
+    out_mid, gains_got = seq(out_mid, gains_got)
+    gains = gains + gains_got
     gains_got = swap(gains, "dp", rest[0])
-    in_0, out_0 = seq(ins(0), outs(0))
-    summed_down = finish(keep[0], got[:h])
-    summed_gate = finish(keep[1], got[h:])
+    summed_pair = finish(keep[1], got)
     if len(rest) == 2:
-        summed_down, summed_gate = seq(summed_down, summed_gate)
+        summed_pair = seq(summed_pair)
 
     def split(a):
         return list(a.reshape(q, a.shape[0] // q, a.shape[1]))
@@ -1006,8 +1010,8 @@
     gt_mine, *gt_split = seq(*back_of(dr_mine, d1_chip, d1_x, tok_mine, ga))
     gt_theirs = jnp.concatenate(seq(*core_swaps(gt_split)))
     grad_tokens = seq(in_order(gt_mine, gt_theirs))
-    in_mid, gains_got, down_x, *send_up = seq(in_mid, gains_got, down_x, *send[2])
-    got_up = first_step(send_up)
+    in_mid, gains_got, down_x, *send_down = seq(in_mid, gains_got, down_x, *send[0])
+    got_down = first_step(send_down)
     gains = gains + gains_got
     gains_got = swap(gains, "dp", far)
     both = seq(*split(in_0 + in_mid), *split(out_0 + out_mid))
@@ -1024,12 +1028,12 @@
     for mask in rest[1:-1]:
         gains = gains + swap(gains, "dp", mask)
     if len(rest) == 2:
-        last, *got_up = seq(last, *got_up)
+        last, *got_down = seq(last, *got_down)
         columns = both[0].shape[1]
         summed_qkv = both[0] + last[:, :columns]
         end = jnp.concatenate([last[:, columns : columns + block], last[:, columns + block :]])
         summed_out = both[2] + end
-    summed_up = finish(keep[2], got_up)
+    summed_down = finish(keep[0], got_down)
     nq, nk = w_query.shape[1], w_key.shape[1]
     gains = gains + 0.0 * seq.token.astype(f32)
     return (
@@ -1043,8 +1047,8 @@
         gains[width + hd : width + 2 * hd],
         summed_out,
         gains[width + 2 * hd :],
-        summed_gate,
-        summed_up,
+        summed_pair[:block],
+        summed_pair[block:],
         summed_down,
     )
 

time: 511 us -> 501 us (0.980); the launches traced: 507 us -> 491 us
  Pallas kernels: 227 us -> 215 us
  waiting for transfers between devices: 190 us -> 181 us
  local copies, waits for them, and re-layouts: 15.8 us -> 21.7 us
    pallas_call x1, Pallas kernels: 25.2 us -> 15.1 us  [own_rest(): pl.pallas_call(rest_kernel, grid_spec=pltpu.PrefetchScalarGridSpec(num_sc...]
    ppermute x68 -> x67, waiting for transfers between devices: 190 us -> 181 us  [swap(): return lax.ppermute(value, axis, [(i, i ^ mask) for i in range(size)])]
    ppermute x68 -> x67, starting transfers between devices: 45.5 us -> 44.6 us  [swap(): return lax.ppermute(value, axis, [(i, i ^ mask) for i in range(size)])]
  transfers between devices with their start and end apart: 68 -> 67, of which waited for: 23 -> 20; matrix products, arithmetic and copies ran while one was open for 5% -> 5% of each run, Pallas kernels for 43% -> 42%
where the time goes in v6:
time: 501 us; the launch traced here: 491 us
  Pallas kernels  215 us (43%)
  waiting for transfers between devices  181 us (36%)
  starting transfers between devices  44.6 us (9%)
  other arithmetic  26.1 us (5%)
  local copies, waits for them, and re-layouts  21.7 us (4%)
    ppermute x67, waiting for transfers between devices, swap(): return lax.ppermute(value, axis, [(i, i ^ mask) for i in range(size)])  181 us
    pallas_call x3, Pallas kernels, group_feed(): pl.pallas_call(functools.partial(group_kernel, len(ns), len(cs), count),...  72.2 us
    ppermute x67, starting transfers between devices, swap(): return lax.ppermute(value, axis, [(i, i ^ mask) for i in range(size)])  44.6 us
    pallas_call x1, Pallas kernels, own_feed(): pl.pallas_call(own_kernel, grid=(hidden // TILE,), in_specs=[whole((half,...  27.3 us
    pallas_call x1, Pallas kernels, attend_back(): pl.pallas_call(functools.partial(attend_back_kernel, half), grid_spec=plt...  24.1 us
    pallas_call x6, Pallas kernels, sum_of(): pl.pallas_call(functools.partial(sum_kernel, len(bs)), in_specs=[whole(x....  24 us
    pallas_call x4, Pallas kernels, pair_grads(): pl.pallas_call(functools.partial(pair_kernel, inward), grid_spec=pltpu.Pr...  19.7 us
    pallas_call x1, Pallas kernels, own_rest(): pl.pallas_call(rest_kernel, grid_spec=pltpu.PrefetchScalarGridSpec(num_sc...  15.1 us
  transfers between devices with their start and end apart: 67, of which 20 were waited for; matrix products, arithmetic and copies ran while one was open for 5% of the time, Pallas kernels for 42%

profile of v6, /device:TPU:0, one launch (start us, length us, event | category | flops | bytes accessed | tf_op | source)
XLA Modules:
  0.0 491.1 jit_solution(7987341169510584651)
XLA Ops:
  3.3 3.1 collective-permute-start.4
  8.7 13.9 %attend.1 = (bf16[512,2048]{1,0:T(8,128)(2,1)}, f32[512,512]{1,0:T(8,128)}, f32[512,256]{1,0:T(8,128)}, bf16[512,256]{1,0:T(8,128)(2,1)}, bf16[512,512]{1,0:T(8,...) custom-call(s32[1]{0:T(128)} %bitcast.1.core_ref, ...), custom_call_target="tpu_custom_call" | custom-call | tf_op jit(solution)/shard_map/attend/pallas_call | solution.py:505
  27.4 4.3 sum_of.6
  36.0 37.4 %collective-permute-done.5 = f32[128,2048]{1,0:T(8,128)} collective-permute-done((f32[128,2048]{1,0:T(8,128)S(1)}, f32[128,2048]{1,0:T(8,128)}, u32[]{:S(2)}, u32[]{:S(2)}) %collective-permute-start.5) | collective-permute-done | bytes 1048608 | tf_op jit(solution)/shard_map/ppermute | solution.py:33
  73.5 5.9 %collective-permute-done.7.c_ref = f32[128,2048]{1,0:T(8,128)S(1)} collective-permute-done((f32[128,2048]{1,0:T(8,128)}, f32[128,2048]{1,0:T(8,128)S(1)}, u32[]{:S(2)}, u32[]{:S(2)}) %collective-permute-start.7) | collective-permute-done | bytes 1048608 | tf_op jit(solution)/shard_map/ppermute | solution.py:33
  80.3 5.6 %resid_of.1 = (f32[256,2048]{1,0:T(8,128)}, f32[256,2048]{1,0:T(8,128)}, f32[128,2048]{1,0:T(8,128)}, f32[64,2048]{1,0:T(8,128)}, f32[64,2048]{1,0:T(8,128)}, /*index=5*/f32[64,2048]{1,0:T(8,128)}, f32[64,2048]{1,0:T(8,128)}) custom-call(s32[1]{0:T(128)} %bitcast.x_at_ref, bf16[256,2048]{1,0:T(8,128)(2,1)} %constant_dynamic-slice_fusion.3.tok_ref.a_ref, ...), custom_call_target="tpu_custom_call" | custom-call | tf_op jit(solution)/shard_map/resid_of/pallas_call | solution.py:353
  95.9 27.3 %own_feed.1 = (bf16[512,2048]{1,0:T(8,128)(2,1)}, bf16[512,1536]{1,0:T(8,128)(2,1)}, bf16[512,1536]{1,0:T(8,128)(2,1)}, bf16[512,1536]{1,0:T(8,128)(2,1)}, f32[2...) custom-call(f32[256,2048]{1,0:T(8,128)} %get-tuple-element.358.ra_re, ...), custom_call_target="tpu_custom_call" | custom-call | tf_op jit(solution)/shard_map/own_feed/pallas_call | solution.py:130
  123.3 15.1 %own_rest.1 = (f32[256,2048]{1,0:T(8,128)}, f32[256,2048]{1,0:T(8,128)}, f32[1536,256]{1,0:T(8,128)}, f32[1536,256]{1,0:T(8,128)}, f32[512,1536]{1,0:T(8,128)}, /*index=5*/f32[512,1536]{1,0:T(8,128)}) custom-call(s32[2]{0:T(128)} %multiply_xor_fusion.1.where_ref, bf16[512,2048]{1,0:T(8,128)(2,1)} %get-tuple-element.381.nb_ref, ...), custom_call_target="tpu_custom_call" | custom-call | tf_op jit(solution)/shard_map/own_rest/pallas_call | solution.py:223
  145.6 3.2 pad_maximum_fusion.1.refs_4_
  148.8 3.7 sum_of.7.refs_0_
  152.5 3.8 few_of.2
  156.3 12.3 %collective-permute-done.22.refs_1_ = f32[128,2048]{1,0:T(8,128)S(1)} collective-permute-done((f32[128,2048]{1,0:T(8,128)}, f32[128,2048]{1,0:T(8,128)S(1)}, u32[]{:S(2)}, u32[]{:S(2)}) %collective-permute-start.22) | collective-permute-done | bytes 1048608 | tf_op jit(solution)/shard_map/ppermute | solution.py:33
  172.7 24.1 %group_feed.3 = (f32[1536,256]{1,0:T(8,128)}, f32[1536,256]{1,0:T(8,128)}, f32[512,1536]{1,0:T(8,128)}, f32[512,1536]{1,0:T(8,128)}) custom-call(s32[2]{0:T(128)} %multiply_xor_fusion.1.where_ref, f32[256,2048]{1,0:T(8,128)} %collective-permute-done.8.refs_0_, f32[256,2048]{1,0:T(8,128)} %collective-permute-done.19.refs_1_, ...), custom_call_target="tpu_custom_call" | custom-call | tf_op jit(solution)/shard_map/group_feed/pallas_call | solution.py:282
  196.8 24.0 %group_feed.4 = (f32[1536,256]{1,0:T(8,128)}, f32[1536,256]{1,0:T(8,128)}, f32[512,1536]{1,0:T(8,128)}, f32[512,1536]{1,0:T(8,128)}) custom-call(s32[2]{0:T(128)} %multiply_xor_fusion.1.where_ref, f32[128,2048]{1,0:T(8,128)} %collective-permute-done.17.refs_0_, f32[128,2048]{1,0:T(8,128)} %copy-done.24, f32[128,2048]{1,0:T(8,128)} %collective-permute-done.26.refs_2_, ...), custom_call_target="tpu_custom_call" | custom-call | tf_op jit(solution)/shard_map/group_feed/pallas_call | solution.py:282
  220.8 4.3 sum_of.8
  232.9 24.1 %attend_back.1 = (bf16[512,2048]{1,0:T(8,128)(2,1)}, f32[256,2048]{1,0:T(8,128)}, bf16[512,1024]{1,0:T(8,128)(2,1)}, f32[512,1024]{1,0:T(8,128)}, f32[256,2048]{...) custom-call(s32[1]{0:T(128)} %bitcast.1.core_ref, ...), custom_call_target="tpu_custom_call" | custom-call | tf_op jit(solution)/shard_map/attend_back/pallas_call | solution.py:641
  257.0 3.1 few_of.3
  264.1 24.2 %group_feed.5 = (f32[1536,256]{1,0:T(8,128)}, f32[1536,256]{1,0:T(8,128)}, f32[512,1536]{1,0:T(8,128)}, f32[512,1536]{1,0:T(8,128)}) custom-call(s32[2]{0:T(128)} %multiply_xor_fusion.1.where_ref, f32[128,2048]{1,0:T(8,128)} %collective-permute-done.23.refs_0_, f32[128,2048]{1,0:T(8,128)} %collective-permute-done.33.refs_1_, f32[128,2048]{1,0:T(8,128)} %copy-done.25, ...), custom_call_target="tpu_custom_call" | custom-call | tf_op jit(solution)/shard_map/group_feed/pallas_call | solution.py:282
  299.0 3.7 sum_of.10.refs_0_
  302.8 3.7 sum_of.9.a_ref
  309.5 4.3 pair_grads.4
  314.8 27.6 %collective-permute-done.38.wide_ref = f32[512,1024]{1,0:T(8,128)S(1)} collective-permute-done((f32[512,1024]{1,0:T(8,128)}, f32[512,1024]{1,0:T(8,128)S(1)}, u32[]{:S(2)}, u32[]{:S(2)}) %collective-permute-start.38) | collective-permute-done | bytes 2097184 | tf_op jit(solution)/shard_map/ppermute | solution.py:33
  343.7 5.5 %pair_grads.5 = f32[512,1024]{1,0:T(8,128)} custom-call(s32[2]{0:T(128)} %broadcast_xor_fusion.3.where_ref, bf16[512,2048]{1,0:T(8,128)(2,1)} %get-tuple-element.359.a_ref, bf16[512,1024]{1,0:T(8,128)(2,1)} %get-tuple-element.488.b_ref, f32[256,1024]{1,0:T(8,128)} %copy-done.12, f32[256,1024]{1,0:T(8,128)} %copy-done.13, f32[512,1024]{1,0:T(8,128)} %copy-done.1), custom_call_target="tpu_custom_call" | custom-call | tf_op jit(solution)/shard_map/pair_grads/pallas_call | solution.py:765
  349.2 9.6 %collective-permute-done.49 = f32[512,1536]{1,0:T(8,128)} collective-permute-done((f32[512,1536]{1,0:T(8,128)}, f32[512,1536]{1,0:T(8,128)}, u32[]{:S(2)}, u32[]{:S(2)}) %collective-permute-start.49) | collective-permute-done | bytes 3145760 | tf_op jit(solution)/shard_map/ppermute | solution.py:33
  362.8 4.3 pair_grads.7
  367.1 5.6 %pair_grads.6 = f32[512,1024]{1,0:T(8,128)} custom-call(s32[2]{0:T(128)} %multiply_xor_fusion.where_ref, bf16[512,2048]{1,0:T(8,128)(2,1)} %get-tuple-element.359.a_ref, bf16[512,1024]{1,0:T(8,128)(2,1)} %get-tuple-element.488.b_ref, f32[256,1024]{1,0:T(8,128)} %copy-done.12, f32[256,1024]{1,0:T(8,128)} %copy-done.13, f32[512,1024]{1,0:T(8,128)} %copy-done.1), custom_call_target="tpu_custom_call" | custom-call | tf_op jit(solution)/shard_map/pair_grads/pallas_call | solution.py:765
  372.7 3.4 add.75
  376.1 6.0 %back_of.1 = (f32[256,2048]{1,0:T(8,128)}, f32[64,2048]{1,0:T(8,128)}, f32[64,2048]{1,0:T(8,128)}, f32[64,2048]{1,0:T(8,128)}, f32[64,2048]{1,0:T(8,128)}) custom-call(f32[256,2048]{1,0:T(8,128)} %get-tuple-element.557.dr_ref, f32[256,2048]{1,0:T(8,128)} %sum_of.9.a_ref, f32[256,2048]{1,0:T(8,128)} %collective-permute-done.55.b_ref, ...), custom_call_target="tpu_custom_call" | custom-call | tf_op jit(solution)/shard_map/back_of/pallas_call | solution.py:699
  388.7 17.6 %collective-permute-done.53 = f32[4352]{0:T(1024)S(1)} collective-permute-done((f32[4352]{0:T(1024)S(1)}, f32[4352]{0:T(1024)S(1)}, u32[]{:S(2)}, u32[]{:S(2)}) %collective-permute-start.53) | collective-permute-done | bytes 17440 | tf_op jit(solution)/shard_map/ppermute | solution.py:33
  413.2 4.3 sum_of.11
  424.2 56.8 %collective-permute-done.65 = f32[256,1536]{1,0:T(8,128)} collective-permute-done((f32[256,1536]{1,0:T(8,128)}, f32[256,1536]{1,0:T(8,128)}, u32[]{:S(2)}, u32[]{:S(2)}) %collective-permute-start.65) | collective-permute-done | bytes 1572896 | tf_op jit(solution)/shard_map/ppermute | solution.py:33
  487.1 2.8 add.87
  (276 shorter events, 94.1 us)
Async XLA Ops:
  3.3 76.1 %collective-permute-start.4 = (f32[256,2048]{1,0:T(8,128)S(1)}, f32[256,2048]{1,0:T(8,128)}, u32[]{:S(2)}, u32[]{:S(2)}) collective-permute-start(f32[256,2048]{1,0:T(8,128)S(1)} %get-tuple-element.328), channel_id=1, source_target_pairs={{0,4},{4,0},{8,12},{12,8},{16,20},{20,16},{24,28},{28,24},{1,5},{5... | collective-permute-start | bytes 6291464 | tf_op jit(solution)/shard_map/ppermute | solution.py:33
  24.8 48.7 %collective-permute-start.5 = (f32[128,2048]{1,0:T(8,128)S(1)}, f32[128,2048]{1,0:T(8,128)}, u32[]{:S(2)}, u32[]{:S(2)}) collective-permute-start(f32[128,2048]{1,0:T(8,128)S(1)} %constant_dynamic-slice_fusion.1), channel_id=1, source_target_pairs={{0,16},{4,20},{8,24},{12,28},{16,0},{20,4},{24,8},{28,12},{1,17},{... | collective-permute-start | bytes 3145736 | tf_op jit(solution)/shard_map/ppermute | solution.py:33
  31.7 41.8 %collective-permute-start.6 = (f32[128,2048]{1,0:T(8,128)}, f32[128,2048]{1,0:T(8,128)S(1)}, u32[]{:S(2)}, u32[]{:S(2)}) collective-permute-start(f32[128,2048]{1,0:T(8,128)} %get-tuple-element.345), channel_id=1, source_target_pairs={{0,2},{1,3},{2,0},{3,1},{4,6},{5,7},{6,4},{7,5},{8,10},{9,11},{10,... | collective-permute-start | bytes 3145736 | tf_op jit(solution)/shard_map/ppermute | solution.py:33
  33.2 46.2 %collective-permute-start.7 = (f32[128,2048]{1,0:T(8,128)}, f32[128,2048]{1,0:T(8,128)S(1)}, u32[]{:S(2)}, u32[]{:S(2)}) collective-permute-start(f32[128,2048]{1,0:T(8,128)} %get-tuple-element.346), channel_id=1, source_target_pairs={{0,2},{1,3},{2,0},{3,1},{4,6},{5,7},{6,4},{7,5},{8,10},{9,11},{10,... | collective-permute-start | bytes 3145736 | tf_op jit(solution)/shard_map/ppermute | solution.py:33
  85.9 56.9 %collective-permute-start.8 = (f32[256,2048]{1,0:T(8,128)}, f32[256,2048]{1,0:T(8,128)}, u32[]{:S(2)}, u32[]{:S(2)}) collective-permute-start(f32[256,2048]{1,0:T(8,128)} %get-tuple-element.360), channel_id=1, source_target_pairs={{0,4},{4,0},{8,12},{12,8},{16,20},{20,16},{24,28},{28,24},{1,5},{5... | collective-permute-start | bytes 6291464 | tf_op jit(solution)/shard_map/ppermute | solution.py:33
  86.9 52.1 %collective-permute-start.17 = (f32[128,2048]{1,0:T(8,128)}, f32[128,2048]{1,0:T(8,128)}, u32[]{:S(2)}, u32[]{:S(2)}) collective-permute-start(f32[128,2048]{1,0:T(8,128)} %get-tuple-element.400), channel_id=1, source_target_pairs={{0,16},{4,20},{8,24},{12,28},{16,0},{20,4},{24,8},{28,12},{1,17},{... | collective-permute-start | bytes 3145736 | tf_op jit(solution)/shard_map/ppermute | solution.py:33
  89.5 49.7 %collective-permute-start.18 = (f32[128,2048]{1,0:T(8,128)}, f32[128,2048]{1,0:T(8,128)}, u32[]{:S(2)}, u32[]{:S(2)}) collective-permute-start(f32[128,2048]{1,0:T(8,128)} %collective-permute-done.5), channel_id=1, source_target_pairs={{0,2},{1,3},{2,0},{3,1},{4,6},{5,7},{6,4},{7,5},{8,10},{9,11},{10,... | collective-permute-start | bytes 3145736 | tf_op jit(solution)/shard_map/ppermute | solution.py:33
  140.6 28.4 %collective-permute-start.20 = (f32[256,2048]{1,0:T(8,128)}, f32[256,2048]{1,0:T(8,128)}, u32[]{:S(2)}, u32[]{:S(2)}) collective-permute-start(f32[256,2048]{1,0:T(8,128)} %collective-permute-done.4.refs_2_), channel_id=1, source_target_pairs={{0,1},{1,0},{2,3},{3,2},{4,5},{5,4},{6,7},{7,6},{8,9},{9,8},{10,11... | collective-permute-start | bytes 6291464 | tf_op jit(solution)/shard_map/ppermute | solution.py:33
  141.3 27.7 %collective-permute-start.21 = (f32[256,2048]{1,0:T(8,128)}, f32[256,2048]{1,0:T(8,128)}, u32[]{:S(2)}, u32[]{:S(2)}) collective-permute-start(f32[256,2048]{1,0:T(8,128)} %get-tuple-element.406), channel_id=1, source_target_pairs={{0,1},{1,0},{2,3},{3,2},{4,5},{5,4},{6,7},{7,6},{8,9},{9,8},{10,11... | collective-permute-start | bytes 6291464 | tf_op jit(solution)/shard_map/ppermute | solution.py:33
  142.8 26.2 %collective-permute-start.19 = (f32[256,2048]{1,0:T(8,128)}, f32[256,2048]{1,0:T(8,128)}, u32[]{:S(2)}, u32[]{:S(2)}) collective-permute-start(f32[256,2048]{1,0:T(8,128)} %collective-permute-done.8.refs_0_), channel_id=1, source_target_pairs={{0,1},{1,0},{2,3},{3,2},{4,5},{5,4},{6,7},{7,6},{8,9},{9,8},{10,11... | collective-permute-start | bytes 6291464 | tf_op jit(solution)/shard_map/ppermute | solution.py:33
  143.0 25.6 %collective-permute-start.22 = (f32[128,2048]{1,0:T(8,128)}, f32[128,2048]{1,0:T(8,128)S(1)}, u32[]{:S(2)}, u32[]{:S(2)}) collective-permute-start(f32[128,2048]{1,0:T(8,128)} %collective-permute-done.17.refs_0_), channel_id=1, source_target_pairs={{0,2},{1,3},{2,0},{3,1},{4,6},{5,7},{6,4},{7,5},{8,10},{9,11},{10,... | collective-permute-start | bytes 3145736 | tf_op jit(solution)/shard_map/ppermute | solution.py:33
  143.6 25.4 %collective-permute-start.23 = (f32[128,2048]{1,0:T(8,128)}, f32[128,2048]{1,0:T(8,128)}, u32[]{:S(2)}, u32[]{:S(2)}) collective-permute-start(f32[128,2048]{1,0:T(8,128)} %collective-permute-done.17.refs_0_), channel_id=1, source_target_pairs={{0,4},{4,0},{8,12},{12,8},{16,20},{20,16},{24,28},{28,24},{1,5},{5... | collective-permute-start | bytes 3145736 | tf_op jit(solution)/shard_map/ppermute | solution.py:33
  169.0 27.8 %collective-permute-start.27 = (f32[256,2048]{1,0:T(8,128)}, f32[256,2048]{1,0:T(8,128)}, u32[]{:S(2)}, u32[]{:S(2)}) collective-permute-start(f32[256,2048]{1,0:T(8,128)} %pad_maximum_fusion.1.refs_4_), channel_id=1, source_target_pairs={{0,1},{1,0},{2,3},{3,2},{4,5},{5,4},{6,7},{7,6},{8,9},{9,8},{10,11... | collective-permute-start | bytes 6291464 | tf_op jit(solution)/shard_map/ppermute | solution.py:33
  169.1 51.7 %collective-permute-start.24 = (f32[256,2048]{1,0:T(8,128)S(1)}, f32[256,2048]{1,0:T(8,128)}, u32[]{:S(2)}, u32[]{:S(2)}) collective-permute-start(f32[256,2048]{1,0:T(8,128)S(1)} %copy-done.3), channel_id=1, source_target_pairs={{0,2},{1,3},{2,0},{3,1},{4,6},{5,7},{6,4},{7,5},{8,10},{9,11},{10,... | collective-permute-start | bytes 6291464 | tf_op jit(solution)/shard_map/ppermute | solution.py:33
  170.6 50.1 %collective-permute-start.25 = (f32[256,2048]{1,0:T(8,128)}, f32[256,2048]{1,0:T(8,128)}, u32[]{:S(2)}, u32[]{:S(2)}) collective-permute-start(f32[256,2048]{1,0:T(8,128)} %pad_maximum_fusion.1.refs_4_), channel_id=1, source_target_pairs={{0,4},{4,0},{8,12},{12,8},{16,20},{20,16},{24,28},{28,24},{1,5},{5... | collective-permute-start | bytes 6291464 | tf_op jit(solution)/shard_map/ppermute | solution.py:33
  172.2 24.6 %collective-permute-start.26 = (f32[128,2048]{1,0:T(8,128)}, f32[128,2048]{1,0:T(8,128)}, u32[]{:S(2)}, u32[]{:S(2)}) collective-permute-start(f32[128,2048]{1,0:T(8,128)} %collective-permute-done.17.refs_0_), channel_id=1, source_target_pairs={{0,1},{1,0},{2,3},{3,2},{4,5},{5,4},{6,7},{7,6},{8,9},{9,8},{10,11... | collective-permute-start | bytes 3145736 | tf_op jit(solution)/shard_map/ppermute | solution.py:33
  172.2 24.6 %collective-permute-start.28 = (f32[128,2048]{1,0:T(8,128)S(1)}, f32[128,2048]{1,0:T(8,128)}, u32[]{:S(2)}, u32[]{:S(2)}) collective-permute-start(f32[128,2048]{1,0:T(8,128)S(1)} %collective-permute-done.22.refs_1_), channel_id=1, source_target_pairs={{0,1},{1,0},{2,3},{3,2},{4,5},{5,4},{6,7},{7,6},{8,9},{9,8},{10,11... | collective-permute-start | bytes 3145736 | tf_op jit(solution)/shard_map/ppermute | solution.py:33
  229.5 30.7 %collective-permute-start.34 = (f32[256,2048]{1,0:T(8,128)}, f32[256,2048]{1,0:T(8,128)}, u32[]{:S(2)}, u32[]{:S(2)}) collective-permute-start(f32[256,2048]{1,0:T(8,128)} %collective-permute-done.25.refs_4_), channel_id=1, source_target_pairs={{0,1},{1,0},{2,3},{3,2},{4,5},{5,4},{6,7},{7,6},{8,9},{9,8},{10,11... | collective-permute-start | bytes 6291464 | tf_op jit(solution)/shard_map/ppermute | solution.py:33
  229.6 30.5 %collective-permute-start.33 = (f32[128,2048]{1,0:T(8,128)}, f32[128,2048]{1,0:T(8,128)}, u32[]{:S(2)}, u32[]{:S(2)}) collective-permute-start(f32[128,2048]{1,0:T(8,128)} %collective-permute-done.23.refs_0_), channel_id=1, source_target_pairs={{0,2},{1,3},{2,0},{3,1},{4,6},{5,7},{6,4},{7,5},{8,10},{9,11},{10,... | collective-permute-start | bytes 3145736 | tf_op jit(solution)/shard_map/ppermute | solution.py:33
  230.2 30.0 %collective-permute-start.35 = (f32[128,2048]{1,0:T(8,128)}, f32[128,2048]{1,0:T(8,128)S(1)}, u32[]{:S(2)}, u32[]{:S(2)}) collective-permute-start(f32[128,2048]{1,0:T(8,128)} %collective-permute-done.23.refs_0_), channel_id=1, source_target_pairs={{0,1},{1,0},{2,3},{3,2},{4,5},{5,4},{6,7},{7,6},{8,9},{9,8},{10,11... | collective-permute-start | bytes 3145736 | tf_op jit(solution)/shard_map/ppermute | solution.py:33
  230.3 29.9 %collective-permute-start.36 = (f32[512,512]{1,0:T(8,128)}, f32[512,512]{1,0:T(8,128)S(1)}, u32[]{:S(2)}, u32[]{:S(2)}) collective-permute-start(f32[512,512]{1,0:T(8,128)} %get-tuple-element.492), channel_id=1, source_target_pairs={{0,8},{4,12},{8,0},{12,4},{16,24},{20,28},{24,16},{28,20},{1,9},{5... | collective-permute-start | bytes 3145736 | tf_op jit(solution)/shard_map/ppermute | solution.py:33
  231.8 28.3 %collective-permute-start.37 = (f32[256,1024]{1,0:T(8,128)}, f32[256,1024]{1,0:T(8,128)S(1)}, u32[]{:S(2)}, u32[]{:S(2)}) collective-permute-start(f32[256,1024]{1,0:T(8,128)} %few_of.2), channel_id=1, source_target_pairs={{0,4},{4,0},{8,12},{12,8},{16,20},{20,16},{24,28},{28,24},{1,5},{5... | collective-permute-start | bytes 3145736 | tf_op jit(solution)/shard_map/ppermute | solution.py:33
  261.1 31.6 %collective-permute-start.40 = (f32[256,1024]{1,0:T(8,128)}, f32[256,1024]{1,0:T(8,128)S(1)}, u32[]{:S(2)}, u32[]{:S(2)}) collective-permute-start(f32[256,1024]{1,0:T(8,128)} %few_of.3), channel_id=1, source_target_pairs={{0,8},{4,12},{8,0},{12,4},{16,24},{20,28},{24,16},{28,20},{1,9},{5... | collective-permute-start | bytes 3145736 | tf_op jit(solution)/shard_map/ppermute | solution.py:33
  288.3 70.5 %collective-permute-start.49 = (f32[512,1536]{1,0:T(8,128)}, f32[512,1536]{1,0:T(8,128)}, u32[]{:S(2)}, u32[]{:S(2)}) collective-permute-start(f32[512,1536]{1,0:T(8,128)} %get-tuple-element.547), channel_id=1, source_target_pairs={{0,8},{4,12},{8,0},{12,4},{16,24},{20,28},{24,16},{28,20},{1,9},{5... | collective-permute-start | bytes 9437192 | tf_op jit(solution)/shard_map/ppermute | solution.py:33
  293.7 48.7 %collective-permute-start.38 = (f32[512,1024]{1,0:T(8,128)}, f32[512,1024]{1,0:T(8,128)S(1)}, u32[]{:S(2)}, u32[]{:S(2)}) collective-permute-start(f32[512,1024]{1,0:T(8,128)} %get-tuple-element.496), channel_id=1, source_target_pairs={{0,4},{4,0},{8,12},{12,8},{16,20},{20,16},{24,28},{28,24},{1,5},{5... | collective-permute-start | bytes 6291464 | tf_op jit(solution)/shard_map/ppermute | solution.py:33
  306.5 69.6 %collective-permute-start.55 = (f32[256,2048]{1,0:T(8,128)}, f32[256,2048]{1,0:T(8,128)}, u32[]{:S(2)}, u32[]{:S(2)}) collective-permute-start(f32[256,2048]{1,0:T(8,128)} %sum_of.9.a_ref), channel_id=1, source_target_pairs={{0,2},{1,3},{2,0},{3,1},{4,6},{5,7},{6,4},{7,5},{8,10},{9,11},{10,... | collective-permute-start | bytes 6291464 | tf_op jit(solution)/shard_map/ppermute | solution.py:33
  313.8 58.9 %collective-permute-start.51 = (f32[1024,256]{1,0:T(8,128)}, f32[1024,256]{1,0:T(8,128)}, u32[]{:S(2)}, u32[]{:S(2)}) collective-permute-start(f32[1024,256]{1,0:T(8,128)} %pair_grads.4), channel_id=1, source_target_pairs={{0,4},{4,0},{8,12},{12,8},{16,20},{20,16},{24,28},{28,24},{1,5},{5... | collective-permute-start | bytes 3145736 | tf_op jit(solution)/shard_map/ppermute | solution.py:33
  358.8 47.5 %collective-permute-start.50 = (f32[512,1024]{1,0:T(8,128)}, f32[512,1024]{1,0:T(8,128)}, u32[]{:S(2)}, u32[]{:S(2)}) collective-permute-start(f32[512,1024]{1,0:T(8,128)} %pair_grads.5), channel_id=1, source_target_pairs={{0,8},{4,12},{8,0},{12,4},{16,24},{20,28},{24,16},{28,20},{1,9},{5... | collective-permute-start | bytes 6291464 | tf_op jit(solution)/shard_map/ppermute | solution.py:33
  359.2 47.1 %collective-permute-start.54 = (f32[256,2048]{1,0:T(8,128)}, f32[256,2048]{1,0:T(8,128)}, u32[]{:S(2)}, u32[]{:S(2)}) collective-permute-start(f32[256,2048]{1,0:T(8,128)} %sum_of.10.refs_0_), channel_id=1, source_target_pairs={{0,2},{1,3},{2,0},{3,1},{4,6},{5,7},{6,4},{7,5},{8,10},{9,11},{10,... | collective-permute-start | bytes 6291464 | tf_op jit(solution)/shard_map/ppermute | solution.py:33
  410.8 70.2 %collective-permute-start.65 = (f32[256,1536]{1,0:T(8,128)}, f32[256,1536]{1,0:T(8,128)}, u32[]{:S(2)}, u32[]{:S(2)}) collective-permute-start(f32[256,1536]{1,0:T(8,128)} %pad_maximum_fusion.2), channel_id=1, source_target_pairs={{0,16},{4,20},{8,24},{12,28},{16,0},{20,4},{24,8},{28,12},{1,17},{... | collective-permute-start | bytes 4718600 | tf_op jit(solution)/shard_map/ppermute | solution.py:33
  411.8 69.2 %collective-permute-start.66 = (f32[1536,256]{1,0:T(8,128)}, f32[1536,256]{1,0:T(8,128)}, u32[]{:S(2)}, u32[]{:S(2)}) collective-permute-start(f32[1536,256]{1,0:T(8,128)} %get-tuple-element.610), channel_id=1, source_target_pairs={{0,8},{4,12},{8,0},{12,4},{16,24},{20,28},{24,16},{28,20},{1,9},{5... | collective-permute-start | bytes 4718600 | tf_op jit(solution)/shard_map/ppermute | solution.py:33
  421.8 64.2 %collective-permute-start.64 = (f32[4352]{0:T(1024)S(1)}, f32[4352]{0:T(1024)S(1)}, u32[]{:S(2)}, u32[]{:S(2)}) collective-permute-start(f32[4352]{0:T(1024)S(1)} %add.80), channel_id=1, source_target_pairs={{0,16},{4,20},{8,24},{12,28},{16,0},{20,4},{24,8},{28,12},{1,17},{... | collective-permute-start | bytes 52232 | tf_op jit(solution)/shard_map/ppermute | solution.py:33
  (88 other events, 734.4 us)
